TPU v7x, 32 devices: a whole 2x2x4 slice. The times are simulated.
32 devices in a mesh: seq: 8 (over z, x), head: 4 (over y, core).
Axes of the slice: x: 2, y: 2, z: 4, core: 2. Of those that a mesh axis runs over, the one named last changes fastest.
Arguments:
- q_raw: bfloat16 [4096, 4096], P('seq', 'head'), may hold values from -120 to 120
- k_raw: bfloat16 [4096, 4096], P('seq', 'head'), may hold values from -6 to 6
- v_raw: bfloat16 [4096, 4096], P('seq', 'head'), may hold values from -6 to 6
- block_scales: float32 [3, 32, 32], P(None, 'seq', 'head'), may hold values from 0.25 to 4
- segment_ids: int32 [4096], P('seq'), may hold values from 0 to 24, as said below
- norm_gain: float32 [4096], P('head'), may hold values from 0.5 to 1.5
Outputs:
- attended: bfloat16 [4096, 4096], P('seq', 'head')
Inputs may be any that keep to these rules, and one draw needn't show every extreme that they name: `segment_ids`: ids start at 0 and never fall, rising by at most one from a token to the next. Each aligned block of 512 tokens has exactly 4 segment starts, except the second and third blocks, which have none; in the second-to-last block all starts lie in the block's first half, in the last block all lie in its second half. No segment starts at the first token of a block except segment 0 at token 0.
All inputs are finite; a program needn't handle non-finite values.
Results may differ from a plain program's by a relative error of at most 0.013.
Values may be sent and summed in bfloat16 or wider, within the bound.
No kernel may reach another device: no remote copies, remote signals or barrier semaphores. Data moves between devices by JAX's collectives and lax.ppermute only.
A program may use at most 64 MiB of HBM per device.

v0:
```python
import jax
import jax.numpy as jnp
from jax import lax
from jax.sharding import PartitionSpec as P

H = 32
HD = 128
CAP = 4


epsilon = 1e-06
missing_id = 1073741824.0


def shifted(block, axis, distance):
    devices = range(lax.axis_size(axis))
    route = [(i - distance, i) for i in devices if i - distance in devices]
    return lax.ppermute(block, axis, route)


def tail_combine(earlier, later):
    early_all, early_sum, early_count = earlier
    late_all, late_sum, late_count = later
    return (
        early_all * late_all,
        late_sum + late_all * early_sum,
        late_count + late_all * early_count,
    )


def exclusive_carries(states):
    inclusive = lax.associative_scan(tail_combine, states)
    width_total = states[1].shape[2]
    starting = (
        jnp.ones((1, 1, 1), jnp.float32),
        jnp.zeros((1, 2, width_total), jnp.float32),
        jnp.zeros((1, 1, 1), jnp.float32),
    )
    return tuple(
        (
            jnp.concatenate([first_state, whole_state[:-1]], axis=0)
            for first_state, whole_state in zip(starting, inclusive)
        )
    )


def finish_landmarks(part_key, part_value, part_count, carry_sum, carry_count):
    slot_index = jnp.arange(CAP, dtype=jnp.int32)
    lead_row = (slot_index == 0).astype(jnp.float32)
    key_total = part_key + lead_row[:, None] * carry_sum[..., 0:1, :]
    value_total = part_value + lead_row[:, None] * carry_sum[..., 1:2, :]
    count_total = part_count + lead_row * carry_count[..., 0]
    slot_size = jnp.maximum(count_total, 1.0)
    land_key = (key_total / slot_size[..., None]).astype(jnp.bfloat16)
    land_value = (value_total / slot_size[..., None]).astype(jnp.bfloat16)
    return (land_key, land_value, jnp.log(slot_size))


def on_device(q_raw, k_raw, v_raw, block_scales, segment_ids, norm_gain):
    token_count, width_total = q_raw.shape
    head_count = block_scales.shape[2]
    head_dim = width_total // head_count
    scale_block = token_count // block_scales.shape[1]
    half_len = token_count // 2
    score_scale = 1.0 / HD**0.5

    def dequantize(raw, which):
        factor = jnp.repeat(jnp.repeat(block_scales[which], scale_block, axis=0), head_dim, axis=1)
        return (raw.astype(jnp.float32) * factor).astype(jnp.bfloat16)

    queries = dequantize(q_raw, 0)
    keys_local = dequantize(k_raw, 1)
    values_local = dequantize(v_raw, 2)
    first_id = segment_ids[0]
    local_seg = segment_ids - first_id
    end_count = segment_ids[token_count - 1] - first_id
    slot_index = jnp.arange(CAP, dtype=jnp.int32)
    slot_pick = (local_seg[None, :] == slot_index[:, None]).astype(jnp.bfloat16)
    part_key = jnp.dot(slot_pick, keys_local, preferred_element_type=jnp.float32)
    part_value = jnp.dot(slot_pick, values_local, preferred_element_type=jnp.float32)
    part_count = jnp.sum(slot_pick.astype(jnp.float32), axis=1)
    in_tail = local_seg == end_count
    tail_row = in_tail.astype(jnp.bfloat16)[None, :]
    tail_sum = jnp.concatenate(
        [
            jnp.dot(tail_row, keys_local, preferred_element_type=jnp.float32),
            jnp.dot(tail_row, values_local, preferred_element_type=jnp.float32),
        ],
        axis=0,
    )
    tail_count = jnp.sum(in_tail.astype(jnp.float32)).reshape(1, 1)
    all_one = (end_count == 0).astype(jnp.float32).reshape(1, 1)
    slot_ids = jnp.where(
        slot_index < end_count, (first_id + slot_index).astype(jnp.float32), missing_id
    )
    gathered_all, gathered_sum, gathered_count = (
        lax.all_gather(all_one, "seq", axis=0, tiled=True),
        lax.all_gather(tail_sum, "seq", axis=0, tiled=True),
        lax.all_gather(tail_count, "seq", axis=0, tiled=True),
    )
    device_total = gathered_all.shape[0]
    carries = exclusive_carries(
        (
            gathered_all.reshape(device_total, 1, 1),
            gathered_sum.reshape(device_total, 2, width_total),
            gathered_count.reshape(device_total, 1, 1),
        )
    )
    position = lax.axis_index("seq")
    carry_sum = lax.dynamic_index_in_dim(carries[1], position, 0, keepdims=False)
    carry_count = lax.dynamic_index_in_dim(carries[2], position, 0, keepdims=False)
    own_key, own_value, own_bias = finish_landmarks(
        part_key, part_value, part_count, carry_sum, carry_count
    )
    table_key, table_value = (
        lax.all_gather(own_key, "seq", axis=0, tiled=True),
        lax.all_gather(own_value, "seq", axis=0, tiled=True),
    )
    table_bias, table_ids = (
        lax.all_gather(own_bias, "seq", axis=0, tiled=True),
        lax.all_gather(slot_ids, "seq", axis=0, tiled=True),
    )
    rim_key = keys_local[token_count - half_len :]
    rim_value = values_local[token_count - half_len :]
    rim_mask = in_tail[token_count - half_len :].astype(jnp.bfloat16)
    prev_key, prev_value, prev_mask = shifted((rim_key, rim_value, rim_mask), "seq", 1)
    prev_row = prev_mask[None, :]
    prev_sum = jnp.concatenate(
        [
            jnp.dot(prev_row, prev_key, preferred_element_type=jnp.float32),
            jnp.dot(prev_row, prev_value, preferred_element_type=jnp.float32),
        ],
        axis=0,
    )
    prev_count = jnp.sum(prev_mask.astype(jnp.float32))
    early_count = carry_count[0, 0] - prev_count
    later_count = carry_count[0, 0]
    early_mean = (carry_sum - prev_sum) / jnp.maximum(early_count, 1.0)
    later_mean = carry_sum / jnp.maximum(later_count, 1.0)
    positions = jnp.arange(token_count, dtype=jnp.int32)
    first_block = positions < half_len
    run_total = jnp.where(local_seg == 0, jnp.where(first_block, early_count, later_count), 0.0)
    run_live = run_total > 0.5
    run_log = jnp.log(jnp.maximum(run_total, 1.0))
    ext_ids = jnp.concatenate([jnp.where(prev_mask > 0, 0, -1).astype(jnp.int32), local_seg])
    ext_pos = jnp.arange(half_len + token_count, dtype=jnp.int32)
    win_mask = (
        (ext_ids[None, :] == local_seg[:, None])
        & (ext_pos[None, :] - half_len <= positions[:, None])
        & (ext_pos[None, :] // half_len >= positions[:, None] // half_len)
    )
    land_mask = table_ids[None, :] < segment_ids.astype(jnp.float32)[:, None]

    def by_head(matrix):
        return jnp.transpose(matrix.reshape(matrix.shape[0], head_count, head_dim), (1, 0, 2))

    head_items = (
        by_head(queries),
        by_head(jnp.concatenate([prev_key, keys_local], axis=0)),
        by_head(jnp.concatenate([prev_value, values_local], axis=0)),
        by_head(table_key),
        by_head(table_value),
        by_head(early_mean),
        by_head(later_mean),
    )

    def per_head(items):
        head_query, head_key, head_value, land_key, land_value, early_head, later_head = items
        win_score = (
            jnp.einsum("td,sd->ts", head_query, head_key, preferred_element_type=jnp.float32)
            * score_scale
        )
        win_score = jnp.where(win_mask, win_score, -jnp.inf)
        land_score = (
            jnp.einsum("td,sd->ts", head_query, land_key, preferred_element_type=jnp.float32)
            * score_scale
            + table_bias[None, :]
        )
        land_score = jnp.where(land_mask, land_score, -jnp.inf)
        rows_key = jnp.where(first_block[:, None], early_head[0][None, :], later_head[0][None, :])
        rows_value = jnp.where(first_block[:, None], early_head[1][None, :], later_head[1][None, :])
        run_score = (
            jnp.sum(head_query.astype(jnp.float32) * rows_key, axis=1) * score_scale + run_log
        )
        run_score = jnp.where(run_live, run_score, -jnp.inf)
        row_max = jnp.maximum(
            jnp.maximum(jnp.max(win_score, axis=1), jnp.max(land_score, axis=1)), run_score
        )
        win_weight = jnp.exp(win_score - row_max[:, None])
        land_weight = jnp.exp(land_score - row_max[:, None])
        run_weight = jnp.exp(run_score - row_max)
        row_total = jnp.sum(win_weight, axis=1) + jnp.sum(land_weight, axis=1) + run_weight
        weighted = jnp.einsum(
            "ts,sd->td",
            win_weight.astype(jnp.bfloat16),
            head_value,
            preferred_element_type=jnp.float32,
        )
        weighted = weighted + jnp.einsum(
            "ts,sd->td",
            land_weight.astype(jnp.bfloat16),
            land_value,
            preferred_element_type=jnp.float32,
        )
        weighted = weighted + run_weight[:, None] * rows_value
        return weighted / row_total[:, None]

    attention = lax.map(per_head, head_items)
    square_sum = jnp.sum(attention * attention, axis=(0, 2))
    square_total = lax.psum(square_sum, "head")
    norm_scale = lax.rsqrt(square_total / (H * HD) + epsilon)
    flat = jnp.transpose(attention, (1, 0, 2)).reshape(token_count, width_total)
    return (flat * norm_scale[:, None] * norm_gain[None, :]).astype(jnp.bfloat16)


def solution(mesh):
    in_specs = (
        P("seq", "head"),
        P("seq", "head"),
        P("seq", "head"),
        P(None, "seq", "head"),
        P("seq"),
        P("head"),
    )
    out_specs = P("seq", "head")
    return jax.shard_map(
        on_device, mesh=mesh, in_specs=in_specs, out_specs=out_specs, check_vma=False
    )
```

profile of v0, /device:TPU:0, one launch (start us, length us, event | category | flops | bytes accessed | tf_op | source)
XLA Modules:
  0.0 242.4 jit_solution(17584048480418568523)
XLA Ops:
  2.5 1.8 convert_reduce_fusion.1
  4.4 4.9 %collective-permute-start.1 = (bf16[256]{0:T(256)(128)(2,1)S(1)}, bf16[256]{0:T(256)(128)(2,1)S(1)}, u32[]{:S(2)}, u32[]{:S(2)}) collective-permute-start(bf16[256]{0:T(256)(128)(2,1)S(1)} %slice_convert_fusion), channel_id=1, source_target_pairs={{0,4},{4,8},{8,12},{12,16},{16,20},{20,24},{24,28},{1,5},{5,9},{9,... | collective-permute-start | bytes 1544 | tf_op jit(solution)/shard_map/ppermute | solution.py:18
  10.0 1.5 copy.30
  12.6 4.3 %collective-permute-start.2 = (bf16[256,1024]{0,1:T(8,128)(2,1)}, bf16[256,1024]{0,1:T(8,128)(2,1)}, u32[]{:S(2)}, u32[]{:S(2)}) collective-permute-start(bf16[256,1024]{0,1:T(8,128)(2,1)} %slice.228), channel_id=1, source_target_pairs={{0,4},{4,8},{8,12},{12,16},{16,20},{20,24},{24,28},{1,5},{5,9},{9,... | collective-permute-start | bytes 1572872 | tf_op jit(solution)/shard_map/ppermute | solution.py:18
  21.2 3.4 %collective-permute-start = (bf16[256,1024]{0,1:T(8,128)(2,1)}, bf16[256,1024]{0,1:T(8,128)(2,1)}, u32[]{:S(2)}, u32[]{:S(2)}) collective-permute-start(bf16[256,1024]{0,1:T(8,128)(2,1)} %slice.218), channel_id=1, source_target_pairs={{0,4},{4,8},{8,12},{12,16},{16,20},{20,24},{24,28},{1,5},{5,9},{9,... | collective-permute-start | bytes 1572872 | tf_op jit(solution)/shard_map/ppermute | solution.py:18
  24.6 27.9 %all-reduce.18 = (f32[8]{0:T(128)S(1)}, f32[8]{0:T(128)S(1)}) all-reduce(f32[8]{0:T(128)S(1)} %dynamic-update-slice.1, f32[8]{0:T(128)S(1)} %dynamic-update-slice), channel_id=1, replica_groups=mesh['seq'=8,'head'=4] {'seq'}, use_global_device_ids=true, to_apply=%add.14 | all-reduce | flops 16 | bytes 128
  56.2 30.5 %all-gather = f32[8,2,1024]{2,1,0:T(2,128)S(1)} all-gather(f32[1,2,1024]{2,1,0:T(2,128)S(1)} %maximum_bitcast_fusion), channel_id=1, replica_groups=mesh['seq'=8,'head'=4] {'seq'}, dimensions={0}, use_global_device_ids=true | all-gather | bytes 73728 | tf_op jit(solution)/shard_map/all_gather | solution.py:98
  96.8 30.5 %all-gather.2 = bf16[8,4,1024]{2,1,0:T(4,128)(2,1)S(1)} all-gather(bf16[1,4,1024]{2,1,0:T(4,128)(2,1)S(1)} %fusion.46), channel_id=1, replica_groups=mesh['seq'=8,'head'=4] {'seq'}, dimensions={0}, use_global_device_ids=true | all-gather | bytes 73728 | tf_op jit(solution)/shard_map/all_gather | solution.py:117
  127.8 30.5 %all-gather.1 = bf16[8,4,1024]{2,1,0:T(4,128)(2,1)S(1)} all-gather(bf16[1,4,1024]{2,1,0:T(4,128)(2,1)S(1)} %fusion.47), channel_id=1, replica_groups=mesh['seq'=8,'head'=4] {'seq'}, dimensions={0}, use_global_device_ids=true | all-gather | bytes 73728 | tf_op jit(solution)/shard_map/all_gather | solution.py:116
  161.1 1.4 fusion.41
  162.5 17.9 %all-reduce.17 = (f32[32]{0:T(128)S(1)}, f32[32]{0:T(128)S(1)}) all-reduce(f32[32]{0:T(128)S(1)} %get-tuple-element.272, f32[32]{0:T(128)S(1)} %fusion.67), channel_id=1, replica_groups=mesh['seq'=8,'head'=4] {'seq'}, use_global_device_ids=true, to_apply=%add.15 | all-reduce | flops 64 | bytes 512
  186.2 2.3 pad_maximum_fusion.1
  188.5 2.3 pad_maximum_fusion
  190.8 41.3 %while.12 = (s32[]{:T(128)}, f32[8,512,128]{2,1,0:T(8,128)}, bf16[8,512,128]{1,2,0:T(8,128)(2,1)S(1)}, bf16[8,768,128]{1,2,0:T(8,128)(2,1)}, bf16[8,32,128]{2,1,...) while((s32[]{:T(128)}, f32[8,512,128]{2,1,0:T(8,128)}, ...), condition=%wide.region_9.10_spmd.clone.clone, body=%wide.region_3.9_spmd.clone.clone.sunk | while | flops 215174656 | bytes 7111869 | solution.py:208
  191.2 1.7 fusion.104
  193.5 1.4 fusion.106
  196.4 1.7 fusion.104
  201.5 1.7 fusion.104
  203.8 1.4 fusion.106
  206.7 1.7 fusion.104
  209.0 1.4 fusion.106
  211.8 1.7 fusion.104
  214.1 1.4 fusion.106
  217.0 1.7 fusion.104
  219.3 1.4 fusion.106
  222.2 1.7 fusion.104
  224.5 1.4 fusion.106
  227.3 1.7 fusion.104
  229.6 1.4 fusion.106
  232.1 1.8 multiply_reduce_fusion.1
  233.9 5.7 %psum.7 = f32[512]{0:T(512)S(1)} all-reduce(f32[512]{0:T(512)S(1)} %multiply_reduce_fusion.1), channel_id=1, replica_groups=mesh['seq'=8,'head'=4] {'head'}, use_global_device_ids=true, to_apply=%region_11.12 | all-reduce | flops 512 | bytes 4096 | tf_op jit(solution)/shard_map/psum | solution.py:210
  239.6 2.8 %fusion.38 = bf16[512,1024]{1,0:T(8,128)(2,1)} fusion(f32[1024]{0:T(1024)S(1)} %copy-done.3, f32[512]{0:T(512)S(1)} %add_rsqrt_fusion, f32[8,512,128]{2,1,0:T(8,128)} %get-tuple-element.85), kind=kLoop, calls=%fused_computation.53 | loop fusion | flops 1572864 | bytes 3151872 | tf_op jit(solution)/shard_map/convert_element_type | solution.py:213
  (208 shorter events, 42.0 us)
Async XLA Ops:
  4.4 176.0 %collective-permute-start.1 = (bf16[256]{0:T(256)(128)(2,1)S(1)}, bf16[256]{0:T(256)(128)(2,1)S(1)}, u32[]{:S(2)}, u32[]{:S(2)}) collective-permute-start(bf16[256]{0:T(256)(128)(2,1)S(1)} %slice_convert_fusion), channel_id=1, source_target_pairs={{0,4},{4,8},{8,12},{12,16},{16,20},{20,24},{24,28},{1,5},{5,9},{9,... | collective-permute-start | bytes 1544 | tf_op jit(solution)/shard_map/ppermute | solution.py:18
  11.7 5.1 %copy-start = (bf16[512,1024]{1,0:T(8,128)(2,1)S(1)}, bf16[512,1024]{1,0:T(8,128)(2,1)}, u32[]{:S(2)}) copy-start(bf16[512,1024]{1,0:T(8,128)(2,1)} %param.9) | copy-start | bytes 3145732
  12.6 171.0 %collective-permute-start.2 = (bf16[256,1024]{0,1:T(8,128)(2,1)}, bf16[256,1024]{0,1:T(8,128)(2,1)}, u32[]{:S(2)}, u32[]{:S(2)}) collective-permute-start(bf16[256,1024]{0,1:T(8,128)(2,1)} %slice.228), channel_id=1, source_target_pairs={{0,4},{4,8},{8,12},{12,16},{16,20},{20,24},{24,28},{1,5},{5,9},{9,... | collective-permute-start | bytes 1572872 | tf_op jit(solution)/shard_map/ppermute | solution.py:18
  17.4 1.1 copy-start.4
  17.6 37.9 %copy-start.2 = (s32[512]{0:T(512)S(1)}, s32[512]{0:T(512)}, u32[]{:S(2)}) copy-start(s32[512]{0:T(512)} %param.12) | copy-start | bytes 6148
  21.2 163.6 %collective-permute-start = (bf16[256,1024]{0,1:T(8,128)(2,1)}, bf16[256,1024]{0,1:T(8,128)(2,1)}, u32[]{:S(2)}, u32[]{:S(2)}) collective-permute-start(bf16[256,1024]{0,1:T(8,128)(2,1)} %slice.218), channel_id=1, source_target_pairs={{0,4},{4,8},{8,12},{12,16},{16,20},{20,24},{24,28},{1,5},{5,9},{9,... | collective-permute-start | bytes 1572872 | tf_op jit(solution)/shard_map/ppermute | solution.py:18
  94.7 65.0 %copy-start.1 = (bf16[512,1024]{1,0:T(8,128)(2,1)S(1)}, bf16[512,1024]{1,0:T(8,128)(2,1)}, u32[]{:S(2)}) copy-start(bf16[512,1024]{1,0:T(8,128)(2,1)} %param.8) | copy-start | bytes 3145732
  232.1 7.5 %copy-start.3 = (f32[1024]{0:T(1024)S(1)}, f32[1024]{0:T(1024)}, u32[]{:S(2)}) copy-start(f32[1024]{0:T(1024)} %param.13) | copy-start | bytes 12292
where the time goes:
time: 244 us; the launch traced here: 242 us
  blocking collectives  143 us (59%)
  matrix products  38.4 us (16%)
  other arithmetic  25.1 us (10%)
  local copies, waits for them, and re-layouts  15.8 us (6%)
  starting transfers between devices  12.5 us (5%)
  between operations  7.23 us (3%)
    unnamed x2, blocking collectives  45.7 us
    all_gather x1, blocking collectives, on_device(): lax.all_gather(own_value, 'seq', axis=0, tiled=True)  30.5 us
    all_gather x1, blocking collectives, on_device(): lax.all_gather(own_key, 'seq', axis=0, tiled=True)  30.5 us
    all_gather x1, blocking collectives, on_device(): lax.all_gather(tail_sum, 'seq', axis=0, tiled=True)  30.5 us
    dot_general x8, matrix products, per_head(): jnp.einsum('td,sd->ts', head_query, head_key, preferred_element_type=jnp....  13.4 us
    ppermute x3, starting transfers between devices, shifted(): return lax.ppermute(block, axis, route)  12.5 us
    dot_general x8, matrix products, per_head(): jnp.einsum('ts,sd->td', win_weight.astype(jnp.bfloat16), head_value, pref...  11.3 us
    dot_general x8, matrix products, per_head(): jnp.einsum('ts,sd->td', land_weight.astype(jnp.bfloat16), land_value, pre...  8.35 us
  transfers between devices with their start and end apart: 3, of which 0 were waited for; matrix products, arithmetic and copies ran while one was open for 10% of the time, Pallas kernels for 0%

commit v1 on v0

v1 whole, which is shorter than its diff:
```python
import functools
import math

import jax
import jax.numpy as jnp
from jax import lax
from jax.experimental import pallas as pl
from jax.experimental.pallas import tpu as pltpu
from jax.sharding import PartitionSpec as P

HD = 128
CAP = 4
LANES = 128
ROWS = 16
EARLY = CAP + 1
epsilon = 1e-06
log_two_e = math.log2(math.e)
heads_per_step = 2
f32 = jnp.float32
bf16 = jnp.bfloat16


def nt_dot(a, b):
    return lax.dot_general(a, b, (((1,), (1,)), ((), ())), preferred_element_type=f32)


def dequantized(ref, scales, which, head, cols, rows_per_scale, first_scale=0):
    parts = []
    for piece in range(ref.shape[0] // rows_per_scale):
        rows = slice(piece * rows_per_scale, (piece + 1) * rows_per_scale)
        parts.append(
            (ref[rows, cols].astype(f32) * scales[which, first_scale + piece, head]).astype(bf16)
        )
    return jnp.concatenate(parts, axis=0)


def columns_of(row):
    pieces = []
    for start in range(0, row.shape[1], LANES):
        piece = jnp.broadcast_to(row[:, start : start + LANES], (LANES, LANES))
        pieces.append(piece.T)
    return jnp.concatenate(pieces, axis=0)


def tail_kernel(which, scale_rows, scales, raw, out):
    step = pl.program_id(0)
    heads = raw.shape[1] // HD
    first = scales.shape[1] - raw.shape[0] // scale_rows
    for local in range(heads):
        cols = slice(local * HD, (local + 1) * HD)
        out[:, cols] = dequantized(
            raw, scales, which, step * heads + local, cols, scale_rows, first
        )


def table_kernel(scale_rows, scales, ids, k_raw, v_raw, table):
    step = pl.program_id(0)
    steps = pl.num_programs(0) - 1
    tokens = ids.shape[1]
    heads = k_raw.shape[1] // HD
    row = ids[...]
    local = row - row[:, 0:1]
    last = local[:, tokens - 1 :]
    slot = lax.broadcasted_iota(jnp.int32, (ROWS, tokens), 0)
    token = lax.broadcasted_iota(jnp.int32, (ROWS, tokens), 1)

    def picked(first_row):
        index = slot - first_row
        whole = (index >= 0) & (index <= CAP) & (local == index)
        early = (index == EARLY) & (local == last) & (token < tokens // 2)
        return (whole | early).astype(f32)

    pick_key, pick_value = picked(0), picked(ROWS // 2)

    @pl.when(step < steps)
    def _():
        for head in range(heads):
            cols = slice(head * HD, (head + 1) * HD)
            key = dequantized(k_raw, scales, 1, step * heads + head, cols, scale_rows)
            value = dequantized(v_raw, scales, 2, step * heads + head, cols, scale_rows)
            sums = jnp.dot(pick_key.astype(bf16), key, preferred_element_type=f32)
            sums = sums + jnp.dot(pick_value.astype(bf16), value, preferred_element_type=f32)
            table[:, :, cols] = jnp.broadcast_to(
                sums.astype(bf16)[None], (table.shape[0], ROWS, HD)
            )

    @pl.when(step == steps)
    def _():
        count = jnp.sum(pick_key + pick_value, axis=1, keepdims=True).astype(jnp.int32)
        index = lax.broadcasted_iota(jnp.int32, (ROWS, 1), 0) & (ROWS // 2 - 1)
        seg = row[:, 0:1] + jnp.where(index == EARLY, last, index)
        lane = lax.broadcasted_iota(jnp.int32, (ROWS, LANES), 1)
        meta = jnp.where(lane == 0, seg & 127, 0)
        meta = jnp.where(lane == 1, seg >> 7, meta)
        meta = jnp.where(lane == 2, count & 127, meta)
        meta = jnp.where(lane == 3, count >> 7, meta)
        meta = meta.astype(f32).astype(bf16)
        table[:, :, 0:LANES] = jnp.broadcast_to(meta[None], (table.shape[0], ROWS, LANES))


def local_kernel(scale_rows, scales, ids, q_raw, k_raw, v_raw, out, stats, near, far):
    step = pl.program_id(0)
    tokens = ids.shape[1]
    half = tokens // 2
    heads = q_raw.shape[1] // HD
    factor = log_two_e / math.sqrt(HD)

    @pl.when(step == 0)
    def _():
        row = ids[...]
        column = columns_of(row)
        for mask, start, width in ((near, 0, half), (far, half, tokens)):
            query = lax.broadcasted_iota(jnp.int32, (half, LANES), 0) + start
            for left in range(0, width, LANES):
                key = lax.broadcasted_iota(jnp.int32, (half, LANES), 1) + left
                live = (column[start : start + half] == row[:, left : left + LANES]) & (
                    key <= query
                )
                mask[:, left : left + LANES] = jnp.where(live, 0.0, -jnp.inf)

    lane = lax.broadcasted_iota(jnp.int32, (half, LANES), 1)
    for head in range(heads):
        cols = slice(head * HD, (head + 1) * HD)
        index = step * heads + head
        query = dequantized(q_raw, scales, 0, index, cols, scale_rows)
        key = dequantized(k_raw, scales, 1, index, cols, scale_rows)
        value = dequantized(v_raw, scales, 2, index, cols, scale_rows)
        for mask, start, width in ((near, 0, half), (far, half, tokens)):
            rows = slice(start, start + half)
            score = nt_dot(query[rows], key[:width]) * factor + mask[...]
            top = jnp.max(score, axis=1, keepdims=True)
            weight = jnp.exp2(score - top)
            total = jnp.sum(weight, axis=1, keepdims=True)
            out[rows, cols] = jnp.dot(
                weight.astype(bf16), value[:width], preferred_element_type=f32
            )
            kept = jnp.where(lane == 2 * head, top, total)
            if head == 0:
                stats[0, rows, :] = kept
            else:
                stats[0, rows, :] = jnp.where(lane >= 2 * head, kept, stats[0, rows, :])


def final_kernel(
    scale_rows, device_count,
    place, scales, ids, q_raw, local, stats, prev_key, prev_value, table, meta,
    out, squares,
    pick_key, pick_value, inverse, land_mask, prev_mask, power,
):
    step = pl.program_id(0)
    tokens = ids.shape[1]
    half = tokens // 2
    heads = q_raw.shape[1] // HD
    factor = log_two_e / math.sqrt(HD)
    land_total = CAP * device_count
    land_pad, entries = pick_key.shape

    @pl.when(step == 0)
    def _():
        me = place[0]
        row = ids[...]
        first = row[:, 0:1]
        column = columns_of(row)
        info = meta[...].astype(f32).T
        seg = info[0:1] + 128.0 * info[1:2]
        entry = lax.broadcasted_iota(jnp.int32, (1, entries), 1)
        device = entry // ROWS
        slot = entry & (ROWS - 1)
        is_key = slot < ROWS // 2
        slot = slot & (ROWS // 2 - 1)
        open_here = seg == first.astype(f32)
        whole = slot <= CAP
        later = open_here & whole & (device < me)
        early = (open_here & whole & (device < me - 1)) | ((slot == EARLY) & (device == me - 1))
        before = open_here & whole & (device == me - 1)
        land = lax.broadcasted_iota(jnp.int32, (land_pad, entries), 0)
        picked = (land < land_total) & (land.astype(f32) == seg) & whole
        picked = picked | ((land == land_total) & early)
        picked = picked | ((land == land_total + 1) & later)
        picked = picked | ((land == land_total + 2) & before)
        for_key = (picked & is_key).astype(f32).astype(bf16)
        pick_key[...] = for_key
        pick_value[...] = (picked & ~is_key).astype(f32).astype(bf16)
        found = jnp.dot(for_key, meta[...], preferred_element_type=f32)
        count = found[:, 2:3] + 128.0 * found[:, 3:4]
        inverse[...] = jnp.broadcast_to(1.0 / jnp.maximum(count, 1.0), inverse.shape)
        counts = nt_dot(info[0:8].astype(bf16), for_key)
        counts = counts[2:3] + 128.0 * counts[3:4]
        bias = jnp.log2(jnp.maximum(counts, 1.0))
        query = lax.broadcasted_iota(jnp.int32, (tokens, LANES), 0)
        opened = column == first
        for left in range(0, land_pad, LANES):
            cols = slice(left, left + LANES)
            lane = lax.broadcasted_iota(jnp.int32, (tokens, LANES), 1) + left
            run = jnp.where(query < half, land_total, land_total + 1)
            live = ((lane < land_total) & (lane < column)) | (
                (lane == run) & opened & (counts[:, cols] > 0.5)
            )
            land_mask[:, cols] = jnp.where(live, bias[:, cols], -jnp.inf)
        tail = counts[:, land_total + 2 : land_total + 3].astype(jnp.int32)
        for left in range(0, half, LANES):
            key = lax.broadcasted_iota(jnp.int32, (half, LANES), 1) + left
            live = (key >= half - tail) & opened[:half]
            prev_mask[:, left : left + LANES] = jnp.where(live, 0.0, -jnp.inf)

    for head in range(heads):
        cols = slice(head * HD, (head + 1) * HD)
        query = dequantized(q_raw, scales, 0, step * heads + head, cols, scale_rows)
        sums = table[:, cols]
        land_key = (
            jnp.dot(pick_key[...], sums, preferred_element_type=f32) * inverse[...]
        ).astype(bf16)
        land_value = (
            jnp.dot(pick_value[...], sums, preferred_element_type=f32) * inverse[...]
        ).astype(bf16)
        for start in (0, half):
            rows = slice(start, start + half)
            top = stats[0, rows, 2 * head : 2 * head + 1]
            total = stats[0, rows, 2 * head + 1 : 2 * head + 2]
            score = nt_dot(query[rows], land_key) * factor + land_mask[rows, :]
            new_top = jnp.maximum(top, jnp.max(score, axis=1, keepdims=True))
            if start == 0:
                prev = nt_dot(query[rows], prev_key[:, cols]) * factor + prev_mask[...]
                new_top = jnp.maximum(new_top, jnp.max(prev, axis=1, keepdims=True))
            shrink = jnp.exp2(top - new_top)
            weight = jnp.exp2(score - new_top)
            total = total * shrink + jnp.sum(weight, axis=1, keepdims=True)
            value = local[rows, cols] * shrink
            value = value + jnp.dot(weight.astype(bf16), land_value, preferred_element_type=f32)
            if start == 0:
                weight = jnp.exp2(prev - new_top)
                total = total + jnp.sum(weight, axis=1, keepdims=True)
                value = value + jnp.dot(
                    weight.astype(bf16), prev_value[:, cols], preferred_element_type=f32
                )
            value = value / total
            out[rows, cols] = value
            if head == 0:
                square = jnp.where(step == 0, 0.0, power[rows, :]) + value * value
            else:
                square = power[rows, :] + value * value
            power[rows, :] = square

    @pl.when(step == pl.num_programs(0) - 1)
    def _():
        ones = jnp.ones((8, LANES), f32)
        squares[...] = lax.dot_general(
            ones, power[...], (((1,), (1,)), ((), ())),
            precision=lax.Precision.HIGHEST, preferred_element_type=f32,
        )[0:1]


def scale_kernel(width, count, *refs):
    squares, (gain, raw, out) = refs[:count], refs[count:]
    total = squares[0][...]
    for ref in squares[1:]:
        total = total + ref[...]
    norm = lax.rsqrt(total / width + epsilon)
    norm = columns_of(norm)
    for left in range(0, raw.shape[1], LANES):
        cols = slice(left, left + LANES)
        out[:, cols] = (raw[:, cols] * norm * gain[:, cols]).astype(out.dtype)


def on_device(q_raw, k_raw, v_raw, block_scales, segment_ids, norm_gain):
    tokens, width = q_raw.shape
    half = tokens // 2
    scale_rows = tokens // block_scales.shape[1]
    devices = lax.axis_size("seq")
    head_devices = lax.axis_size("head")
    step_width = heads_per_step * HD
    steps = width // step_width
    entries = devices * ROWS
    land_pad = -(-(CAP * devices + 3) // LANES) * LANES
    smem = pl.BlockSpec(memory_space=pltpu.SMEM)
    sds = jax.ShapeDtypeStruct
    ids = segment_ids.reshape(1, tokens)
    ids_spec = pl.BlockSpec((1, tokens), lambda s: (0, 0))
    full_rows = pl.BlockSpec((tokens, step_width), lambda s: (0, s))
    half_rows = pl.BlockSpec((half, step_width), lambda s: (0, s))

    def tails(raw, which):
        return pl.pallas_call(
            functools.partial(tail_kernel, which, scale_rows),
            name="tail_%d" % which,
            grid=(2,),
            in_specs=[smem, pl.BlockSpec((half, width // 2), lambda s: (1, s))],
            out_specs=pl.BlockSpec((half, width // 2), lambda s: (0, s)),
            out_shape=sds((half, width), bf16),
            cost_estimate=pl.CostEstimate(flops=half * width, bytes_accessed=4 * half * width, transcendentals=0),
        )(block_scales, raw)

    def shifted(block):
        return lax.ppermute(block, "seq", [(i - 1, i) for i in range(1, devices)])

    prev_key = shifted(tails(k_raw, 1))
    prev_value = shifted(tails(v_raw, 2))

    table_steps = 4
    table_width = width // table_steps
    last = table_steps - 1
    clipped = pl.BlockSpec((tokens, table_width), lambda s: (0, jnp.minimum(s, last)))
    table = pl.pallas_call(
        functools.partial(table_kernel, scale_rows),
        name="table",
        grid=(table_steps + 1,),
        in_specs=[smem, ids_spec, clipped, clipped],
        out_specs=pl.BlockSpec((devices, ROWS, table_width), lambda s: (0, 0, s)),
        out_shape=sds((devices, ROWS, width + LANES), bf16),
        cost_estimate=pl.CostEstimate(flops=64 * tokens * width, bytes_accessed=4 * tokens * width, transcendentals=0),
    )(block_scales, ids, k_raw, v_raw)
    table = lax.all_to_all(table, "seq", 0, 0, tiled=True).reshape(entries, width + LANES)

    attended, stats = pl.pallas_call(
        functools.partial(local_kernel, scale_rows),
        name="local",
        grid=(steps,),
        in_specs=[smem, ids_spec, full_rows, full_rows, full_rows],
        out_specs=[full_rows, pl.BlockSpec((1, tokens, LANES), lambda s: (s, 0, 0))],
        out_shape=[sds((tokens, width), f32), sds((steps, tokens, LANES), f32)],
        scratch_shapes=[pltpu.VMEM((half, half), f32), pltpu.VMEM((half, tokens), f32)],
        cost_estimate=pl.CostEstimate(
            flops=3 * half * tokens * width * 2, bytes_accessed=10 * tokens * width, transcendentals=half * tokens * 12
        ),
    )(block_scales, ids, q_raw, k_raw, v_raw)

    place = lax.axis_index("seq").astype(jnp.int32).reshape(1)
    attended, squares = pl.pallas_call(
        functools.partial(final_kernel, scale_rows, devices),
        name="final",
        grid=(steps,),
        in_specs=[
            smem, smem, ids_spec, full_rows, full_rows,
            pl.BlockSpec((1, tokens, LANES), lambda s: (s, 0, 0)),
            half_rows, half_rows,
            pl.BlockSpec((entries, step_width), lambda s: (0, s)),
            pl.BlockSpec((entries, LANES), lambda s: (0, width // LANES)),
        ],
        out_specs=[full_rows, pl.BlockSpec((1, tokens), lambda s: (0, 0))],
        out_shape=[sds((tokens, width), f32), sds((1, tokens), f32)],
        scratch_shapes=[
            pltpu.VMEM((land_pad, entries), bf16),
            pltpu.VMEM((land_pad, entries), bf16),
            pltpu.VMEM((land_pad, LANES), f32),
            pltpu.VMEM((tokens, land_pad), f32),
            pltpu.VMEM((half, half), f32),
            pltpu.VMEM((tokens, LANES), f32),
        ],
        cost_estimate=pl.CostEstimate(
            flops=2 * half * tokens * width * 2, bytes_accessed=14 * tokens * width, transcendentals=half * tokens * 8
        ),
    )(place, block_scales, ids, q_raw, attended, stats, prev_key, prev_value, table, table)

    parts = [squares] + [
        lax.ppermute(squares, "head", [(i, (i + d) % head_devices) for i in range(head_devices)])
        for d in range(1, head_devices)
    ]
    rows_out = tokens // 4
    part_spec = pl.BlockSpec((1, rows_out), lambda s: (0, s))
    row_spec = pl.BlockSpec((rows_out, width), lambda s: (s, 0))
    return pl.pallas_call(
        functools.partial(scale_kernel, width * head_devices, head_devices),
        name="scale",
        grid=(4,),
        in_specs=[part_spec] * head_devices + [pl.BlockSpec((1, width), lambda s: (0, 0)), row_spec],
        out_specs=row_spec,
        out_shape=sds((tokens, width), bf16),
        cost_estimate=pl.CostEstimate(flops=3 * tokens * width, bytes_accessed=6 * tokens * width, transcendentals=tokens),
    )(*parts, norm_gain.reshape(1, width), attended)


def solution(mesh):
    in_specs = (
        P("seq", "head"), P("seq", "head"), P("seq", "head"),
        P(None, "seq", "head"), P("seq"), P("head"),
    )
    return jax.shard_map(
        on_device, mesh=mesh, in_specs=in_specs, out_specs=P("seq", "head"), check_vma=False
    )
```

time: 244 us -> 57 us (0.23)
  the two profiles are of different devices: /device:TPU:0 before, /device:TPU:16 now
where the time goes in v1:
time: 57 us; the launch traced here: 56.5 us
  Pallas kernels  29.4 us (52%)
  starting transfers between devices  13.7 us (24%)
  waiting for transfers between devices  11.7 us (21%)
  local copies, waits for them, and re-layouts  1.65 us (3%)
    pallas_call x1, Pallas kernels, on_device(): pl.pallas_call(functools.partial(final_kernel, scale_rows, devices), name...  9.67 us
    all_to_all x1, waiting for transfers between devices, on_device(): lax.all_to_all(table, 'seq', 0, 0, tiled=True)  8.65 us
    pallas_call x1, Pallas kernels, on_device(): pl.pallas_call(functools.partial(local_kernel, scale_rows), name='local',...  7.73 us
    ppermute x2, starting transfers between devices, shifted(): return lax.ppermute(block, 'seq', [(i - 1, i) for i in range(1, devices)])  6.83 us
    all_to_all x1, starting transfers between devices, on_device(): lax.all_to_all(table, 'seq', 0, 0, tiled=True)  5.13 us
    pallas_call x1, Pallas kernels, on_device(): pl.pallas_call(functools.partial(table_kernel, scale_rows), name='table',...  4.45 us
    pallas_call x1, Pallas kernels, on_device(): pl.pallas_call(functools.partial(scale_kernel, width * head_devices, head...  3.84 us
    pallas_call x2, Pallas kernels, tails(): pl.pallas_call(functools.partial(tail_kernel, which, scale_rows), name='t...  3.69 us
  transfers between devices with their start and end apart: 6, of which 3 were waited for; matrix products, arithmetic and copies ran while one was open for 0% of the time, Pallas kernels for 25%

profile of v1, /device:TPU:16, one launch (start us, length us, event | category | flops | bytes accessed | tf_op | source)
XLA Modules:
  0.0 56.5 jit_solution(3791103721565118974)
XLA Ops:
  0.0 1.8 %tail_2.1 = bf16[256,1024]{1,0:T(8,128)(2,1)} custom-call(f32[3,4,8]{2,1,0:T(4,128)} %scales.9, bf16[512,1024]{1,0:T(8,128)(2,1)} %v_raw.3), custom_call_target="tpu_custom_call" | custom-call | flops 262144 | bytes 1048576 | tf_op jit(solution)/shard_map/tail_2/pallas_call | solution.py:283
  1.8 3.4 %collective-permute-start.1 = (bf16[256,1024]{1,0:T(8,128)(2,1)}, bf16[256,1024]{1,0:T(8,128)(2,1)S(1)}, u32[]{:S(2)}, u32[]{:S(2)}) collective-permute-start(bf16[256,1024]{1,0:T(8,128)(2,1)} %tail_2.1), channel_id=1, source_target_pairs={{0,4},{4,8},{8,12},{12,16},{16,20},{20,24},{24,28},{1,5},{5,9},{9,... | collective-permute-start | bytes 1572872 | tf_op jit(solution)/shard_map/ppermute | solution.py:294
  5.2 1.8 %tail_1.1 = bf16[256,1024]{1,0:T(8,128)(2,1)} custom-call(f32[3,4,8]{2,1,0:T(4,128)} %scales.9, bf16[512,1024]{1,0:T(8,128)(2,1)} %k_raw.3), custom_call_target="tpu_custom_call" | custom-call | flops 262144 | bytes 1048576 | tf_op jit(solution)/shard_map/tail_1/pallas_call | solution.py:283
  7.1 3.4 %collective-permute-start = (bf16[256,1024]{1,0:T(8,128)(2,1)}, bf16[256,1024]{1,0:T(8,128)(2,1)S(1)}, u32[]{:S(2)}, u32[]{:S(2)}) collective-permute-start(bf16[256,1024]{1,0:T(8,128)(2,1)} %tail_1.1), channel_id=1, source_target_pairs={{0,4},{4,8},{8,12},{12,16},{16,20},{20,24},{24,28},{1,5},{5,9},{9,... | collective-permute-start | bytes 1572872 | tf_op jit(solution)/shard_map/ppermute | solution.py:294
  10.5 4.5 %table.1 = bf16[8,16,1152]{2,1,0:T(8,128)(2,1)} custom-call(f32[3,4,8]{2,1,0:T(4,128)} %scales.9, s32[1,512]{1,0:T(1,128)} %bitcast.6, bf16[512,1024]{1,0:T(8,128)(2,1)} %k_raw.3, bf16[512,1024]{1,0:T(8,128)(2,1)} %v_raw.3), custom_call_target="tpu_custom_call" | custom-call | flops 33554432 | bytes 2097152 | tf_op jit(solution)/shard_map/table/pallas_call | solution.py:303
  15.0 5.1 %all-to-all-start = ((bf16[8,16,1152]{2,1,0:T(8,128)(2,1)}), bf16[8,16,1152]{2,1,0:T(8,128)(2,1)S(1)}, u32[]{:S(2)}, u32[]{:S(2)}) async-start(bf16[8,16,1152]{2,1,0:T(8,128)(2,1)} %table.1), calls=%async_computation | async-start | bytes 589824 | tf_op jit(solution)/shard_map/all_to_all | solution.py:312
  20.1 7.7 %local.1 = (f32[512,1024]{1,0:T(8,128)}, f32[4,512,128]{2,1,0:T(8,128)}) custom-call(f32[3,4,8]{2,1,0:T(4,128)} %scales.9, s32[1,512]{1,0:T(1,128)} %bitcast.7, bf16[512,1024]{1,0:T(8,128)(2,1)} %q_raw.3, bf16[512,1024]{1,0:T(8,128)(2,1)} %k_raw.3, bf16[512,1024]{1,0:T(8,128)(2,1)} %v_raw.3), custom_call_target="tpu_custom_call" | custom-call | flops 805306368 | bytes 5242880 | tf_op jit(solution)/shard_map/local/pallas_call | solution.py:314
  27.8 8.7 %all-to-all-done = bf16[8,16,1152]{2,1,0:T(8,128)(2,1)S(1)} async-done(((bf16[8,16,1152]{2,1,0:T(8,128)(2,1)}), bf16[8,16,1152]{2,1,0:T(8,128)(2,1)S(1)}, u32[]{:S(2)}, u32[]{:S(2)}) %all-to-all-start) | async-done | bytes 294944 | tf_op jit(solution)/shard_map/all_to_all | solution.py:312
  36.5 0.0 copy-start
  36.5 0.0 collective-permute-done.1.prev_value
  36.5 0.0 copy-start.1
  36.5 0.0 collective-permute-done.prev_key
  36.5 0.0 copy-start.2
  36.5 0.7 %copy-done = bf16[8,16,1152]{2,1,0:T(8,128)(2,1)} copy-done((bf16[8,16,1152]{2,1,0:T(8,128)(2,1)}, bf16[8,16,1152]{2,1,0:T(8,128)(2,1)S(1)}, u32[]{:S(2)}) %copy-start) | copy-done | bytes 294936
  37.2 0.2 copy-done.1
  37.4 0.2 copy-done.2
  37.6 9.7 %final.1 = (f32[512,1024]{1,0:T(8,128)}, f32[1,512]{1,0:T(1,128)}) custom-call(s32[1]{0:T(128)} %bitcast.place, f32[3,4,8]{2,1,0:T(4,128)} %scales.9, s32[1,512]{1,0:T(1,128)} %bitcast.8, bf16[512,1024]{1,0:T(8,128)(2,1)} %q_raw.3, f32[512,1024]{1,0:T(8,128)} %get-tuple-element.9.local, f32[4,512,128]{2,1,0:T(8,128)} %get-tuple-element.10.stats, ...), custom_call_target="tpu_custom_call" | custom-call | flops 536870912 | bytes 7340032 | tf_op jit(solution)/shard_map/final/pallas_call | solution.py:328
  47.3 0.0 collective-permute-start.4
  47.3 1.6 %collective-permute-start.3 = (f32[1,512]{1,0:T(1,128)}, f32[1,512]{1,0:T(1,128)S(1)}, u32[]{:S(2)}, u32[]{:S(2)}) collective-permute-start(f32[1,512]{1,0:T(1,128)} %get-tuple-element.11.refs_0_), channel_id=1, source_target_pairs={{0,2},{1,3},{2,0},{3,1},{4,6},{5,7},{6,4},{7,5},{8,10},{9,11},{10,... | collective-permute-start | bytes 6152 | tf_op jit(solution)/shard_map/ppermute | solution.py:355
  48.9 0.2 collective-permute-start.2
  49.0 0.0 collective-permute-done.4.refs_3_
  49.0 0.0 copy-start.3
  49.0 2.1 %collective-permute-done.3.refs_2_ = f32[1,512]{1,0:T(1,128)S(1)} collective-permute-done((f32[1,512]{1,0:T(1,128)}, f32[1,512]{1,0:T(1,128)S(1)}, u32[]{:S(2)}, u32[]{:S(2)}) %collective-permute-start.3) | collective-permute-done | bytes 2080 | tf_op jit(solution)/shard_map/ppermute | solution.py:355
  51.1 0.0 copy-start.4
  51.1 0.9 %collective-permute-done.2.refs_1_ = f32[1,512]{1,0:T(1,128)S(1)} collective-permute-done((f32[1,512]{1,0:T(1,128)}, f32[1,512]{1,0:T(1,128)S(1)}, u32[]{:S(2)}, u32[]{:S(2)}) %collective-permute-start.2) | collective-permute-done | bytes 2080 | tf_op jit(solution)/shard_map/ppermute | solution.py:355
  52.1 0.0 copy-start.5
  52.1 0.0 copy-done.3
  52.1 0.0 copy-done.4
  52.1 0.6 %copy-done.5 = f32[1,512]{1,0:T(1,128)} copy-done((f32[1,512]{1,0:T(1,128)}, f32[1,512]{1,0:T(1,128)S(1)}, u32[]{:S(2)}) %copy-start.5) | copy-done | bytes 2072
  52.7 3.8 %scale.1 = bf16[512,1024]{1,0:T(8,128)(2,1)} custom-call(f32[1,512]{1,0:T(1,128)} %get-tuple-element.11.refs_0_, f32[1,512]{1,0:T(1,128)} %copy-done.5, f32[1,512]{1,0:T(1,128)} %copy-done.4, f32[1,512]{1,0:T(1,128)} %copy-done.3, f32[1,1024]{1,0:T(1,128)} %bitcast.9, f32[512,1024]{1,0:T(8,128)} %get-tuple-element.12.refs_5_), custom_call_target="tpu_custom_call" | custom-call | flops 1572864 | bytes 3145728 | tf_op jit(solution)/shard_map/scale/pallas_call | solution.py:361
Async XLA Ops:
  1.8 34.7 %collective-permute-start.1 = (bf16[256,1024]{1,0:T(8,128)(2,1)}, bf16[256,1024]{1,0:T(8,128)(2,1)S(1)}, u32[]{:S(2)}, u32[]{:S(2)}) collective-permute-start(bf16[256,1024]{1,0:T(8,128)(2,1)} %tail_2.1), channel_id=1, source_target_pairs={{0,4},{4,8},{8,12},{12,16},{16,20},{20,24},{24,28},{1,5},{5,9},{9,... | collective-permute-start | bytes 1572872 | tf_op jit(solution)/shard_map/ppermute | solution.py:294
  7.1 29.4 %collective-permute-start = (bf16[256,1024]{1,0:T(8,128)(2,1)}, bf16[256,1024]{1,0:T(8,128)(2,1)S(1)}, u32[]{:S(2)}, u32[]{:S(2)}) collective-permute-start(bf16[256,1024]{1,0:T(8,128)(2,1)} %tail_1.1), channel_id=1, source_target_pairs={{0,4},{4,8},{8,12},{12,16},{16,20},{20,24},{24,28},{1,5},{5,9},{9,... | collective-permute-start | bytes 1572872 | tf_op jit(solution)/shard_map/ppermute | solution.py:294
  15.0 21.5 %all-to-all-start = ((bf16[8,16,1152]{2,1,0:T(8,128)(2,1)}), bf16[8,16,1152]{2,1,0:T(8,128)(2,1)S(1)}, u32[]{:S(2)}, u32[]{:S(2)}) async-start(bf16[8,16,1152]{2,1,0:T(8,128)(2,1)} %table.1), calls=%async_computation | async-start | bytes 589824 | tf_op jit(solution)/shard_map/all_to_all | solution.py:312
  36.5 0.7 %copy-start = (bf16[8,16,1152]{2,1,0:T(8,128)(2,1)}, bf16[8,16,1152]{2,1,0:T(8,128)(2,1)S(1)}, u32[]{:S(2)}) copy-start(bf16[8,16,1152]{2,1,0:T(8,128)(2,1)S(1)} %all-to-all-done) | copy-start | bytes 884740
  36.5 0.9 %copy-start.1 = (bf16[256,1024]{1,0:T(8,128)(2,1)}, bf16[256,1024]{1,0:T(8,128)(2,1)S(1)}, u32[]{:S(2)}) copy-start(bf16[256,1024]{1,0:T(8,128)(2,1)S(1)} %collective-permute-done.1.prev_value) | copy-start | bytes 1572868
  36.5 1.1 %copy-start.2 = (bf16[256,1024]{1,0:T(8,128)(2,1)}, bf16[256,1024]{1,0:T(8,128)(2,1)S(1)}, u32[]{:S(2)}) copy-start(bf16[256,1024]{1,0:T(8,128)(2,1)S(1)} %collective-permute-done.prev_key) | copy-start | bytes 1572868
  47.3 1.8 %collective-permute-start.4 = (f32[1,512]{1,0:T(1,128)}, f32[1,512]{1,0:T(1,128)S(1)}, u32[]{:S(2)}, u32[]{:S(2)}) collective-permute-start(f32[1,512]{1,0:T(1,128)} %get-tuple-element.11.refs_0_), channel_id=1, source_target_pairs={{0,3},{1,0},{2,1},{3,2},{4,7},{5,4},{6,5},{7,6},{8,11},{9,8},{10,9... | collective-permute-start | bytes 6152 | tf_op jit(solution)/shard_map/ppermute | solution.py:355
  47.3 3.9 %collective-permute-start.3 = (f32[1,512]{1,0:T(1,128)}, f32[1,512]{1,0:T(1,128)S(1)}, u32[]{:S(2)}, u32[]{:S(2)}) collective-permute-start(f32[1,512]{1,0:T(1,128)} %get-tuple-element.11.refs_0_), channel_id=1, source_target_pairs={{0,2},{1,3},{2,0},{3,1},{4,6},{5,7},{6,4},{7,5},{8,10},{9,11},{10,... | collective-permute-start | bytes 6152 | tf_op jit(solution)/shard_map/ppermute | solution.py:355
  48.9 3.2 %collective-permute-start.2 = (f32[1,512]{1,0:T(1,128)}, f32[1,512]{1,0:T(1,128)S(1)}, u32[]{:S(2)}, u32[]{:S(2)}) collective-permute-start(f32[1,512]{1,0:T(1,128)} %get-tuple-element.11.refs_0_), channel_id=1, source_target_pairs={{0,1},{1,2},{2,3},{3,0},{4,5},{5,6},{6,7},{7,4},{8,9},{9,10},{10,1... | collective-permute-start | bytes 6152 | tf_op jit(solution)/shard_map/ppermute | solution.py:355
  49.0 3.1 %copy-start.3 = (f32[1,512]{1,0:T(1,128)}, f32[1,512]{1,0:T(1,128)S(1)}, u32[]{:S(2)}) copy-start(f32[1,512]{1,0:T(1,128)S(1)} %collective-permute-done.4.refs_3_) | copy-start | bytes 6148
  51.1 1.0 %copy-start.4 = (f32[1,512]{1,0:T(1,128)}, f32[1,512]{1,0:T(1,128)S(1)}, u32[]{:S(2)}) copy-start(f32[1,512]{1,0:T(1,128)S(1)} %collective-permute-done.3.refs_2_) | copy-start | bytes 6148
  52.1 0.6 %copy-start.5 = (f32[1,512]{1,0:T(1,128)}, f32[1,512]{1,0:T(1,128)S(1)}, u32[]{:S(2)}) copy-start(f32[1,512]{1,0:T(1,128)S(1)} %collective-permute-done.2.refs_1_) | copy-start | bytes 6148

commit v2 on v0

v2 whole, which is shorter than its diff:
```python
import functools
import math

import jax
import jax.numpy as jnp
from jax import lax
from jax.experimental import pallas as pl
from jax.experimental.pallas import tpu as pltpu
from jax.sharding import PartitionSpec as P

HD = 128
CAP = 4
LANES = 128
SLOTS = CAP + 2
EARLY = CAP + 1
epsilon = 1e-06
factor = math.log2(math.e) / math.sqrt(HD)
f32 = jnp.float32
bf16 = jnp.bfloat16
i32 = jnp.int32
vmem_limit = 20 * 2**20


def nt_dot(a, b):
    return lax.dot_general(a, b, (((1,), (1,)), ((), ())), preferred_element_type=f32)


def nn_dot(a, b):
    return jnp.dot(a, b, preferred_element_type=f32)


def iota(shape, axis):
    return lax.broadcasted_iota(i32, shape, axis)


def columns_of(row):
    pieces = []
    for start in range(0, row.shape[1], LANES):
        pieces.append(jnp.broadcast_to(row[:, start : start + LANES], (LANES, LANES)).T)
    return jnp.concatenate(pieces, axis=0)


def head_cols(head):
    return pl.ds(pl.multiple_of(head * HD, HD), HD)


def dequantized(raw, scales, which, head, first, cols, scale_rows):
    parts = []
    for piece in range(raw.shape[0] // scale_rows):
        rows = slice(piece * scale_rows, (piece + 1) * scale_rows)
        parts.append((raw[rows, cols].astype(f32) * scales[which, first + piece, head]).astype(bf16))
    return jnp.concatenate(parts, axis=0)


def tail_kernel(scale_rows, scales, raw, out):
    first = scales.shape[1] - raw.shape[0] // scale_rows
    for head in range(raw.shape[1] // HD):
        cols = slice(head * HD, (head + 1) * HD)
        out[:, cols] = dequantized(raw, scales, 1, head, first, cols, scale_rows)


def table_kernel(scale_rows, scales, ids, k_raw, tail_key, v_raw, table, front_key, front_value, tail_value, sums):
    tokens = ids.shape[1]
    half = tokens // 2
    heads = v_raw.shape[1] // HD
    row = ids[...]
    local = row - row[:, 0:1]
    last = local[:, tokens - 1 :]
    slot = iota((2 * 8, tokens), 0)
    token = iota((2 * 8, tokens), 1)
    picked = (slot <= CAP) & (local == slot)
    picked = picked | ((slot == EARLY) & (local == last) & (token < half))
    picked = picked.astype(f32)
    pick = picked.astype(bf16)
    for head in range(heads):
        cols = slice(head * HD, (head + 1) * HD)
        front = dequantized(k_raw, scales, 1, head, 0, cols, scale_rows)
        front_key[:, cols] = front
        found = nn_dot(pick[:, :half], front) + nn_dot(pick[:, half:], tail_key[:, cols])
        for index in range(SLOTS):
            sums[head : head + 1, index * HD : (index + 1) * HD] = found[index : index + 1]
        value = dequantized(v_raw, scales, 2, head, 0, cols, scale_rows)
        front_value[cols, :] = value[:half].T
        tail_value[cols, :] = value[half:].T
        found = nn_dot(pick, value)
        for index in range(SLOTS):
            sums[head : head + 1, (SLOTS + index) * HD : (SLOTS + index + 1) * HD] = found[index : index + 1]
    count = jnp.sum(picked, axis=1, keepdims=True).astype(i32)
    lane = iota((heads, LANES), 1)
    meta = jnp.zeros((heads, LANES), i32)
    for index in range(SLOTS):
        seg = row[:, 0:1] + (last if index == EARLY else index)
        number = count[index : index + 1]
        for place, value in enumerate((seg & 127, seg >> 7, number & 127, number >> 7)):
            meta = jnp.where(lane == 4 * index + place, value, meta)
    sums[:, 2 * SLOTS * HD :] = meta.astype(f32)
    table[...] = jnp.broadcast_to(sums[...].astype(bf16)[None], table.shape)


def with_ones(value):
    return jnp.concatenate([value, jnp.ones((16, value.shape[1]), bf16)], axis=0)


def local_kernel(
    scale_rows, scales, ids, q_raw, front_key, tail_key, front_value, tail_value,
    query_out, out, tops, totals, near, far,
):
    tokens = ids.shape[1]
    half = tokens // 2
    heads = q_raw.shape[1] // HD
    row = ids[...]
    column = columns_of(row)
    for mask, start, width in ((near, 0, half), (far, half, tokens)):
        for left in range(0, half, LANES):
            query = iota((width, LANES), 1) + (start + left)
            live = column[:width] == row[:, start + left : start + left + LANES]
            live = live & (iota((width, LANES), 0) <= query)
            mask[:, left : left + LANES] = jnp.where(live, 0.0, -jnp.inf)

    def one_head(head):
        cols = head_cols(head)
        query = dequantized(q_raw, scales, 0, head, 0, cols, scale_rows)
        query_out[:, cols] = query
        scores = (
            nt_dot(front_key[:, cols], query[:half]) * factor + near[...],
            nt_dot(jnp.concatenate([front_key[:, cols], tail_key[:, cols]], axis=0), query[half:]) * factor + far[...],
        )
        values = (
            front_value[cols, :],
            jnp.concatenate([front_value[cols, :], tail_value[cols, :]], axis=1),
        )
        for part in range(2):
            where = slice(part * half, (part + 1) * half)
            top = jnp.max(scores[part], axis=0, keepdims=True)
            weight = jnp.exp2(scores[part] - top).astype(bf16)
            found = nn_dot(with_ones(values[part]), weight)
            out[cols, where] = found[:HD]
            tops[pl.ds(head, 1), where] = top
            totals[pl.ds(head, 1), where] = found[HD : HD + 1]

    def body(pair, carry):
        one_head(2 * pair)
        one_head(2 * pair + 1)
        return carry

    lax.fori_loop(0, heads // 2, body, 0)


def landmark_kernel(
    device_count,
    place, ids, query, local, tops, totals, table,
    open_out, open_tops, open_totals, done_out, done_squares, prev_mask,
    picks, bias,
):
    tokens = ids.shape[1]
    half = tokens // 2
    heads = query.shape[1] // HD
    lands = CAP * device_count
    land_pad, entries = picks.shape[1:]
    me = place[0]
    row = ids[...]
    first = row[:, 0:1]
    info = table[:, 2 * SLOTS * HD :].astype(f32).T
    entry = iota((1, entries), 1)
    device = entry // heads
    entry_head = entry - device * heads
    land = iota((land_pad, entries), 0)
    count = jnp.zeros((land_pad, 1), f32)
    for index in range(SLOTS):
        seg = info[4 * index : 4 * index + 1] + 128.0 * info[4 * index + 1 : 4 * index + 2]
        number = info[4 * index + 2 : 4 * index + 3] + 128.0 * info[4 * index + 3 : 4 * index + 4]
        if index == EARLY:
            picked = (land == lands) & (device == me - 1)
        else:
            is_open = seg == first.astype(f32)
            picked = (land < lands) & (land.astype(f32) == seg)
            picked = picked | ((land == lands) & is_open & (device < me - 1))
            picked = picked | ((land == lands + 1) & is_open & (device < me))
            picked = picked | ((land == lands + 2) & is_open & (device == me - 1))
        picked = picked.astype(f32)
        picks[index] = picked.astype(bf16)
        count = count + jnp.sum(
            picked * jnp.where(entry_head == 0, number, 0.0), axis=1, keepdims=True
        )
    inverse = jnp.broadcast_to(1.0 / jnp.maximum(count, 1.0), (land_pad, HD))
    amount = jnp.broadcast_to(count, (land_pad, LANES))
    log_count = jnp.log2(jnp.maximum(amount, 1.0))
    for left in range(0, tokens, LANES):
        seg = row[:, left : left + LANES]
        index = iota((land_pad, LANES), 0)
        run = lands if left < half else lands + 1
        live = ((index < lands) & (index < seg)) | ((index == run) & (seg == first) & (amount > 0.5))
        bias[:, left : left + LANES] = jnp.where(live, log_count, -jnp.inf)
    tail = count[lands + 2 : lands + 3].astype(i32)
    for left in range(0, half, LANES):
        live = (iota((half, LANES), 0) >= half - tail) & (row[:, left : left + LANES] == first)
        prev_mask[:, left : left + LANES] = jnp.where(live, 0.0, -jnp.inf)

    def one_head(head):
        cols = head_cols(head)
        mine = (entry_head == head).astype(f32).astype(bf16)
        key = jnp.zeros((land_pad, HD), f32)
        value = jnp.zeros((land_pad, HD), f32)
        for index in range(SLOTS):
            pick = picks[index] * mine
            key = key + nn_dot(pick, table[:, index * HD : (index + 1) * HD])
            value = value + nn_dot(pick, table[:, (SLOTS + index) * HD : (SLOTS + index + 1) * HD])
        key = (key * inverse).astype(bf16)
        value = (value * inverse).astype(bf16)
        value = jnp.concatenate([value, jnp.ones((land_pad, 16), bf16)], axis=1)
        score = nt_dot(key, query[:, cols]) * factor + bias[...]
        top = tops[pl.ds(head, 1), :]
        new_top = jnp.maximum(top, jnp.max(score, axis=0, keepdims=True))
        shrink = jnp.exp2(top - new_top)
        weight = jnp.exp2(score - new_top).astype(bf16)
        found = lax.dot_general(value, weight, (((0,), (0,)), ((), ())), preferred_element_type=f32)
        total = totals[pl.ds(head, 1), :] * shrink + found[HD : HD + 1]
        found = local[cols, :] * shrink + found[:HD]
        open_tops[pl.ds(head, 1), :] = new_top[:, :half]
        open_totals[pl.ds(head, 1), :] = total[:, :half]
        open_out[cols, :] = found[:, :half]
        done = found[:, half:] * (1.0 / total[:, half:])
        done_out[cols, :] = done
        return jnp.sum(done * done, axis=0, keepdims=True)

    def body(pair, squares):
        return squares + one_head(2 * pair) + one_head(2 * pair + 1)

    done_squares[...] = lax.fori_loop(0, heads // 2, body, jnp.zeros((1, half), f32))


def halo_kernel(
    query, local, tops, totals, prev_mask, done_squares, prev_key, prev_value,
    out, squares,
):
    half = prev_mask.shape[0]
    heads = query.shape[1] // HD

    def one_head(head):
        cols = head_cols(head)
        score = nt_dot(prev_key[:, cols], query[:half, cols]) * factor + prev_mask[...]
        top = tops[pl.ds(head, 1), :]
        new_top = jnp.maximum(top, jnp.max(score, axis=0, keepdims=True))
        shrink = jnp.exp2(top - new_top)
        weight = jnp.exp2(score - new_top).astype(bf16)
        found = nn_dot(with_ones(prev_value[cols, :]), weight)
        total = totals[pl.ds(head, 1), :] * shrink + found[HD : HD + 1]
        done = (local[cols, :] * shrink + found[:HD]) * (1.0 / total)
        out[cols, :] = done
        return jnp.sum(done * done, axis=0, keepdims=True)

    def body(pair, carry):
        return carry + one_head(2 * pair) + one_head(2 * pair + 1)

    squares[:, :half] = lax.fori_loop(0, heads // 2, body, jnp.zeros((1, half), f32))
    squares[:, half:] = done_squares[...]


def scale_kernel(width, count, *refs):
    parts, (gain, front, back, out) = refs[:count], refs[count:]
    total = parts[0][...]
    for ref in parts[1:]:
        total = total + ref[...]
    norm = lax.rsqrt(total / width + epsilon)
    half = front.shape[1]
    heads = front.shape[0] // HD
    gains = columns_of(gain[...])
    for head in range(heads):
        cols = slice(head * HD, (head + 1) * HD)
        for source, start in ((front, 0), (back, half)):
            for left in range(0, half, LANES):
                rows = slice(start + left, start + left + LANES)
                value = source[cols, left : left + LANES] * norm[:, rows] * gains[cols]
                out[rows, cols] = value.astype(bf16).T


def on_device(q_raw, k_raw, v_raw, block_scales, segment_ids, norm_gain):
    tokens, width = q_raw.shape
    half = tokens // 2
    heads = width // HD
    scale_rows = tokens // block_scales.shape[1]
    devices = lax.axis_size("seq")
    head_devices = lax.axis_size("head")
    entries = devices * heads
    land_pad = -(-(CAP * devices + 3) // 16) * 16
    smem = pl.BlockSpec(memory_space=pltpu.SMEM)
    vmem = pl.BlockSpec(memory_space=pltpu.VMEM)
    sds = jax.ShapeDtypeStruct
    ids = segment_ids.reshape(1, tokens)
    wide = 2 * SLOTS * HD + LANES

    def call(kernel, name, out_shape, in_specs, args, flops, moved, scratch=(), out_specs=None, limit=vmem_limit, **more):
        return pl.pallas_call(
            kernel,
            name=name,
            out_shape=out_shape,
            in_specs=in_specs,
            out_specs=jax.tree.map(lambda _: vmem, out_shape) if out_specs is None else out_specs,
            scratch_shapes=list(scratch),
            compiler_params=pltpu.CompilerParams(vmem_limit_bytes=limit),
            cost_estimate=pl.CostEstimate(flops=flops, bytes_accessed=moved, transcendentals=0),
            **more,
        )(*args)

    def shifted(block):
        return lax.ppermute(block, "seq", [(i - 1, i) for i in range(1, devices)])

    tail_key = call(
        functools.partial(tail_kernel, scale_rows), "tail", sds((half, width), bf16),
        [smem, pl.BlockSpec((half, width), lambda s: (1, 0))], (block_scales, k_raw),
        half * width, 4 * half * width, grid=(1,), out_specs=pl.BlockSpec((half, width), lambda s: (0, 0)),
    )
    prev_key = shifted(tail_key)
    table, front_key, front_value, tail_value = call(
        functools.partial(table_kernel, scale_rows), "table",
        [sds((devices, heads, wide), bf16), sds((half, width), bf16), sds((width, half), bf16), sds((width, half), bf16)],
        [smem, pl.BlockSpec((1, tokens), lambda s: (0, 0)), pl.BlockSpec((half, width), lambda s: (0, 0)),
         pl.BlockSpec((half, width), lambda s: (0, 0)), pl.BlockSpec((tokens, width), lambda s: (0, 0))],
        (block_scales, ids, k_raw, tail_key, v_raw),
        64 * tokens * width, 4 * tokens * width, grid=(1,),
        out_specs=[
            pl.BlockSpec((devices, heads, wide), lambda s: (0, 0, 0)), pl.BlockSpec((half, width), lambda s: (0, 0)),
            pl.BlockSpec((width, half), lambda s: (0, 0)), pl.BlockSpec((width, half), lambda s: (0, 0)),
        ],
        scratch=[pltpu.VMEM((heads, wide), f32)],
    )
    table = lax.all_to_all(table, "seq", 0, 0, tiled=True).reshape(entries, wide)
    prev_value = shifted(tail_value)
    query, local, tops, totals = call(
        functools.partial(local_kernel, scale_rows), "local",
        [sds((tokens, width), bf16), sds((width, tokens), f32), sds((heads, tokens), f32), sds((heads, tokens), f32)],
        [smem] + [vmem] * 6, (block_scales, ids, q_raw, front_key, tail_key, front_value, tail_value),
        6 * half * tokens * width, 12 * tokens * width,
        scratch=[pltpu.VMEM((half, half), f32), pltpu.VMEM((tokens, half), f32)],
    )
    place = lax.axis_index("seq").astype(i32).reshape(1)
    part, tops, totals, back, back_squares, prev_mask = call(
        functools.partial(landmark_kernel, devices), "landmark",
        [sds((width, half), f32), sds((heads, half), f32), sds((heads, half), f32), sds((width, half), f32), sds((1, half), f32), sds((half, half), f32)],
        [smem] + [vmem] * 6, (place, ids, query, local, tops, totals, table),
        half * tokens * width, 12 * tokens * width,
        scratch=[pltpu.VMEM((SLOTS, land_pad, entries), bf16), pltpu.VMEM((land_pad, tokens), f32)],
    )
    front, squares = call(
        halo_kernel, "halo", [sds((width, half), f32), sds((1, tokens), f32)],
        [vmem] * 8, (query, part, tops, totals, prev_mask, back_squares, prev_key, prev_value),
        2 * half * tokens * width, 8 * tokens * width,
    )
    parts = [squares] + [
        lax.ppermute(squares, "head", [(i, (i + d) % head_devices) for i in range(head_devices)])
        for d in range(1, head_devices)
    ]
    return call(
        functools.partial(scale_kernel, width * head_devices, head_devices), "scale", sds((tokens, width), bf16),
        [vmem] * (head_devices + 3), (*parts, norm_gain.reshape(1, width), front, back),
        3 * tokens * width, 6 * tokens * width,
    )


def solution(mesh):
    in_specs = (
        P("seq", "head"), P("seq", "head"), P("seq", "head"),
        P(None, "seq", "head"), P("seq"), P("head"),
    )
    return jax.shard_map(
        on_device, mesh=mesh, in_specs=in_specs, out_specs=P("seq", "head"), check_vma=False
    )
```

time: 244 us -> 52 us (0.21)
  the two profiles are of different devices: /device:TPU:0 before, /device:TPU:16 now
where the time goes in v2:
time: 52 us; the launch traced here: 51.4 us
  Pallas kernels  18 us (35%)
  starting transfers between devices  13.8 us (27%)
  local copies, waits for them, and re-layouts  10.5 us (20%)
  waiting for transfers between devices  9.05 us (17%)
    pallas_call x6, Pallas kernels, call(): pl.pallas_call(kernel, name=name, out_shape=out_shape, in_specs=in_specs,...  18 us
    unnamed x28, local copies, waits for them, and re-layouts  10.5 us
    ppermute x2, starting transfers between devices, shifted(): return lax.ppermute(block, 'seq', [(i - 1, i) for i in range(1, devices)])  6.85 us
    all_to_all x1, waiting for transfers between devices, on_device(): lax.all_to_all(table, 'seq', 0, 0, tiled=True).reshape(entries, wide)  6.19 us
    all_to_all x1, starting transfers between devices, on_device(): lax.all_to_all(table, 'seq', 0, 0, tiled=True).reshape(entries, wide)  5.14 us
    ppermute x3, waiting for transfers between devices, on_device(): lax.ppermute(squares, 'head', [(i, (i + d) % head_devices) for i in range...  2.86 us
    ppermute x3, starting transfers between devices, on_device(): lax.ppermute(squares, 'head', [(i, (i + d) % head_devices) for i in range...  1.79 us
  transfers between devices with their start and end apart: 6, of which 3 were waited for; matrix products, arithmetic and copies ran while one was open for 0% of the time, Pallas kernels for 23%

profile of v2, /device:TPU:16, one launch (start us, length us, event | category | flops | bytes accessed | tf_op | source)
XLA Modules:
  0.0 51.4 jit_solution(3701142448963207649)
XLA Ops:
  0.0 1.2 %copy-done = bf16[512,1024]{1,0:T(8,128)(2,1)S(1)} copy-done((bf16[512,1024]{1,0:T(8,128)(2,1)S(1)}, bf16[512,1024]{1,0:T(8,128)(2,1)}, u32[]{:S(2)}) %copy-start) | copy-done | bytes 1048600
  1.2 0.7 %copy-done.9 = f32[3,4,8]{2,1,0:T(4,128)S(1)} copy-done((f32[3,4,8]{2,1,0:T(4,128)S(1)}, f32[3,4,8]{2,1,0:T(4,128)}, u32[]{:S(2)}) %copy-start.9) | copy-done | bytes 408
  1.9 0.8 %tail.1.tail_key = bf16[256,1024]{1,0:T(8,128)(2,1)S(1)} custom-call(f32[3,4,8]{2,1,0:T(4,128)S(1)} %copy-done.9, bf16[512,1024]{1,0:T(8,128)(2,1)S(1)} %copy-done), custom_call_target="tpu_custom_call" | custom-call | flops 262144 | bytes 1048576 | tf_op jit(solution)/shard_map/tail/pallas_call | solution.py:293
  2.7 3.4 %collective-permute-start = (bf16[256,1024]{1,0:T(8,128)(2,1)S(1)}, bf16[256,1024]{1,0:T(8,128)(2,1)S(1)}, u32[]{:S(2)}, u32[]{:S(2)}) collective-permute-start(bf16[256,1024]{1,0:T(8,128)(2,1)S(1)} %tail.1.tail_key), channel_id=1, source_target_pairs={{0,4},{4,8},{8,12},{12,16},{16,20},{20,24},{24,28},{1,5},{5,9},{9,... | collective-permute-start | bytes 1572872 | tf_op jit(solution)/shard_map/ppermute | solution.py:306
  6.1 0.0 copy-start.4
  6.1 1.2 %copy-done.4 = bf16[512,1024]{1,0:T(8,128)(2,1)S(1)} copy-done((bf16[512,1024]{1,0:T(8,128)(2,1)S(1)}, bf16[512,1024]{1,0:T(8,128)(2,1)}, u32[]{:S(2)}) %copy-start.4) | copy-done | bytes 1048600
  7.3 0.7 %copy-done.11 = s32[512]{0:T(512)S(1)} copy-done((s32[512]{0:T(512)S(1)}, s32[512]{0:T(512)}, u32[]{:S(2)}) %copy-start.11) | copy-done | bytes 2072
  8.0 2.2 %table.1 = (bf16[8,8,1664]{2,1,0:T(8,128)(2,1)}, bf16[256,1024]{1,0:T(8,128)(2,1)S(1)}, bf16[1024,256]{1,0:T(8,128)(2,1)S(1)}, bf16[1024,256]{1,0:T(8,128)(2,1)}) custom-call(f32[3,4,8]{2,1,0:T(4,128)S(1)} %copy-done.9, s32[1,512]{1,0:T(1,128)S(1)} %bitcast.5, bf16[512,1024]{1,0:T(8,128)(2,1)S(1)} %copy-done, bf16[256,1024]{1,0:T(8,128)(2,1)S(1)} %tail.1.tail_key, ...), custom_call_target="tpu_custom_call" | custom-call | flops 33554432 | bytes 2097152 | tf_op jit(solution)/shard_map/table/pallas_call | solution.py:293
  10.2 0.8 %copy-done.5 = bf16[256,1024]{1,0:T(8,128)(2,1)} copy-done((bf16[256,1024]{1,0:T(8,128)(2,1)}, bf16[256,1024]{1,0:T(8,128)(2,1)S(1)}, u32[]{:S(2)}) %copy-start.5) | copy-done | bytes 524312
  11.0 0.8 %copy-done.7 = bf16[1024,256]{1,0:T(8,128)(2,1)} copy-done((bf16[1024,256]{1,0:T(8,128)(2,1)}, bf16[1024,256]{1,0:T(8,128)(2,1)S(1)}, u32[]{:S(2)}) %copy-start.7) | copy-done | bytes 524312
  11.8 3.4 %collective-permute-start.1 = (bf16[1024,256]{1,0:T(8,128)(2,1)}, bf16[1024,256]{1,0:T(8,128)(2,1)}, u32[]{:S(2)}, u32[]{:S(2)}) collective-permute-start(bf16[1024,256]{1,0:T(8,128)(2,1)} %get-tuple-element.23.tail_value), channel_id=1, source_target_pairs={{0,4},{4,8},{8,12},{12,16},{16,20},{20,24},{24,28},{1,5},{5,9},{9,... | collective-permute-start | bytes 1572872 | tf_op jit(solution)/shard_map/ppermute | solution.py:306
  15.3 5.1 %all-to-all-start = ((bf16[8,8,1664]{2,1,0:T(8,128)(2,1)}), bf16[8,8,1664]{2,1,0:T(8,128)(2,1)S(1)}, u32[]{:S(2)}, u32[]{:S(2)}) async-start(bf16[8,8,1664]{2,1,0:T(8,128)(2,1)} %get-tuple-element.28), calls=%async_computation | async-start | bytes 425984 | tf_op jit(solution)/shard_map/all_to_all | solution.py:327
  20.4 0.0 copy-done.3
  20.4 1.0 %copy-done.6 = bf16[256,1024]{1,0:T(8,128)(2,1)S(1)} copy-done((bf16[256,1024]{1,0:T(8,128)(2,1)S(1)}, bf16[256,1024]{1,0:T(8,128)(2,1)}, u32[]{:S(2)}) %copy-start.6) | copy-done | bytes 524312
  21.5 1.0 %copy-done.8 = bf16[1024,256]{1,0:T(8,128)(2,1)S(1)} copy-done((bf16[1024,256]{1,0:T(8,128)(2,1)S(1)}, bf16[1024,256]{1,0:T(8,128)(2,1)}, u32[]{:S(2)}) %copy-start.8) | copy-done | bytes 524312
  22.5 5.2 %local.1 = (bf16[512,1024]{1,0:T(8,128)(2,1)S(1)}, f32[1024,512]{1,0:T(8,128)S(1)}, f32[8,512]{1,0:T(8,128)S(1)}, f32[8,512]{1,0:T(8,128)S(1)}) custom-call(f32[3,4,8]{2,1,0:T(4,128)S(1)} %copy-done.10, s32[1,512]{1,0:T(1,128)S(1)} %bitcast.6, bf16[512,1024]{1,0:T(8,128)(2,1)S(1)} %copy-done.3, bf16[256,1024]{1,0:T(8,128)(2,1)S(1)} %copy-done.6, ...), custom_call_target="tpu_custom_call" | custom-call | flops 805306368 | bytes 6291456 | tf_op jit(solution)/shard_map/local/pallas_call | solution.py:293
  27.8 1.3 %copy-done.1 = f32[1024,512]{1,0:T(8,128)} copy-done((f32[1024,512]{1,0:T(8,128)}, f32[1024,512]{1,0:T(8,128)S(1)}, u32[]{:S(2)}) %copy-start.1) | copy-done | bytes 2097176
  29.1 6.2 %all-to-all-done = bf16[8,8,1664]{2,1,0:T(8,128)(2,1)S(1)} async-done(((bf16[8,8,1664]{2,1,0:T(8,128)(2,1)}), bf16[8,8,1664]{2,1,0:T(8,128)(2,1)S(1)}, u32[]{:S(2)}, u32[]{:S(2)}) %all-to-all-start) | async-done | bytes 213024 | tf_op jit(solution)/shard_map/all_to_all | solution.py:327
  35.3 1.6 %copy-done.2 = f32[1024,512]{1,0:T(8,128)S(1)} copy-done((f32[1024,512]{1,0:T(8,128)S(1)}, f32[1024,512]{1,0:T(8,128)}, u32[]{:S(2)}) %copy-start.2) | copy-done | bytes 2097176
  36.9 4.2 %landmark.1 = (f32[1024,256]{1,0:T(8,128)S(1)}, f32[8,256]{1,0:T(8,128)S(1)}, f32[8,256]{1,0:T(8,128)S(1)}, f32[1024,256]{1,0:T(8,128)S(1)}, f32[1,256]{1,0:T(1,128)S(1)}, /*index=5*/f32[256,256]{1,0:T(8,128)S(1)}) custom-call(s32[1]{0:T(128)} %bitcast.1.place, s32[1,512]{1,0:T(1,128)S(1)} %bitcast.7, bf16[512,1024]{1,0:T(8,128)(2,1)S(1)} %get-tuple-element.24.query, ...), custom_call_target="tpu_custom_call" | custom-call | flops 134217728 | bytes 6291456 | tf_op jit(solution)/shard_map/landmark/pallas_call | solution.py:293
  41.1 0.0 copy-start.13
  41.1 0.0 collective-permute-done.prev_key
  41.1 0.0 collective-permute-done.1.prev_value
  41.1 4.1 %halo.1 = (f32[1024,256]{1,0:T(8,128)S(1)}, f32[1,512]{1,0:T(1,128)S(1)}) custom-call(bf16[512,1024]{1,0:T(8,128)(2,1)S(1)} %get-tuple-element.24.query, f32[1024,256]{1,0:T(8,128)S(1)} %get-tuple-element.29.local, f32[8,256]{1,0:T(8,128)S(1)} %get-tuple-element.30.tops, f32[8,256]{1,0:T(8,128)S(1)} %get-tuple-element.31.totals, ...), custom_call_target="tpu_custom_call" | custom-call | flops 268435456 | bytes 4194304 | tf_op jit(solution)/shard_map/halo/pallas_call | solution.py:293
  45.2 0.1 collective-permute-start.4
  45.2 1.6 %collective-permute-start.3 = (f32[1,512]{1,0:T(1,128)S(1)}, f32[1,512]{1,0:T(1,128)S(1)}, u32[]{:S(2)}, u32[]{:S(2)}) collective-permute-start(f32[1,512]{1,0:T(1,128)S(1)} %get-tuple-element.34.refs_0_), channel_id=1, source_target_pairs={{0,2},{1,3},{2,0},{3,1},{4,6},{5,7},{6,4},{7,5},{8,10},{9,11},{10,... | collective-permute-start | bytes 6152 | tf_op jit(solution)/shard_map/ppermute | solution.py:350
  46.8 0.2 collective-permute-start.2
  47.0 0.0 collective-permute-done.4.refs_3_
  47.0 1.9 %collective-permute-done.3.refs_2_ = f32[1,512]{1,0:T(1,128)S(1)} collective-permute-done((f32[1,512]{1,0:T(1,128)S(1)}, f32[1,512]{1,0:T(1,128)S(1)}, u32[]{:S(2)}, u32[]{:S(2)}) %collective-permute-start.3) | collective-permute-done | bytes 2080 | tf_op jit(solution)/shard_map/ppermute | solution.py:350
  48.9 0.9 %collective-permute-done.2.refs_1_ = f32[1,512]{1,0:T(1,128)S(1)} collective-permute-done((f32[1,512]{1,0:T(1,128)S(1)}, f32[1,512]{1,0:T(1,128)S(1)}, u32[]{:S(2)}, u32[]{:S(2)}) %collective-permute-start.2) | collective-permute-done | bytes 2080 | tf_op jit(solution)/shard_map/ppermute | solution.py:350
  49.8 0.0 copy-done.13
  49.8 1.6 %scale.1 = bf16[512,1024]{1,0:T(8,128)(2,1)} custom-call(f32[1,512]{1,0:T(1,128)S(1)} %get-tuple-element.34.refs_0_, f32[1,512]{1,0:T(1,128)S(1)} %collective-permute-done.2.refs_1_, f32[1,512]{1,0:T(1,128)S(1)} %collective-permute-done.3.refs_2_, f32[1,512]{1,0:T(1,128)S(1)} %collective-permute-done.4.refs_3_, f32[1,1024]{1,0:T(1,128)S(1)} %bitcast.8, ...), custom_call_target="tpu_custom_call" | custom-call | flops 1572864 | bytes 3145728 | tf_op jit(solution)/shard_map/scale/pallas_call | solution.py:293
  (14 shorter events, 0.0 us)
Async XLA Ops:
  0.0 1.2 %copy-start = (bf16[512,1024]{1,0:T(8,128)(2,1)S(1)}, bf16[512,1024]{1,0:T(8,128)(2,1)}, u32[]{:S(2)}) copy-start(bf16[512,1024]{1,0:T(8,128)(2,1)} %k_raw.1) | copy-start | bytes 3145732
  1.2 0.7 %copy-start.9 = (f32[3,4,8]{2,1,0:T(4,128)S(1)}, f32[3,4,8]{2,1,0:T(4,128)}, u32[]{:S(2)}) copy-start(f32[3,4,8]{2,1,0:T(4,128)} %scales.5) | copy-start | bytes 1156
  1.9 18.5 %copy-start.3 = (bf16[512,1024]{1,0:T(8,128)(2,1)S(1)}, bf16[512,1024]{1,0:T(8,128)(2,1)}, u32[]{:S(2)}) copy-start(bf16[512,1024]{1,0:T(8,128)(2,1)} %q_raw.1) | copy-start | bytes 3145732
  1.9 18.5 %copy-start.10 = (f32[3,4,8]{2,1,0:T(4,128)S(1)}, f32[3,4,8]{2,1,0:T(4,128)}, u32[]{:S(2)}) copy-start(f32[3,4,8]{2,1,0:T(4,128)} %scales.5) | copy-start | bytes 1156
  1.9 18.5 %copy-start.12 = (s32[512]{0:T(512)S(1)}, s32[512]{0:T(512)}, u32[]{:S(2)}) copy-start(s32[512]{0:T(512)} %param.10) | copy-start | bytes 6148
  2.7 38.4 %collective-permute-start = (bf16[256,1024]{1,0:T(8,128)(2,1)S(1)}, bf16[256,1024]{1,0:T(8,128)(2,1)S(1)}, u32[]{:S(2)}, u32[]{:S(2)}) collective-permute-start(bf16[256,1024]{1,0:T(8,128)(2,1)S(1)} %tail.1.tail_key), channel_id=1, source_target_pairs={{0,4},{4,8},{8,12},{12,16},{16,20},{20,24},{24,28},{1,5},{5,9},{9,... | collective-permute-start | bytes 1572872 | tf_op jit(solution)/shard_map/ppermute | solution.py:306
  6.1 1.2 %copy-start.4 = (bf16[512,1024]{1,0:T(8,128)(2,1)S(1)}, bf16[512,1024]{1,0:T(8,128)(2,1)}, u32[]{:S(2)}) copy-start(bf16[512,1024]{1,0:T(8,128)(2,1)} %v_raw.1) | copy-start | bytes 3145732
  7.3 0.7 %copy-start.11 = (s32[512]{0:T(512)S(1)}, s32[512]{0:T(512)}, u32[]{:S(2)}) copy-start(s32[512]{0:T(512)} %param.10) | copy-start | bytes 6148
  10.2 0.8 %copy-start.5 = (bf16[256,1024]{1,0:T(8,128)(2,1)}, bf16[256,1024]{1,0:T(8,128)(2,1)S(1)}, u32[]{:S(2)}) copy-start(bf16[256,1024]{1,0:T(8,128)(2,1)S(1)} %get-tuple-element.21.front_key) | copy-start | bytes 1572868
  11.0 0.8 %copy-start.7 = (bf16[1024,256]{1,0:T(8,128)(2,1)}, bf16[1024,256]{1,0:T(8,128)(2,1)S(1)}, u32[]{:S(2)}) copy-start(bf16[1024,256]{1,0:T(8,128)(2,1)S(1)} %get-tuple-element.22.front_value) | copy-start | bytes 1572868
  11.8 29.3 %collective-permute-start.1 = (bf16[1024,256]{1,0:T(8,128)(2,1)}, bf16[1024,256]{1,0:T(8,128)(2,1)}, u32[]{:S(2)}, u32[]{:S(2)}) collective-permute-start(bf16[1024,256]{1,0:T(8,128)(2,1)} %get-tuple-element.23.tail_value), channel_id=1, source_target_pairs={{0,4},{4,8},{8,12},{12,16},{16,20},{20,24},{24,28},{1,5},{5,9},{9,... | collective-permute-start | bytes 1572872 | tf_op jit(solution)/shard_map/ppermute | solution.py:306
  15.3 20.0 %all-to-all-start = ((bf16[8,8,1664]{2,1,0:T(8,128)(2,1)}), bf16[8,8,1664]{2,1,0:T(8,128)(2,1)S(1)}, u32[]{:S(2)}, u32[]{:S(2)}) async-start(bf16[8,8,1664]{2,1,0:T(8,128)(2,1)} %get-tuple-element.28), calls=%async_computation | async-start | bytes 425984 | tf_op jit(solution)/shard_map/all_to_all | solution.py:327
  20.4 1.0 %copy-start.6 = (bf16[256,1024]{1,0:T(8,128)(2,1)S(1)}, bf16[256,1024]{1,0:T(8,128)(2,1)}, u32[]{:S(2)}) copy-start(bf16[256,1024]{1,0:T(8,128)(2,1)} %copy-done.5) | copy-start | bytes 1572868
  21.5 1.0 %copy-start.8 = (bf16[1024,256]{1,0:T(8,128)(2,1)S(1)}, bf16[1024,256]{1,0:T(8,128)(2,1)}, u32[]{:S(2)}) copy-start(bf16[1024,256]{1,0:T(8,128)(2,1)} %copy-done.7) | copy-start | bytes 1572868
  27.8 1.3 %copy-start.1 = (f32[1024,512]{1,0:T(8,128)}, f32[1024,512]{1,0:T(8,128)S(1)}, u32[]{:S(2)}) copy-start(f32[1024,512]{1,0:T(8,128)S(1)} %get-tuple-element.25.local) | copy-start | bytes 6291460
  35.3 1.6 %copy-start.2 = (f32[1024,512]{1,0:T(8,128)S(1)}, f32[1024,512]{1,0:T(8,128)}, u32[]{:S(2)}) copy-start(f32[1024,512]{1,0:T(8,128)} %copy-done.1) | copy-start | bytes 6291460
  41.1 8.8 %copy-start.13 = (f32[1024]{0:T(1024)S(1)}, f32[1024]{0:T(1024)}, u32[]{:S(2)}) copy-start(f32[1024]{0:T(1024)} %param.11) | copy-start | bytes 12292
  45.2 1.8 %collective-permute-start.4 = (f32[1,512]{1,0:T(1,128)S(1)}, f32[1,512]{1,0:T(1,128)S(1)}, u32[]{:S(2)}, u32[]{:S(2)}) collective-permute-start(f32[1,512]{1,0:T(1,128)S(1)} %get-tuple-element.34.refs_0_), channel_id=1, source_target_pairs={{0,3},{1,0},{2,1},{3,2},{4,7},{5,4},{6,5},{7,6},{8,11},{9,8},{10,9... | collective-permute-start | bytes 6152 | tf_op jit(solution)/shard_map/ppermute | solution.py:350
  45.2 3.7 %collective-permute-start.3 = (f32[1,512]{1,0:T(1,128)S(1)}, f32[1,512]{1,0:T(1,128)S(1)}, u32[]{:S(2)}, u32[]{:S(2)}) collective-permute-start(f32[1,512]{1,0:T(1,128)S(1)} %get-tuple-element.34.refs_0_), channel_id=1, source_target_pairs={{0,2},{1,3},{2,0},{3,1},{4,6},{5,7},{6,4},{7,5},{8,10},{9,11},{10,... | collective-permute-start | bytes 6152 | tf_op jit(solution)/shard_map/ppermute | solution.py:350
  46.8 3.0 %collective-permute-start.2 = (f32[1,512]{1,0:T(1,128)S(1)}, f32[1,512]{1,0:T(1,128)S(1)}, u32[]{:S(2)}, u32[]{:S(2)}) collective-permute-start(f32[1,512]{1,0:T(1,128)S(1)} %get-tuple-element.34.refs_0_), channel_id=1, source_target_pairs={{0,1},{1,2},{2,3},{3,0},{4,5},{5,6},{6,7},{7,4},{8,9},{9,10},{10,1... | collective-permute-start | bytes 6152 | tf_op jit(solution)/shard_map/ppermute | solution.py:350

commit v3 on v2

v3 whole, which is shorter than its diff:
```python
import functools
import math

import jax
import jax.numpy as jnp
from jax import lax
from jax.experimental import pallas as pl
from jax.experimental.pallas import tpu as pltpu
from jax.sharding import PartitionSpec as P


HD = 128
CAP = 4
LANES = 128
SLOTS = CAP + 2
EARLY = CAP + 1
epsilon = 1e-06
factor = math.log2(math.e) / math.sqrt(HD)
f32 = jnp.float32
bf16 = jnp.bfloat16
i32 = jnp.int32
vmem_limit = 20 * 2**20
whole_vmem = 60 * 1024 * 2**10
pipeline_depth = 2


def nt_dot(a, b):
    return lax.dot_general(a, b, (((1,), (1,)), ((), ())), preferred_element_type=f32)


def nn_dot(a, b):
    return jnp.dot(a, b, preferred_element_type=f32)


def iota(shape, axis):
    return lax.broadcasted_iota(i32, shape, axis)


def columns_of(row):
    pieces = []
    for start in range(0, row.shape[1], LANES):
        pieces.append(jnp.broadcast_to(row[:, start : start + LANES], (LANES, LANES)).T)
    return jnp.concatenate(pieces, axis=0)


def dequantized(raw, scales, which, head, cols, scale_rows, first=0):
    parts = []
    for piece in range(raw.shape[0] // scale_rows):
        rows = slice(piece * scale_rows, (piece + 1) * scale_rows)
        parts.append((raw[rows, cols].astype(f32) * scales[which, first + piece, head]).astype(bf16))
    return jnp.concatenate(parts, axis=0)


def tail_kernel(scale_rows, scales, raw, out):
    first = scales.shape[1] - raw.shape[0] // scale_rows
    heads = raw.shape[1] // HD
    for head in range(heads):
        cols = slice(head * HD, (head + 1) * HD)
        index = pl.program_id(0) * heads + head
        out[:, cols] = dequantized(raw, scales, 1, index, cols, scale_rows, first)


def table_kernel(scale_rows, scales, ids, k_raw, v_raw, table, tail_value, sums, parts):
    step = pl.program_id(0)
    tokens = ids.shape[1]
    half = tokens // 2
    heads = v_raw.shape[1] // HD
    all_heads = sums.shape[0]
    row = ids[...]
    local = row - row[:, 0:1]
    last = local[:, tokens - 1 :]
    slot = iota((2 * 8, tokens), 0)
    token = iota((2 * 8, tokens), 1)
    picked = (slot <= CAP) & (local == slot)
    picked = picked | ((slot == EARLY) & (local == last) & (token < half))
    picked = picked.astype(f32)
    pick = picked.astype(bf16)
    for head in range(heads):
        cols = slice(head * HD, (head + 1) * HD)
        index = step * heads + head
        key = dequantized(k_raw, scales, 1, index, cols, scale_rows)
        value = dequantized(v_raw, scales, 2, index, cols, scale_rows)
        tail_value[cols, :] = value[half:].T
        parts[index, 0] = nn_dot(pick, key)[:8]
        parts[index, 1] = nn_dot(pick, value)[:8]

    @pl.when(step == pl.num_programs(0) - 1)
    def _():
        count = jnp.sum(picked, axis=1, keepdims=True).astype(i32)
        lane = iota((all_heads, LANES), 1)
        meta = jnp.zeros((all_heads, LANES), i32)
        for index in range(SLOTS):
            seg = row[:, 0:1] + (last if index == EARLY else index)
            number = count[index : index + 1]
            for place, value in enumerate((seg & 127, seg >> 7, number & 127, number >> 7)):
                meta = jnp.where(lane == 4 * index + place, value, meta)
        for head in range(all_heads):
            for which in range(2):
                found = parts[head, which]
                for place in range(SLOTS):
                    where = slice((which * SLOTS + place) * HD, (which * SLOTS + place + 1) * HD)
                    sums[head : head + 1, where] = found[place : place + 1]
        sums[:, 2 * SLOTS * HD :] = meta.astype(f32)
        table[...] = jnp.broadcast_to(sums[...].astype(bf16)[None], table.shape)


def with_ones(value):
    return jnp.concatenate([value, jnp.ones((16, value.shape[1]), bf16)], axis=0)


def main_kernel(
    scale_rows, device_count,
    place, scales, ids, table, gain, q_raw, k_raw, v_raw,
    query_out, open_out, open_tops, open_totals, back_out, back_squares, prev_mask,
    near, far, picks, bias, inverse,
):
    step = pl.program_id(0)
    tokens = ids.shape[1]
    half = tokens // 2
    heads = q_raw.shape[1] // HD
    lands = CAP * device_count
    land_pad, entries = picks.shape[1:]
    all_heads = entries // device_count
    entry = iota((1, entries), 1)
    entry_device = entry // all_heads
    entry_head = entry - entry_device * all_heads

    @pl.when(step == 0)
    def _():
        me = place[0]
        row = ids[...]
        first = row[:, 0:1]
        column = columns_of(row)
        for mask, start, width in ((near, 0, half), (far, half, tokens)):
            for left in range(0, half, LANES):
                query = iota((width, LANES), 1) + (start + left)
                live = column[:width] == row[:, start + left : start + left + LANES]
                live = live & (iota((width, LANES), 0) <= query)
                mask[:, left : left + LANES] = jnp.where(live, 0.0, -jnp.inf)
        info = table[:, 2 * SLOTS * HD :].astype(f32).T
        land = iota((land_pad, entries), 0)
        count = jnp.zeros((land_pad, 1), f32)
        for index in range(SLOTS):
            seg = info[4 * index : 4 * index + 1] + 128.0 * info[4 * index + 1 : 4 * index + 2]
            number = info[4 * index + 2 : 4 * index + 3] + 128.0 * info[4 * index + 3 : 4 * index + 4]
            if index == EARLY:
                picked = (land == lands) & (entry_device == me - 1)
            else:
                is_open = seg == first.astype(f32)
                picked = (land < lands) & (land.astype(f32) == seg)
                picked = picked | ((land == lands) & is_open & (entry_device < me - 1))
                picked = picked | ((land == lands + 1) & is_open & (entry_device < me))
                picked = picked | ((land == lands + 2) & is_open & (entry_device == me - 1))
            picked = picked.astype(f32)
            picks[index] = picked.astype(bf16)
            count = count + jnp.sum(
                picked * jnp.where(entry_head == 0, number, 0.0), axis=1, keepdims=True
            )
        inverse[...] = jnp.broadcast_to(1.0 / jnp.maximum(count, 1.0), inverse.shape)
        amount = jnp.broadcast_to(count, (land_pad, LANES))
        log_count = jnp.log2(jnp.maximum(amount, 1.0))
        for left in range(0, tokens, LANES):
            seg = row[:, left : left + LANES]
            index = iota((land_pad, LANES), 0)
            run = lands if left < half else lands + 1
            live = ((index < lands) & (index < seg)) | ((index == run) & (seg == first) & (amount > 0.5))
            bias[:, left : left + LANES] = jnp.where(live, log_count, -jnp.inf)
        tail = count[lands + 2 : lands + 3].astype(i32)
        for left in range(0, half, LANES):
            live = (iota((half, LANES), 0) >= half - tail) & (row[:, left : left + LANES] == first)
            prev_mask[:, left : left + LANES] = jnp.where(live, 0.0, -jnp.inf)
        back_squares[...] = jnp.zeros(back_squares.shape, f32)

    def prepared(head):
        cols = slice(head * HD, (head + 1) * HD)
        index = step * heads + head
        query = dequantized(q_raw, scales, 0, index, cols, scale_rows)
        key = dequantized(k_raw, scales, 1, index, cols, scale_rows)
        value = dequantized(v_raw, scales, 2, index, cols, scale_rows).T
        query_out[:, cols] = query[:half]
        mine = (entry_head == index).astype(f32).astype(bf16)
        land_key = jnp.zeros((land_pad, HD), f32)
        land_value = jnp.zeros((land_pad, HD), f32)
        for slot in range(SLOTS):
            pick = picks[slot] * mine
            land_key = land_key + nn_dot(pick, table[:, slot * HD : (slot + 1) * HD])
            land_value = land_value + nn_dot(pick, table[:, (SLOTS + slot) * HD : (SLOTS + slot + 1) * HD])
        land_key = (land_key * inverse[...]).astype(bf16)
        land_value = (land_value * inverse[...]).astype(bf16)
        land_value = jnp.concatenate([land_value, jnp.ones((land_pad, 16), bf16)], axis=1)
        return query, key, value, land_key, land_value

    ready = {}

    def scores_of(task):
        head, part = task
        if head not in ready:
            ready[head] = prepared(head)
        query, key, _, land_key, _ = ready[head]
        rows = slice(part * half, (part + 1) * half)
        mask = far if part else near
        score = nt_dot(key[: (part + 1) * half], query[rows]) * factor + mask[...]
        return score, nt_dot(land_key, query[rows]) * factor + bias[:, rows]

    tasks = [(head, part) for head in range(heads) for part in range(2)]
    scores = [scores_of(task) for task in tasks[:pipeline_depth]]
    for number, (head, part) in enumerate(tasks):
        if number + pipeline_depth < len(tasks):
            scores.append(scores_of(tasks[number + pipeline_depth]))
        cols = slice(head * HD, (head + 1) * HD)
        score, land_score = scores[number]
        _, _, value, _, land_value = ready[head]
        top = jnp.maximum(
            jnp.max(score, axis=0, keepdims=True), jnp.max(land_score, axis=0, keepdims=True)
        )
        weight = jnp.exp2(score - top).astype(bf16)
        land_weight = jnp.exp2(land_score - top).astype(bf16)
        found = nn_dot(with_ones(value[:, : (part + 1) * half]), weight)
        found = found + lax.dot_general(
            land_value, land_weight, (((0,), (0,)), ((), ())), preferred_element_type=f32
        )
        total = found[HD : HD + 1]
        if part == 0:
            open_out[cols, :] = found[:HD]
            open_tops[0, head : head + 1, :] = top
            open_totals[0, head : head + 1, :] = total
        else:
            done = found[:HD] * (1.0 / total)
            back_squares[...] += jnp.sum(done * done, axis=0, keepdims=True)
            back_out[:, cols] = done.T * gain[:, cols]


def halo_kernel(
    query, local, tops, totals, gain, prev_mask, done_squares, prev_key, prev_value,
    out, squares,
):
    half = prev_mask.shape[0]
    heads = query.shape[1] // HD
    per_step = tops.shape[1]
    chunk = 256
    tasks = [(head, left) for head in range(heads) for left in range(0, half, chunk)]

    def score_of(task):
        head, left = task
        cols = slice(head * HD, (head + 1) * HD)
        rows = slice(left, left + chunk)
        return nt_dot(prev_key[:, cols], query[rows, cols]) * factor + prev_mask[:, rows]

    def finish(task, score):
        head, left = task
        cols = slice(head * HD, (head + 1) * HD)
        rows = slice(left, left + chunk)
        step, place = head // per_step, head % per_step
        top = tops[step, place : place + 1, rows]
        new_top = jnp.maximum(top, jnp.max(score, axis=0, keepdims=True))
        shrink = jnp.exp2(top - new_top)
        weight = jnp.exp2(score - new_top).astype(bf16)
        found = nn_dot(with_ones(prev_value[cols, :]), weight)
        total = totals[step, place : place + 1, rows] * shrink + found[HD : HD + 1]
        done = (local[cols, rows] * shrink + found[:HD]) * (1.0 / total)
        return done

    sums = [jnp.zeros((1, chunk), f32)] * (half // chunk)
    depth = 2
    scores = [score_of(task) for task in tasks[:depth]]
    for number, task in enumerate(tasks):
        if number + depth < len(tasks):
            scores.append(score_of(tasks[number + depth]))
        done = finish(task, scores[number])
        head, left = task
        sums[left // chunk] = sums[left // chunk] + jnp.sum(done * done, axis=0, keepdims=True)
        out[left : left + chunk, head * HD : (head + 1) * HD] = done.T * gain[:, head * HD : (head + 1) * HD]
    for index, found in enumerate(sums):
        squares[:, index * chunk : (index + 1) * chunk] = found
    squares[:, half:] = done_squares[...]


def scale_kernel(width, count, *refs):
    parts, (front, back, out, ready, sems) = refs[:count], refs[count:]
    total = parts[0][...]
    for ref in parts[1:]:
        total = total + ref[...]
    norm = columns_of(lax.rsqrt(total / width + epsilon))
    half = front.shape[0]
    copies = []
    for part, source in enumerate((front, back)):
        for start in range(0, half, LANES):
            rows = slice(part * half + start, part * half + start + LANES)
            for left in range(0, front.shape[1], LANES):
                cols = slice(left, left + LANES)
                ready[rows, cols] = (source[start : start + LANES, cols] * norm[rows]).astype(bf16)
            copy = pltpu.make_async_copy(ready.at[rows], out.at[rows], sems.at[len(copies)])
            copy.start()
            copies.append(copy)
    for copy in copies:
        copy.wait()


def on_device(q_raw, k_raw, v_raw, block_scales, segment_ids, norm_gain):
    tokens, width = q_raw.shape
    half = tokens // 2
    heads = width // HD
    scale_rows = tokens // block_scales.shape[1]
    devices = lax.axis_size("seq")
    head_devices = lax.axis_size("head")
    entries = devices * heads
    land_pad = -(-(CAP * devices + 3) // 16) * 16
    smem = pl.BlockSpec(memory_space=pltpu.SMEM)
    vmem = pl.BlockSpec(memory_space=pltpu.VMEM)
    sds = jax.ShapeDtypeStruct
    ids = segment_ids.reshape(1, tokens)
    wide = 2 * SLOTS * HD + LANES

    def call(kernel, out_shape, in_specs, args, flops, moved, scratch=(), out_specs=None, limit=vmem_limit, **more):
        return pl.pallas_call(
            kernel,
            out_shape=out_shape,
            in_specs=in_specs,
            out_specs=jax.tree.map(lambda _: vmem, out_shape) if out_specs is None else out_specs,
            scratch_shapes=list(scratch),
            compiler_params=pltpu.CompilerParams(vmem_limit_bytes=limit),
            cost_estimate=pl.CostEstimate(flops=flops, bytes_accessed=moved, transcendentals=0),
            **more,
        )(*args)

    def shifted(block):
        return lax.ppermute(block, "seq", [(i - 1, i) for i in range(1, devices)])

    tail_steps = 2
    tail_key = call(
        functools.partial(tail_kernel, scale_rows), sds((half, width), bf16),
        [smem, pl.BlockSpec((half, width // tail_steps), lambda s: (1, s))], (block_scales, k_raw),
        half * width, 4 * half * width, grid=(tail_steps,), limit=whole_vmem,
        out_specs=pl.BlockSpec((half, width // tail_steps), lambda s: (0, s)),
    )
    prev_key = shifted(tail_key)
    table_steps = 4
    table_piece = width // table_steps
    table, tail_value = call(
        functools.partial(table_kernel, scale_rows),
        [sds((devices, heads, wide), bf16), sds((width, half), bf16)],
        [smem, pl.BlockSpec((1, tokens), lambda s: (0, 0))] + [pl.BlockSpec((tokens, table_piece), lambda s: (0, s))] * 2,
        (block_scales, ids, k_raw, v_raw),
        64 * tokens * width, 4 * tokens * width, grid=(table_steps,), limit=whole_vmem,
        out_specs=[pl.BlockSpec((devices, heads, wide), lambda s: (0, 0, 0)), pl.BlockSpec((table_piece, half), lambda s: (s, 0))],
        scratch=[pltpu.VMEM((heads, wide), f32), pltpu.VMEM((heads, 2, 8, HD), f32)],
    )
    table = lax.all_to_all(table, "seq", 0, 0, tiled=True)
    table = table.reshape(entries, wide)
    prev_value = shifted(tail_value)
    place = lax.axis_index("seq").astype(i32).reshape(1)
    gain = norm_gain.reshape(1, width)
    step_heads = 4
    steps = heads // step_heads
    piece = step_heads * HD

    def whole(*shape):
        return pl.BlockSpec(shape, lambda s: (0,) * len(shape))

    rows_in = pl.BlockSpec((tokens, piece), lambda s: (0, s))
    stat = pl.BlockSpec((1, step_heads, half), lambda s: (s, 0, 0))
    query, part, tops, totals, back, back_squares, prev_mask = call(
        functools.partial(main_kernel, scale_rows, devices),
        [sds((half, width), bf16), sds((width, half), f32), sds((steps, step_heads, half), f32),
         sds((steps, step_heads, half), f32), sds((half, width), f32), sds((1, half), f32), sds((half, half), f32)],
        [smem, smem, whole(1, tokens), whole(entries, wide), pl.BlockSpec((1, piece), lambda s: (0, s))] + [rows_in] * 3,
        (place, block_scales, ids, table, gain, q_raw, k_raw, v_raw),
        7 * half * tokens * width, 12 * tokens * width, grid=(steps,),
        out_specs=[
            pl.BlockSpec((half, piece), lambda s: (0, s)), pl.BlockSpec((piece, half), lambda s: (s, 0)), stat, stat,
            pl.BlockSpec((half, piece), lambda s: (0, s)), whole(1, half), whole(half, half),
        ],
        scratch=[
            pltpu.VMEM((half, half), f32), pltpu.VMEM((tokens, half), f32),
            pltpu.VMEM((SLOTS, land_pad, entries), bf16), pltpu.VMEM((land_pad, tokens), f32),
            pltpu.VMEM((land_pad, HD), f32),
        ],
    )
    front, squares = call(
        halo_kernel, [sds((half, width), f32), sds((1, tokens), f32)],
        [vmem] * 9, (query, part, tops, totals, gain, prev_mask, back_squares, prev_key, prev_value),
        2 * half * tokens * width, 8 * tokens * width,
    )
    parts = [squares] + [
        lax.ppermute(squares, "head", [(i, (i + d) % head_devices) for i in range(head_devices)])
        for d in range(1, head_devices)
    ]
    return call(
        functools.partial(scale_kernel, width * head_devices, head_devices), sds((tokens, width), bf16),
        [vmem] * (head_devices + 2), (*parts, front, back),
        3 * tokens * width, 6 * tokens * width, out_specs=pl.BlockSpec(memory_space=pl.ANY),
        scratch=[pltpu.VMEM((tokens, width), bf16), pltpu.SemaphoreType.DMA((tokens // LANES,))],
    )


def solution(mesh):
    in_specs = (
        P("seq", "head"), P("seq", "head"), P("seq", "head"),
        P(None, "seq", "head"), P("seq"), P("head"),
    )

    return jax.shard_map(on_device, mesh=mesh, in_specs=in_specs, out_specs=P("seq", "head"), check_vma=False)
```

time: 52 us -> 48.7 us (0.937)
  waiting for transfers between devices: 9.05 us -> 19.3 us
  local copies, waits for them, and re-layouts: 10.5 us -> 1.25 us
  Pallas kernels: 18 us -> 14 us
    all_to_all x1, waiting for transfers between devices: 6.19 us -> 16.4 us  [on_device(): table = lax.all_to_all(table, 'seq', 0, 0, tiled=True)]
    unnamed x28 -> x12, local copies, waits for them, and re-layouts: 10.5 us -> 1.25 us
    pallas_call x6 -> x5, Pallas kernels: 18 us -> 14 us  [call(): pl.pallas_call(kernel, out_shape=out_shape, in_specs=in_specs, out_specs=...]
  transfers between devices with their start and end apart: 6 -> 6, of which waited for: 3 -> 3; matrix products, arithmetic and copies ran while one was open for 0% -> 0% of each run, Pallas kernels for 23% -> 20%
where the time goes in v3:
time: 48.7 us; the launch traced here: 48.4 us
  waiting for transfers between devices  19.3 us (40%)
  Pallas kernels  14 us (29%)
  starting transfers between devices  13.8 us (28%)
  local copies, waits for them, and re-layouts  1.25 us (3%)
    all_to_all x1, waiting for transfers between devices, on_device(): table = lax.all_to_all(table, 'seq', 0, 0, tiled=True)  16.4 us
    pallas_call x5, Pallas kernels, call(): pl.pallas_call(kernel, out_shape=out_shape, in_specs=in_specs, out_specs=...  14 us
    ppermute x2, starting transfers between devices, shifted(): return lax.ppermute(block, 'seq', [(i - 1, i) for i in range(1, devices)])  6.83 us
    all_to_all x1, starting transfers between devices, on_device(): table = lax.all_to_all(table, 'seq', 0, 0, tiled=True)  5.14 us
    ppermute x3, waiting for transfers between devices, on_device(): lax.ppermute(squares, 'head', [(i, (i + d) % head_devices) for i in range...  2.86 us
    ppermute x3, starting transfers between devices, on_device(): lax.ppermute(squares, 'head', [(i, (i + d) % head_devices) for i in range...  1.8 us
    unnamed x12, local copies, waits for them, and re-layouts  1.25 us
  transfers between devices with their start and end apart: 6, of which 3 were waited for; matrix products, arithmetic and copies ran while one was open for 0% of the time, Pallas kernels for 20%

profile of v3, /device:TPU:16, one launch (start us, length us, event | category | flops | bytes accessed | tf_op | source)
XLA Modules:
  0.0 48.4 jit_solution(16179784240901518239)
XLA Ops:
  0.0 1.8 %shard_map.66 = bf16[256,1024]{1,0:T(8,128)(2,1)} custom-call(f32[3,4,8]{2,1,0:T(4,128)} %scales.5, bf16[512,1024]{1,0:T(8,128)(2,1)} %raw.1), custom_call_target="tpu_custom_call" | custom-call | flops 262144 | bytes 1048576 | tf_op jit(solution)/shard_map/pallas_call | solution.py:315
  1.8 3.4 %collective-permute-start = (bf16[256,1024]{1,0:T(8,128)(2,1)}, bf16[256,1024]{1,0:T(8,128)(2,1)S(1)}, u32[]{:S(2)}, u32[]{:S(2)}) collective-permute-start(bf16[256,1024]{1,0:T(8,128)(2,1)} %shard_map.66), channel_id=1, source_target_pairs={{0,4},{4,8},{8,12},{12,16},{16,20},{20,24},{24,28},{1,5},{5,9},{9,... | collective-permute-start | bytes 1572872 | tf_op jit(solution)/shard_map/ppermute | solution.py:327
  5.2 0.0 copy-start
  5.2 0.0 copy-start.1
  5.3 4.3 %shard_map.64 = (bf16[8,8,1664]{2,1,0:T(8,128)(2,1)}, bf16[1024,256]{1,0:T(8,128)(2,1)}) custom-call(f32[3,4,8]{2,1,0:T(4,128)} %scales.5, s32[1,512]{1,0:T(1,128)} %bitcast.7, bf16[512,1024]{1,0:T(8,128)(2,1)} %raw.1, bf16[512,1024]{1,0:T(8,128)(2,1)} %v_raw.3), custom_call_target="tpu_custom_call" | custom-call | flops 33554432 | bytes 2097152 | tf_op jit(solution)/shard_map/pallas_call | solution.py:315
  9.6 3.4 %collective-permute-start.1 = (bf16[1024,256]{1,0:T(8,128)(2,1)}, bf16[1024,256]{1,0:T(8,128)(2,1)S(1)}, u32[]{:S(2)}, u32[]{:S(2)}) collective-permute-start(bf16[1024,256]{1,0:T(8,128)(2,1)} %get-tuple-element.23), channel_id=1, source_target_pairs={{0,4},{4,8},{8,12},{12,16},{16,20},{20,24},{24,28},{1,5},{5,9},{9,... | collective-permute-start | bytes 1572872 | tf_op jit(solution)/shard_map/ppermute | solution.py:327
  13.1 0.0 copy-start.4
  13.1 5.1 %all-to-all-start = ((bf16[8,8,1664]{2,1,0:T(8,128)(2,1)}), bf16[8,8,1664]{2,1,0:T(8,128)(2,1)S(1)}, u32[]{:S(2)}, u32[]{:S(2)}) async-start(bf16[8,8,1664]{2,1,0:T(8,128)(2,1)} %get-tuple-element.16), calls=%async_computation | async-start | bytes 425984 | tf_op jit(solution)/shard_map/all_to_all | solution.py:348
  18.2 0.0 copy-start.2
  18.2 0.0 copy-start.3
  18.2 16.4 %all-to-all-done = bf16[8,8,1664]{2,1,0:T(8,128)(2,1)S(1)} async-done(((bf16[8,8,1664]{2,1,0:T(8,128)(2,1)}), bf16[8,8,1664]{2,1,0:T(8,128)(2,1)S(1)}, u32[]{:S(2)}, u32[]{:S(2)}) %all-to-all-start) | async-done | bytes 213024 | tf_op jit(solution)/shard_map/all_to_all | solution.py:348
  34.6 0.0 copy-done
  34.6 0.0 copy-done.1
  34.6 0.0 copy-done.4
  34.6 0.0 copy-done.2
  34.6 0.0 copy-done.3
  34.6 0.0 copy-start.5
  34.7 1.2 %copy-done.5 = bf16[512,1024]{1,0:T(8,128)(2,1)S(1)} copy-done((bf16[512,1024]{1,0:T(8,128)(2,1)S(1)}, bf16[512,1024]{1,0:T(8,128)(2,1)}, u32[]{:S(2)}) %copy-start.5) | copy-done | bytes 1048600
  35.9 5.4 %shard_map.65 = (bf16[256,1024]{1,0:T(8,128)(2,1)S(1)}, f32[1024,256]{1,0:T(8,128)S(1)}, f32[2,4,256]{2,1,0:T(4,128)S(1)}, f32[2,4,256]{2,1,0:T(4,128)S(1)}, f32...) custom-call(s32[1]{0:T(128)} %bitcast.place, f32[3,4,8]{2,1,0:T(4,128)S(1)} %copy-done.2, ...), custom_call_target="tpu_custom_call" | custom-call | flops 939524096 | bytes 6291456 | tf_op jit(solution)/shard_map/pallas_call | solution.py:315
  41.3 0.0 collective-permute-done.prev_key
  41.3 0.0 collective-permute-done.1.prev_value
  41.3 1.3 %shard_map.67 = (f32[256,1024]{1,0:T(8,128)S(1)}, f32[1,512]{1,0:T(1,128)S(1)}) custom-call(bf16[256,1024]{1,0:T(8,128)(2,1)S(1)} %get-tuple-element.17.query, f32[1024,256]{1,0:T(8,128)S(1)} %get-tuple-element.18.local, f32[2,4,256]{2,1,0:T(4,128)S(1)} %get-tuple-element.19.tops, f32[2,4,256]{2,1,0:T(4,128)S(1)} %get-tuple-element.20.totals, ...), custom_call_target="tpu_custom_call" | custom-call | flops 268435456 | bytes 4194304 | tf_op jit(solution)/shard_map/pallas_call | solution.py:315
  42.6 0.1 collective-permute-start.4
  42.6 1.6 %collective-permute-start.3 = (f32[1,512]{1,0:T(1,128)S(1)}, f32[1,512]{1,0:T(1,128)S(1)}, u32[]{:S(2)}, u32[]{:S(2)}) collective-permute-start(f32[1,512]{1,0:T(1,128)S(1)} %get-tuple-element.24.refs_0_), channel_id=1, source_target_pairs={{0,2},{1,3},{2,0},{3,1},{4,6},{5,7},{6,4},{7,5},{8,10},{9,11},{10,... | collective-permute-start | bytes 6152 | tf_op jit(solution)/shard_map/ppermute | solution.py:385
  44.2 0.2 collective-permute-start.2
  44.4 0.0 collective-permute-done.4.refs_3_
  44.4 1.9 %collective-permute-done.3.refs_2_ = f32[1,512]{1,0:T(1,128)S(1)} collective-permute-done((f32[1,512]{1,0:T(1,128)S(1)}, f32[1,512]{1,0:T(1,128)S(1)}, u32[]{:S(2)}, u32[]{:S(2)}) %collective-permute-start.3) | collective-permute-done | bytes 2080 | tf_op jit(solution)/shard_map/ppermute | solution.py:385
  46.3 1.0 %collective-permute-done.2.refs_1_ = f32[1,512]{1,0:T(1,128)S(1)} collective-permute-done((f32[1,512]{1,0:T(1,128)S(1)}, f32[1,512]{1,0:T(1,128)S(1)}, u32[]{:S(2)}, u32[]{:S(2)}) %collective-permute-start.2) | collective-permute-done | bytes 2080 | tf_op jit(solution)/shard_map/ppermute | solution.py:385
  47.2 1.1 %shard_map.68 = bf16[512,1024]{1,0:T(8,128)(2,1)} custom-call(f32[1,512]{1,0:T(1,128)S(1)} %get-tuple-element.24.refs_0_, f32[1,512]{1,0:T(1,128)S(1)} %collective-permute-done.2.refs_1_, f32[1,512]{1,0:T(1,128)S(1)} %collective-permute-done.3.refs_2_, f32[1,512]{1,0:T(1,128)S(1)} %collective-permute-done.4.refs_3_, ...), custom_call_target="tpu_custom_call" | custom-call | flops 1572864 | bytes 3145728 | tf_op jit(solution)/shard_map/pallas_call | solution.py:315
Async XLA Ops:
  1.8 39.4 %collective-permute-start = (bf16[256,1024]{1,0:T(8,128)(2,1)}, bf16[256,1024]{1,0:T(8,128)(2,1)S(1)}, u32[]{:S(2)}, u32[]{:S(2)}) collective-permute-start(bf16[256,1024]{1,0:T(8,128)(2,1)} %shard_map.66), channel_id=1, source_target_pairs={{0,4},{4,8},{8,12},{12,16},{16,20},{20,24},{24,28},{1,5},{5,9},{9,... | collective-permute-start | bytes 1572872 | tf_op jit(solution)/shard_map/ppermute | solution.py:327
  5.2 29.4 %copy-start = (bf16[512,1024]{1,0:T(8,128)(2,1)S(1)}, bf16[512,1024]{1,0:T(8,128)(2,1)}, u32[]{:S(2)}) copy-start(bf16[512,1024]{1,0:T(8,128)(2,1)} %raw.1) | copy-start | bytes 3145732
  5.2 29.4 %copy-start.1 = (bf16[512,1024]{1,0:T(8,128)(2,1)S(1)}, bf16[512,1024]{1,0:T(8,128)(2,1)}, u32[]{:S(2)}) copy-start(bf16[512,1024]{1,0:T(8,128)(2,1)} %v_raw.3) | copy-start | bytes 3145732
  9.6 31.7 %collective-permute-start.1 = (bf16[1024,256]{1,0:T(8,128)(2,1)}, bf16[1024,256]{1,0:T(8,128)(2,1)S(1)}, u32[]{:S(2)}, u32[]{:S(2)}) collective-permute-start(bf16[1024,256]{1,0:T(8,128)(2,1)} %get-tuple-element.23), channel_id=1, source_target_pairs={{0,4},{4,8},{8,12},{12,16},{16,20},{20,24},{24,28},{1,5},{5,9},{9,... | collective-permute-start | bytes 1572872 | tf_op jit(solution)/shard_map/ppermute | solution.py:327
  13.1 21.6 %copy-start.4 = (s32[512]{0:T(512)S(1)}, s32[512]{0:T(512)}, u32[]{:S(2)}) copy-start(s32[512]{0:T(512)} %param.10) | copy-start | bytes 6148
  13.1 21.6 %all-to-all-start = ((bf16[8,8,1664]{2,1,0:T(8,128)(2,1)}), bf16[8,8,1664]{2,1,0:T(8,128)(2,1)S(1)}, u32[]{:S(2)}, u32[]{:S(2)}) async-start(bf16[8,8,1664]{2,1,0:T(8,128)(2,1)} %get-tuple-element.16), calls=%async_computation | async-start | bytes 425984 | tf_op jit(solution)/shard_map/all_to_all | solution.py:348
  18.2 16.4 %copy-start.2 = (f32[3,4,8]{2,1,0:T(4,128)S(1)}, f32[3,4,8]{2,1,0:T(4,128)}, u32[]{:S(2)}) copy-start(f32[3,4,8]{2,1,0:T(4,128)} %scales.5) | copy-start | bytes 1156
  18.2 16.4 %copy-start.3 = (f32[1024]{0:T(1024)S(1)}, f32[1024]{0:T(1024)}, u32[]{:S(2)}) copy-start(f32[1024]{0:T(1024)} %param.11) | copy-start | bytes 12292
  34.6 1.2 %copy-start.5 = (bf16[512,1024]{1,0:T(8,128)(2,1)S(1)}, bf16[512,1024]{1,0:T(8,128)(2,1)}, u32[]{:S(2)}) copy-start(bf16[512,1024]{1,0:T(8,128)(2,1)} %q_raw.1) | copy-start | bytes 3145732
  42.6 1.8 %collective-permute-start.4 = (f32[1,512]{1,0:T(1,128)S(1)}, f32[1,512]{1,0:T(1,128)S(1)}, u32[]{:S(2)}, u32[]{:S(2)}) collective-permute-start(f32[1,512]{1,0:T(1,128)S(1)} %get-tuple-element.24.refs_0_), channel_id=1, source_target_pairs={{0,3},{1,0},{2,1},{3,2},{4,7},{5,4},{6,5},{7,6},{8,11},{9,8},{10,9... | collective-permute-start | bytes 6152 | tf_op jit(solution)/shard_map/ppermute | solution.py:385
  42.6 3.7 %collective-permute-start.3 = (f32[1,512]{1,0:T(1,128)S(1)}, f32[1,512]{1,0:T(1,128)S(1)}, u32[]{:S(2)}, u32[]{:S(2)}) collective-permute-start(f32[1,512]{1,0:T(1,128)S(1)} %get-tuple-element.24.refs_0_), channel_id=1, source_target_pairs={{0,2},{1,3},{2,0},{3,1},{4,6},{5,7},{6,4},{7,5},{8,10},{9,11},{10,... | collective-permute-start | bytes 6152 | tf_op jit(solution)/shard_map/ppermute | solution.py:385
  44.2 3.0 %collective-permute-start.2 = (f32[1,512]{1,0:T(1,128)S(1)}, f32[1,512]{1,0:T(1,128)S(1)}, u32[]{:S(2)}, u32[]{:S(2)}) collective-permute-start(f32[1,512]{1,0:T(1,128)S(1)} %get-tuple-element.24.refs_0_), channel_id=1, source_target_pairs={{0,1},{1,2},{2,3},{3,0},{4,5},{5,6},{6,7},{7,4},{8,9},{9,10},{10,1... | collective-permute-start | bytes 6152 | tf_op jit(solution)/shard_map/ppermute | solution.py:385

commit v4 on v3

v4 whole, which is shorter than its diff:
```python
import functools
import math

import jax
import jax.numpy as jnp
from jax import lax
from jax.experimental import pallas as pl
from jax.experimental.pallas import tpu as pltpu
from jax.sharding import PartitionSpec as P


HD = 128
CAP = 4
LANES = 128
SLOTS = CAP + 2
EARLY = CAP + 1
epsilon = 1e-06
factor = math.log2(math.e) / math.sqrt(HD)
f32 = jnp.float32
bf16 = jnp.bfloat16
i32 = jnp.int32
vmem_limit = 20 * 2**20
whole_vmem = 60 * 1024 * 2**10
pipeline_depth = 2


def nt_dot(a, b):
    return lax.dot_general(a, b, (((1,), (1,)), ((), ())), preferred_element_type=f32)


def nn_dot(a, b):
    return jnp.dot(a, b, preferred_element_type=f32)


def iota(shape, axis):
    return lax.broadcasted_iota(i32, shape, axis)


def columns_of(row):
    pieces = []
    for start in range(0, row.shape[1], LANES):
        pieces.append(jnp.broadcast_to(row[:, start : start + LANES], (LANES, LANES)).T)
    return jnp.concatenate(pieces, axis=0)


def dequantized(raw, scales, which, head, cols, scale_rows, first=0):
    parts = []
    for piece in range(raw.shape[0] // scale_rows):
        rows = slice(piece * scale_rows, (piece + 1) * scale_rows)
        parts.append((raw[rows, cols].astype(f32) * scales[which, first + piece, head]).astype(bf16))
    return jnp.concatenate(parts, axis=0)


def table_kernel(scale_rows, pieces, scales, ids, k_raw, v_raw, table, tail_value, keys, values, sums, packed, tails, sems, out_sems):
    tokens = ids.shape[1]
    half = tokens // 2
    heads = sums.shape[0]
    piece = heads * HD // pieces
    copies = []
    for number in range(pieces):
        cols = slice(number * piece, (number + 1) * piece)
        for which, (source, target) in enumerate(((k_raw, keys), (v_raw, values))):
            copy = pltpu.make_async_copy(source.at[:, cols], target.at[:, cols], sems.at[number, which])
            copy.start()
            copies.append(copy)
    row = ids[...]
    local = row - row[:, 0:1]
    last = local[:, tokens - 1 :]
    slot = iota((2 * 8, tokens), 0)
    token = iota((2 * 8, tokens), 1)
    picked = (slot <= CAP) & (local == slot)
    picked = picked | ((slot == EARLY) & (local == last) & (token < half))
    picked = picked.astype(f32)
    pick = picked.astype(bf16)
    count = jnp.sum(picked, axis=1, keepdims=True).astype(i32)
    lane = iota((heads, LANES), 1)
    head_row = iota((heads, LANES), 0)
    meta = jnp.zeros((heads, LANES), i32)
    for index in range(SLOTS):
        seg = row[:, 0:1] + (last if index == EARLY else index)
        number = count[index : index + 1]
        for place, value in enumerate((seg & 127, seg >> 7, number & 127, number >> 7)):
            meta = jnp.where(lane == 4 * index + place, value, meta)
    tail_blocks = half // scale_rows
    scale = jnp.zeros((heads, LANES), f32)
    part = jnp.zeros((heads, LANES), i32)
    for block in range(tail_blocks):
        for head in range(heads):
            value = scales[1, scales.shape[1] - tail_blocks + block, head]
            here = (lane >= 4 * SLOTS + 3 * block) & (lane < 4 * SLOTS + 3 * block + 3)
            scale = jnp.where(here & (head_row == head), value, scale)
        for place in range(3):
            part = jnp.where(lane == 4 * SLOTS + 3 * block + place, place, part)
    high = scale.astype(bf16).astype(f32)
    middle = (scale - high).astype(bf16).astype(f32)
    low = scale - high - middle
    scale = jnp.where(part == 0, high, jnp.where(part == 1, middle, low))
    sums[:, 2 * SLOTS * HD :] = jnp.where(lane < 4 * SLOTS, meta.astype(f32), scale)
    writes = []
    for number in range(pieces):
        found = []
        for which, source in enumerate((keys, values)):
            copies[2 * number + which].wait()
            for head in range(number * piece // HD, (number + 1) * piece // HD):
                cols = slice(head * HD, (head + 1) * HD)
                value = dequantized(source, scales, 1 + which, head, cols, scale_rows)
                if which:
                    tails[:, cols] = value[half:]
                found.append((head, which * SLOTS, nn_dot(pick, value)))
        for head, start, total in found:
            for index in range(SLOTS):
                where = slice((start + index) * HD, (start + index + 1) * HD)
                sums[head : head + 1, where] = total[index : index + 1]
        cols = slice(number * piece, (number + 1) * piece)
        copy = pltpu.make_async_copy(tails.at[:, cols], tail_value.at[:, cols], out_sems.at[number])
        copy.start()
        writes.append(copy)
    packed[...] = jnp.broadcast_to(sums[...].astype(bf16)[None], packed.shape)
    copy = pltpu.make_async_copy(packed, table, out_sems.at[pieces])
    copy.start()
    writes.append(copy)
    for copy in writes:
        copy.wait()


def with_ones(value):
    return jnp.concatenate([value, jnp.ones((16, value.shape[1]), bf16)], axis=0)


def main_kernel(
    scale_rows, device_count,
    place, scales, ids, table, gain, q_raw, k_raw, v_raw, prev_raw,
    open_out, prev_weights, back_out, back_squares,
    near, far, picks, bias, inverse, prev_mask, prev_scales,
):
    step = pl.program_id(0)
    tokens = ids.shape[1]
    half = tokens // 2
    heads = q_raw.shape[1] // HD
    lands = CAP * device_count
    land_pad, entries = picks.shape[1:]
    all_heads = entries // device_count
    entry = iota((1, entries), 1)
    entry_device = entry // all_heads
    entry_head = entry - entry_device * all_heads

    @pl.when(step == 0)
    def _():
        me = place[0]
        row = ids[...]
        first = row[:, 0:1]
        column = columns_of(row)
        for mask, start, width in ((near, 0, half), (far, half, tokens)):
            for left in range(0, half, LANES):
                query = iota((width, LANES), 1) + (start + left)
                live = column[:width] == row[:, start + left : start + left + LANES]
                live = live & (iota((width, LANES), 0) <= query)
                mask[:, left : left + LANES] = jnp.where(live, 0.0, -jnp.inf)
        info = table[:, 2 * SLOTS * HD :].astype(f32).T
        land = iota((land_pad, entries), 0)
        count = jnp.zeros((land_pad, 1), f32)
        for index in range(SLOTS):
            seg = info[4 * index : 4 * index + 1] + 128.0 * info[4 * index + 1 : 4 * index + 2]
            number = info[4 * index + 2 : 4 * index + 3] + 128.0 * info[4 * index + 3 : 4 * index + 4]
            if index == EARLY:
                picked = (land == lands) & (entry_device == me - 1)
            else:
                is_open = seg == first.astype(f32)
                picked = (land < lands) & (land.astype(f32) == seg)
                picked = picked | ((land == lands) & is_open & (entry_device < me - 1))
                picked = picked | ((land == lands + 1) & is_open & (entry_device < me))
                picked = picked | ((land == lands + 2) & is_open & (entry_device == me - 1))
            picked = picked.astype(f32)
            picks[index] = picked.astype(bf16)
            count = count + jnp.sum(
                picked * jnp.where(entry_head == 0, number, 0.0), axis=1, keepdims=True
            )
        inverse[...] = jnp.broadcast_to(1.0 / jnp.maximum(count, 1.0), inverse.shape)
        amount = jnp.broadcast_to(count, (land_pad, LANES))
        log_count = jnp.log2(jnp.maximum(amount, 1.0))
        for left in range(0, tokens, LANES):
            seg = row[:, left : left + LANES]
            index = iota((land_pad, LANES), 0)
            run = lands if left < half else lands + 1
            live = ((index < lands) & (index < seg)) | ((index == run) & (seg == first) & (amount > 0.5))
            bias[:, left : left + LANES] = jnp.where(live, log_count, -jnp.inf)
        tail = count[lands + 2 : lands + 3].astype(i32)
        for left in range(0, half, LANES):
            live = (iota((half, LANES), 0) >= half - tail) & (row[:, left : left + LANES] == first)
            prev_mask[:, left : left + LANES] = jnp.where(live, 0.0, -jnp.inf)
        back_squares[...] = jnp.zeros(back_squares.shape, f32)
        info = table[:, 2 * SLOTS * HD :].astype(f32).reshape(device_count, all_heads, LANES)
        of_device = lax.broadcasted_iota(i32, info.shape, 0)
        info = jnp.sum(jnp.where(of_device == me - 1, info, 0.0), axis=0)
        for group in range(all_heads // heads):
            prev_scales[group] = info[group * heads : (group + 1) * heads]

    def prepared(head):
        cols = slice(head * HD, (head + 1) * HD)
        index = step * heads + head
        query = dequantized(q_raw, scales, 0, index, cols, scale_rows)
        key = dequantized(k_raw, scales, 1, index, cols, scale_rows)
        value = dequantized(v_raw, scales, 2, index, cols, scale_rows).T
        pieces = []
        for block in range(half // scale_rows):
            at = 4 * SLOTS + 3 * block
            parts = prev_scales[step, head : head + 1, at : at + 3]
            scale = parts[:, 0:1] + parts[:, 1:2] + parts[:, 2:3]
            raw = prev_raw[block * scale_rows : (block + 1) * scale_rows, cols]
            pieces.append((raw.astype(f32) * scale).astype(bf16))
        prev_key = jnp.concatenate(pieces, axis=0)
        mine = (entry_head == index).astype(f32).astype(bf16)
        land_key = jnp.zeros((land_pad, HD), f32)
        land_value = jnp.zeros((land_pad, HD), f32)
        for slot in range(SLOTS):
            pick = picks[slot] * mine
            land_key = land_key + nn_dot(pick, table[:, slot * HD : (slot + 1) * HD])
            land_value = land_value + nn_dot(pick, table[:, (SLOTS + slot) * HD : (SLOTS + slot + 1) * HD])
        land_key = (land_key * inverse[...]).astype(bf16)
        land_value = (land_value * inverse[...]).astype(bf16)
        land_value = jnp.concatenate([land_value, jnp.ones((land_pad, 16), bf16)], axis=1)
        return query, key, value, land_key, land_value, prev_key

    ready = {}

    def scores_of(task):
        head, part = task
        if head not in ready:
            ready[head] = prepared(head)
        query, key, _, land_key, _, prev_key = ready[head]
        rows = slice(part * half, (part + 1) * half)
        mask = far if part else near
        score = nt_dot(key[: (part + 1) * half], query[rows]) * factor + mask[...]
        land_score = nt_dot(land_key, query[rows]) * factor + bias[:, rows]
        if part:
            return score, land_score, None
        return score, land_score, nt_dot(prev_key, query[rows]) * factor + prev_mask[...]

    tasks = [(head, part) for head in range(heads) for part in range(2)]
    scores = [scores_of(task) for task in tasks[:pipeline_depth]]
    for number, (head, part) in enumerate(tasks):
        if number + pipeline_depth < len(tasks):
            scores.append(scores_of(tasks[number + pipeline_depth]))
        cols = slice(head * HD, (head + 1) * HD)
        score, land_score, prev_score = scores[number]
        _, _, value, _, land_value, _ = ready[head]
        top = jnp.maximum(
            jnp.max(score, axis=0, keepdims=True), jnp.max(land_score, axis=0, keepdims=True)
        )
        if part == 0:
            top = jnp.maximum(top, jnp.max(prev_score, axis=0, keepdims=True))
        weight = jnp.exp2(score - top).astype(bf16)
        land_weight = jnp.exp2(land_score - top).astype(bf16)
        found = nn_dot(with_ones(value[:, : (part + 1) * half]), weight)
        found = found + lax.dot_general(
            land_value, land_weight, (((0,), (0,)), ((), ())), preferred_element_type=f32
        )
        total = found[HD : HD + 1]
        if part == 0:
            prev_weight = jnp.exp2(prev_score - top)
            share = 1.0 / (total + jnp.sum(prev_weight, axis=0, keepdims=True))
            open_out[:, cols] = (found[:HD] * share).T
            prev_weights[head] = (prev_weight * share).astype(bf16).T
        else:
            done = found[:HD] * (1.0 / total)
            back_squares[...] += jnp.sum(done * done, axis=0, keepdims=True)
            back_out[:, cols] = done.T * gain[:, cols]


def halo_kernel(opened, prev_weights, gain, back_squares, prev_value, out, squares):
    heads, half = prev_weights.shape[:2]
    found = []
    power = jnp.zeros((half, HD), f32)
    for head in range(heads + pipeline_depth):
        if head < heads:
            found.append(nn_dot(prev_weights[head], prev_value[:, head * HD : (head + 1) * HD]))
        done = head - pipeline_depth
        if done >= 0:
            cols = slice(done * HD, (done + 1) * HD)
            value = opened[:, cols] + found[done]
            power = power + value * value
            out[:, cols] = value * gain[:, cols]
    for start in range(0, half, LANES):
        total = jnp.sum(power[start : start + LANES].T, axis=0, keepdims=True)
        squares[:, start : start + LANES] = total
    squares[:, half:] = back_squares[...]


def scale_kernel(width, count, *refs):
    parts, (front, back, out, ready, sems) = refs[:count], refs[count:]
    total = parts[0][...]
    for ref in parts[1:]:
        total = total + ref[...]
    norm = columns_of(lax.rsqrt(total / width + epsilon))
    half = front.shape[0]
    copies = []
    for part, source in enumerate((front, back)):
        for start in range(0, half, LANES):
            rows = slice(part * half + start, part * half + start + LANES)
            for left in range(0, front.shape[1], LANES):
                cols = slice(left, left + LANES)
                ready[rows, cols] = (source[start : start + LANES, cols] * norm[rows]).astype(bf16)
            copy = pltpu.make_async_copy(ready.at[rows], out.at[rows], sems.at[len(copies)])
            copy.start()
            copies.append(copy)
    for copy in copies:
        copy.wait()


def on_device(q_raw, k_raw, v_raw, block_scales, segment_ids, norm_gain):
    tokens, width = q_raw.shape
    half = tokens // 2
    heads = width // HD
    scale_rows = tokens // block_scales.shape[1]
    devices = lax.axis_size("seq")
    head_devices = lax.axis_size("head")
    entries = devices * heads
    land_pad = -(-(CAP * devices + 3) // 16) * 16
    smem = pl.BlockSpec(memory_space=pltpu.SMEM)
    vmem = pl.BlockSpec(memory_space=pltpu.VMEM)
    hbm = pl.BlockSpec(memory_space=pltpu.HBM)
    sds = jax.ShapeDtypeStruct
    ids = segment_ids.reshape(1, tokens)
    wide = 2 * SLOTS * HD + LANES

    def call(kernel, out_shape, in_specs, args, flops, moved, scratch=(), out_specs=None, limit=vmem_limit, **more):
        return pl.pallas_call(
            kernel,
            out_shape=out_shape,
            in_specs=in_specs,
            out_specs=jax.tree.map(lambda _: vmem, out_shape) if out_specs is None else out_specs,
            scratch_shapes=list(scratch),
            compiler_params=pltpu.CompilerParams(vmem_limit_bytes=limit),
            cost_estimate=pl.CostEstimate(flops=flops, bytes_accessed=moved, transcendentals=0),
            **more,
        )(*args)

    def shifted(block):
        return lax.ppermute(block, "seq", [(i - 1, i) for i in range(1, devices)])

    prev_key = shifted(k_raw[half:])
    table_pieces = 4
    table, tail_value = call(
        functools.partial(table_kernel, scale_rows, table_pieces),
        [sds((devices, heads, wide), bf16), sds((half, width), bf16)],
        [smem, vmem, hbm, hbm], (block_scales, ids, k_raw, v_raw),
        64 * tokens * width, 4 * tokens * width, out_specs=[hbm, hbm], limit=whole_vmem,
        scratch=[
            pltpu.VMEM((tokens, width), bf16), pltpu.VMEM((tokens, width), bf16),
            pltpu.VMEM((heads, wide), f32), pltpu.VMEM((devices, heads, wide), bf16), pltpu.VMEM((half, width), bf16),
            pltpu.SemaphoreType.DMA((table_pieces, 2)), pltpu.SemaphoreType.DMA((table_pieces + 1,)),
        ],
    )
    table = lax.all_to_all(table, "seq", 0, 0, tiled=True)
    table = table.reshape(entries, wide)
    prev_value = shifted(tail_value)
    place = lax.axis_index("seq").astype(i32).reshape(1)
    gain = norm_gain.reshape(1, width)
    step_heads = 4
    steps = heads // step_heads
    piece = step_heads * HD

    def whole(*shape):
        return pl.BlockSpec(shape, lambda s: (0,) * len(shape))

    rows_in = pl.BlockSpec((tokens, piece), lambda s: (0, s))
    half_rows = pl.BlockSpec((half, piece), lambda s: (0, s))
    opened, prev_weights, back, back_squares = call(
        functools.partial(main_kernel, scale_rows, devices),
        [sds((half, width), f32), sds((heads, half, half), bf16), sds((half, width), f32), sds((1, half), f32)],
        [smem, smem, whole(1, tokens), whole(entries, wide), pl.BlockSpec((1, piece), lambda s: (0, s))] + [rows_in] * 3 + [half_rows],
        (place, block_scales, ids, table, gain, *(pltpu.with_memory_space_constraint(x, pltpu.HBM) for x in (q_raw, k_raw, v_raw)), prev_key),
        8 * half * tokens * width, 12 * tokens * width, grid=(steps,),
        out_specs=[half_rows, pl.BlockSpec((step_heads, half, half), lambda s: (s, 0, 0)), half_rows, whole(1, half)],
        scratch=[
            pltpu.VMEM((half, half), f32), pltpu.VMEM((tokens, half), f32),
            pltpu.VMEM((SLOTS, land_pad, entries), bf16), pltpu.VMEM((land_pad, tokens), f32),
            pltpu.VMEM((land_pad, HD), f32), pltpu.VMEM((half, half), f32), pltpu.VMEM((steps, step_heads, LANES), f32),
        ],
    )
    front, squares = call(
        halo_kernel, [sds((half, width), f32), sds((1, tokens), f32)],
        [vmem] * 5, (opened, prev_weights, gain, back_squares, prev_value),
        half * half * width * 2, 8 * tokens * width,
    )
    pairs = head_devices & (head_devices - 1) == 0
    parts = [squares] + [
        lax.ppermute(squares, "head", [(i, i ^ d if pairs else (i + d) % head_devices) for i in range(head_devices)])
        for d in range(1, head_devices)
    ]
    return call(
        functools.partial(scale_kernel, width * head_devices, head_devices), sds((tokens, width), bf16),
        [vmem] * (head_devices + 2), (*parts, front, back),
        3 * tokens * width, 6 * tokens * width, out_specs=pl.BlockSpec(memory_space=pl.ANY),
        scratch=[pltpu.VMEM((tokens, width), bf16), pltpu.SemaphoreType.DMA((tokens // LANES,))],
    )


def solution(mesh):
    in_specs = (
        P("seq", "head"), P("seq", "head"), P("seq", "head"),
        P(None, "seq", "head"), P("seq"), P("head"),
    )

    return jax.shard_map(on_device, mesh=mesh, in_specs=in_specs, out_specs=P("seq", "head"), check_vma=False)
```

time: 48.7 us -> 46.7 us (0.959)
  the two profiles are of different devices: /device:TPU:16 before, /device:TPU:17 now
where the time goes in v4:
time: 46.7 us; the launch traced here: 46.4 us
  waiting for transfers between devices  16.9 us (36%)
  starting transfers between devices  16 us (34%)
  Pallas kernels  12.3 us (26%)
  local copies, waits for them, and re-layouts  1.09 us (2%)
    all_to_all x1, waiting for transfers between devices, on_device(): table = lax.all_to_all(table, 'seq', 0, 0, tiled=True)  15 us
    pallas_call x4, Pallas kernels, call(): pl.pallas_call(kernel, out_shape=out_shape, in_specs=in_specs, out_specs=...  12.3 us
    ppermute x2, starting transfers between devices, shifted(): return lax.ppermute(block, 'seq', [(i - 1, i) for i in range(1, devices)])  6.3 us
    ppermute x3, starting transfers between devices, on_device(): lax.ppermute(squares, 'head', [(i, i ^ d if pairs else (i + d) % head_dev...  5.08 us
    all_to_all x1, starting transfers between devices, on_device(): table = lax.all_to_all(table, 'seq', 0, 0, tiled=True)  4.58 us
    ppermute x3, waiting for transfers between devices, on_device(): lax.ppermute(squares, 'head', [(i, i ^ d if pairs else (i + d) % head_dev...  1.96 us
    slice x1, local copies, waits for them, and re-layouts, on_device(): prev_key = shifted(k_raw[half:])  1.08 us
  transfers between devices with their start and end apart: 6, of which 3 were waited for; matrix products, arithmetic and copies ran while one was open for 0% of the time, Pallas kernels for 23%

profile of v4, /device:TPU:17, one launch (start us, length us, event | category | flops | bytes accessed | tf_op | source)
XLA Modules:
  0.0 46.4 jit_solution(16036837369109462823)
XLA Ops:
  0.0 1.1 %slice.3 = bf16[256,1024]{1,0:T(8,128)(2,1)S(1)} slice(bf16[512,1024]{1,0:T(8,128)(2,1)} %k_raw.3), slice={[256:512], [0:1024]} | slice | bytes 1048576 | tf_op jit(solution)/shard_map/slice | solution.py:341
  1.1 3.1 %collective-permute-start = (bf16[256,1024]{1,0:T(8,128)(2,1)S(1)}, bf16[256,1024]{1,0:T(8,128)(2,1)S(1)}, u32[]{:S(2)}, u32[]{:S(2)}) collective-permute-start(bf16[256,1024]{1,0:T(8,128)(2,1)S(1)} %slice.3), channel_id=1, source_target_pairs={{0,4},{4,8},{8,12},{12,16},{16,20},{20,24},{24,28},{1,5},{5,9},{9,... | collective-permute-start | bytes 1572872 | tf_op jit(solution)/shard_map/ppermute | solution.py:339
  4.2 4.0 %shard_map.64 = (bf16[8,8,1664]{2,1,0:T(8,128)(2,1)}, bf16[256,1024]{1,0:T(8,128)(2,1)}) custom-call(f32[3,4,8]{2,1,0:T(4,128)} %scales.3, s32[1,512]{1,0:T(1,128)} %bitcast.7, bf16[512,1024]{1,0:T(8,128)(2,1)} %k_raw.3, bf16[512,1024]{1,0:T(8,128)(2,1)} %v_raw.3), custom_call_target="tpu_custom_call" | custom-call | flops 33554432 | bytes 2097152 | tf_op jit(solution)/shard_map/pallas_call | solution.py:327
  8.2 3.2 %collective-permute-start.1 = (bf16[256,1024]{1,0:T(8,128)(2,1)}, bf16[256,1024]{1,0:T(8,128)(2,1)S(1)}, u32[]{:S(2)}, u32[]{:S(2)}) collective-permute-start(bf16[256,1024]{1,0:T(8,128)(2,1)} %get-tuple-element.17), channel_id=1, source_target_pairs={{0,4},{4,8},{8,12},{12,16},{16,20},{20,24},{24,28},{1,5},{5,9},{9,... | collective-permute-start | bytes 1572872 | tf_op jit(solution)/shard_map/ppermute | solution.py:339
  11.4 0.0 copy-start.2
  11.4 4.6 %all-to-all-start = ((bf16[8,8,1664]{2,1,0:T(8,128)(2,1)}), bf16[8,8,1664]{2,1,0:T(8,128)(2,1)S(1)}, u32[]{:S(2)}, u32[]{:S(2)}) async-start(bf16[8,8,1664]{2,1,0:T(8,128)(2,1)} %get-tuple-element.13), calls=%async_computation | async-start | bytes 425984 | tf_op jit(solution)/shard_map/all_to_all | solution.py:354
  16.0 0.0 copy-start
  16.0 0.0 copy-start.1
  16.0 15.0 %all-to-all-done = bf16[8,8,1664]{2,1,0:T(8,128)(2,1)S(1)} async-done(((bf16[8,8,1664]{2,1,0:T(8,128)(2,1)}), bf16[8,8,1664]{2,1,0:T(8,128)(2,1)S(1)}, u32[]{:S(2)}, u32[]{:S(2)}) %all-to-all-start) | async-done | bytes 213024 | tf_op jit(solution)/shard_map/all_to_all | solution.py:354
  30.9 0.0 collective-permute-done.prev_raw
  30.9 0.0 copy-done.2
  30.9 0.0 copy-done
  30.9 0.0 copy-done.1
  30.9 6.7 %shard_map.65 = (f32[256,1024]{1,0:T(8,128)S(1)}, bf16[8,256,256]{2,1,0:T(8,128)(2,1)S(1)}, f32[256,1024]{1,0:T(8,128)S(1)}, f32[1,256]{1,0:T(1,128)S(1)}) custom-call(s32[1]{0:T(128)} %bitcast.place, f32[3,4,8]{2,1,0:T(4,128)S(1)} %copy-done, s32[1,512]{1,0:T(1,128)S(1)} %bitcast.8, bf16[64,1664]{1,0:T(8,128)(2,1)S(1)} %bitcast.4, f32[1,1024]{1,0:T(1,128)S(1)} %bitcast.5, ...), custom_call_target="tpu_custom_call" | custom-call | flops 1073741824 | bytes 6291456 | tf_op jit(solution)/shard_map/pallas_call | solution.py:327
  37.7 0.0 collective-permute-done.1.prev_value
  37.7 0.5 %shard_map.66 = (f32[256,1024]{1,0:T(8,128)S(1)}, f32[1,512]{1,0:T(1,128)S(1)}) custom-call(f32[256,1024]{1,0:T(8,128)S(1)} %get-tuple-element.14.opened, bf16[8,256,256]{2,1,0:T(8,128)(2,1)S(1)} %get-tuple-element.15.prev_weights, f32[1,1024]{1,0:T(1,128)S(1)} %bitcast.6, f32[1,256]{1,0:T(1,128)S(1)} %get-tuple-element.16.back_squares, ...), custom_call_target="tpu_custom_call" | custom-call | flops 134217728 | bytes 4194304 | tf_op jit(solution)/shard_map/pallas_call | solution.py:327
  38.2 4.6 %collective-permute-start.4 = (f32[1,512]{1,0:T(1,128)S(1)}, f32[1,512]{1,0:T(1,128)S(1)}, u32[]{:S(2)}, u32[]{:S(2)}) collective-permute-start(f32[1,512]{1,0:T(1,128)S(1)} %get-tuple-element.18.refs_0_), channel_id=1, source_target_pairs={{0,3},{1,2},{2,1},{3,0},{4,7},{5,6},{6,5},{7,4},{8,11},{9,10},{10,... | collective-permute-start | bytes 6152 | tf_op jit(solution)/shard_map/ppermute | solution.py:388
  42.8 0.2 collective-permute-start.3
  43.0 0.2 collective-permute-start.2
  43.3 1.0 %collective-permute-done.4.refs_3_ = f32[1,512]{1,0:T(1,128)S(1)} collective-permute-done((f32[1,512]{1,0:T(1,128)S(1)}, f32[1,512]{1,0:T(1,128)S(1)}, u32[]{:S(2)}, u32[]{:S(2)}) %collective-permute-start.4) | collective-permute-done | bytes 2080 | tf_op jit(solution)/shard_map/ppermute | solution.py:388
  44.3 0.9 %collective-permute-done.3.refs_2_ = f32[1,512]{1,0:T(1,128)S(1)} collective-permute-done((f32[1,512]{1,0:T(1,128)S(1)}, f32[1,512]{1,0:T(1,128)S(1)}, u32[]{:S(2)}, u32[]{:S(2)}) %collective-permute-start.3) | collective-permute-done | bytes 2080 | tf_op jit(solution)/shard_map/ppermute | solution.py:388
  45.2 0.0 collective-permute-done.2.refs_1_
  45.2 1.1 %shard_map.67 = bf16[512,1024]{1,0:T(8,128)(2,1)} custom-call(f32[1,512]{1,0:T(1,128)S(1)} %get-tuple-element.18.refs_0_, f32[1,512]{1,0:T(1,128)S(1)} %collective-permute-done.2.refs_1_, f32[1,512]{1,0:T(1,128)S(1)} %collective-permute-done.3.refs_2_, f32[1,512]{1,0:T(1,128)S(1)} %collective-permute-done.4.refs_3_, ...), custom_call_target="tpu_custom_call" | custom-call | flops 1572864 | bytes 3145728 | tf_op jit(solution)/shard_map/pallas_call | solution.py:327
Async XLA Ops:
  1.1 29.8 %collective-permute-start = (bf16[256,1024]{1,0:T(8,128)(2,1)S(1)}, bf16[256,1024]{1,0:T(8,128)(2,1)S(1)}, u32[]{:S(2)}, u32[]{:S(2)}) collective-permute-start(bf16[256,1024]{1,0:T(8,128)(2,1)S(1)} %slice.3), channel_id=1, source_target_pairs={{0,4},{4,8},{8,12},{12,16},{16,20},{20,24},{24,28},{1,5},{5,9},{9,... | collective-permute-start | bytes 1572872 | tf_op jit(solution)/shard_map/ppermute | solution.py:339
  8.2 29.5 %collective-permute-start.1 = (bf16[256,1024]{1,0:T(8,128)(2,1)}, bf16[256,1024]{1,0:T(8,128)(2,1)S(1)}, u32[]{:S(2)}, u32[]{:S(2)}) collective-permute-start(bf16[256,1024]{1,0:T(8,128)(2,1)} %get-tuple-element.17), channel_id=1, source_target_pairs={{0,4},{4,8},{8,12},{12,16},{16,20},{20,24},{24,28},{1,5},{5,9},{9,... | collective-permute-start | bytes 1572872 | tf_op jit(solution)/shard_map/ppermute | solution.py:339
  11.4 19.6 %copy-start.2 = (s32[512]{0:T(512)S(1)}, s32[512]{0:T(512)}, u32[]{:S(2)}) copy-start(s32[512]{0:T(512)} %param.10) | copy-start | bytes 6148
  11.4 19.5 %all-to-all-start = ((bf16[8,8,1664]{2,1,0:T(8,128)(2,1)}), bf16[8,8,1664]{2,1,0:T(8,128)(2,1)S(1)}, u32[]{:S(2)}, u32[]{:S(2)}) async-start(bf16[8,8,1664]{2,1,0:T(8,128)(2,1)} %get-tuple-element.13), calls=%async_computation | async-start | bytes 425984 | tf_op jit(solution)/shard_map/all_to_all | solution.py:354
  16.0 15.0 %copy-start = (f32[3,4,8]{2,1,0:T(4,128)S(1)}, f32[3,4,8]{2,1,0:T(4,128)}, u32[]{:S(2)}) copy-start(f32[3,4,8]{2,1,0:T(4,128)} %scales.3) | copy-start | bytes 1156
  16.0 15.0 %copy-start.1 = (f32[1024]{0:T(1024)S(1)}, f32[1024]{0:T(1024)}, u32[]{:S(2)}) copy-start(f32[1024]{0:T(1024)} %param.11) | copy-start | bytes 12292
  38.2 6.1 %collective-permute-start.4 = (f32[1,512]{1,0:T(1,128)S(1)}, f32[1,512]{1,0:T(1,128)S(1)}, u32[]{:S(2)}, u32[]{:S(2)}) collective-permute-start(f32[1,512]{1,0:T(1,128)S(1)} %get-tuple-element.18.refs_0_), channel_id=1, source_target_pairs={{0,3},{1,2},{2,1},{3,0},{4,7},{5,6},{6,5},{7,4},{8,11},{9,10},{10,... | collective-permute-start | bytes 6152 | tf_op jit(solution)/shard_map/ppermute | solution.py:388
  42.8 2.4 %collective-permute-start.3 = (f32[1,512]{1,0:T(1,128)S(1)}, f32[1,512]{1,0:T(1,128)S(1)}, u32[]{:S(2)}, u32[]{:S(2)}) collective-permute-start(f32[1,512]{1,0:T(1,128)S(1)} %get-tuple-element.18.refs_0_), channel_id=1, source_target_pairs={{0,2},{1,3},{2,0},{3,1},{4,6},{5,7},{6,4},{7,5},{8,10},{9,11},{10,... | collective-permute-start | bytes 6152 | tf_op jit(solution)/shard_map/ppermute | solution.py:388
  43.0 2.2 %collective-permute-start.2 = (f32[1,512]{1,0:T(1,128)S(1)}, f32[1,512]{1,0:T(1,128)S(1)}, u32[]{:S(2)}, u32[]{:S(2)}) collective-permute-start(f32[1,512]{1,0:T(1,128)S(1)} %get-tuple-element.18.refs_0_), channel_id=1, source_target_pairs={{0,1},{1,0},{2,3},{3,2},{4,5},{5,4},{6,7},{7,6},{8,9},{9,8},{10,11... | collective-permute-start | bytes 6152 | tf_op jit(solution)/shard_map/ppermute | solution.py:388

commit v5 on v4

--- a/solution.py
+++ b/solution.py
@@ -335,10 +335,7 @@
             **more,
         )(*args)
 
-    def shifted(block):
-        return lax.ppermute(block, "seq", [(i - 1, i) for i in range(1, devices)])
-
-    prev_key = shifted(k_raw[half:])
+    prev_key = lax.ppermute(k_raw[half:], "seq", [(i, (i + 1) % devices) for i in range(devices)])
     table_pieces = 4
     table, tail_value = call(
         functools.partial(table_kernel, scale_rows, table_pieces),
@@ -353,7 +350,7 @@
     )
     table = lax.all_to_all(table, "seq", 0, 0, tiled=True)
     table = table.reshape(entries, wide)
-    prev_value = shifted(tail_value)
+    prev_value = lax.ppermute(tail_value, "seq", [(i - 1, i) for i in range(1, devices)])
     place = lax.axis_index("seq").astype(i32).reshape(1)
     gain = norm_gain.reshape(1, width)
     step_heads = 4

time: 46.7 us -> 44.9 us (0.961)
  starting transfers between devices: 16 us -> 14.1 us
    ppermute x2, starting transfers between devices: 6.3 us -> 4.44 us  [the longest x1 3.18 us: on_device(): lax.ppermute(tail_value, 'seq', [(i - 1, i) for i in range(1, devices)])]
  transfers between devices with their start and end apart: 6 -> 6, of which waited for: 3 -> 3; matrix products, arithmetic and copies ran while one was open for 0% -> 0% of each run, Pallas kernels for 23% -> 24%
where the time goes in v5:
time: 44.9 us; the launch traced here: 44.5 us
  waiting for transfers between devices  16.9 us (38%)
  starting transfers between devices  14.1 us (31%)
  Pallas kernels  12.3 us (27%)
  local copies, waits for them, and re-layouts  1.09 us (2%)
    all_to_all x1, waiting for transfers between devices, on_device(): table = lax.all_to_all(table, 'seq', 0, 0, tiled=True)  15 us
    pallas_call x4, Pallas kernels, call(): pl.pallas_call(kernel, out_shape=out_shape, in_specs=in_specs, out_specs=...  12.3 us
    ppermute x3, starting transfers between devices, on_device(): lax.ppermute(squares, 'head', [(i, i ^ d if pairs else (i + d) % head_dev...  5.09 us
    all_to_all x1, starting transfers between devices, on_device(): table = lax.all_to_all(table, 'seq', 0, 0, tiled=True)  4.58 us
    ppermute x1, starting transfers between devices, on_device(): lax.ppermute(tail_value, 'seq', [(i - 1, i) for i in range(1, devices)])  3.18 us
    ppermute x3, waiting for transfers between devices, on_device(): lax.ppermute(squares, 'head', [(i, i ^ d if pairs else (i + d) % head_dev...  1.96 us
    ppermute x1, starting transfers between devices, on_device(): lax.ppermute(k_raw[half:], 'seq', [(i, (i + 1) % devices) for i in range(...  1.26 us
    slice x1, local copies, waits for them, and re-layouts, on_device(): k_raw[half:]  1.08 us
  transfers between devices with their start and end apart: 6, of which 3 were waited for; matrix products, arithmetic and copies ran while one was open for 0% of the time, Pallas kernels for 24%

profile of v5, /device:TPU:17, one launch (start us, length us, event | category | flops | bytes accessed | tf_op | source)
XLA Modules:
  0.0 44.5 jit_solution(487938788890365201)
XLA Ops:
  0.0 1.1 %slice.3 = bf16[256,1024]{1,0:T(8,128)(2,1)S(1)} slice(bf16[512,1024]{1,0:T(8,128)(2,1)} %k_raw.3), slice={[256:512], [0:1024]} | slice | bytes 1048576 | tf_op jit(solution)/shard_map/slice | solution.py:338
  1.1 1.3 %collective-permute-start = (bf16[256,1024]{1,0:T(8,128)(2,1)S(1)}, bf16[256,1024]{1,0:T(8,128)(2,1)S(1)}, u32[]{:S(2)}, u32[]{:S(2)}) collective-permute-start(bf16[256,1024]{1,0:T(8,128)(2,1)S(1)} %slice.3), channel_id=1, source_target_pairs={{0,4},{4,8},{8,12},{12,16},{16,20},{20,24},{24,28},{28,0},{1,5},{5... | collective-permute-start | bytes 1572872 | tf_op jit(solution)/shard_map/ppermute | solution.py:338
  2.3 4.0 %shard_map.64 = (bf16[8,8,1664]{2,1,0:T(8,128)(2,1)}, bf16[256,1024]{1,0:T(8,128)(2,1)}) custom-call(f32[3,4,8]{2,1,0:T(4,128)} %scales.3, s32[1,512]{1,0:T(1,128)} %bitcast.7, bf16[512,1024]{1,0:T(8,128)(2,1)} %k_raw.3, bf16[512,1024]{1,0:T(8,128)(2,1)} %v_raw.3), custom_call_target="tpu_custom_call" | custom-call | flops 33554432 | bytes 2097152 | tf_op jit(solution)/shard_map/pallas_call | solution.py:327
  6.3 3.2 %collective-permute-start.1 = (bf16[256,1024]{1,0:T(8,128)(2,1)}, bf16[256,1024]{1,0:T(8,128)(2,1)S(1)}, u32[]{:S(2)}, u32[]{:S(2)}) collective-permute-start(bf16[256,1024]{1,0:T(8,128)(2,1)} %get-tuple-element.17), channel_id=1, source_target_pairs={{0,4},{4,8},{8,12},{12,16},{16,20},{20,24},{24,28},{1,5},{5,9},{9,... | collective-permute-start | bytes 1572872 | tf_op jit(solution)/shard_map/ppermute | solution.py:353
  9.5 0.0 copy-start.2
  9.5 4.6 %all-to-all-start = ((bf16[8,8,1664]{2,1,0:T(8,128)(2,1)}), bf16[8,8,1664]{2,1,0:T(8,128)(2,1)S(1)}, u32[]{:S(2)}, u32[]{:S(2)}) async-start(bf16[8,8,1664]{2,1,0:T(8,128)(2,1)} %get-tuple-element.13), calls=%async_computation | async-start | bytes 425984 | tf_op jit(solution)/shard_map/all_to_all | solution.py:351
  14.1 0.0 copy-start
  14.1 0.0 copy-start.1
  14.1 15.0 %all-to-all-done = bf16[8,8,1664]{2,1,0:T(8,128)(2,1)S(1)} async-done(((bf16[8,8,1664]{2,1,0:T(8,128)(2,1)}), bf16[8,8,1664]{2,1,0:T(8,128)(2,1)S(1)}, u32[]{:S(2)}, u32[]{:S(2)}) %all-to-all-start) | async-done | bytes 213024 | tf_op jit(solution)/shard_map/all_to_all | solution.py:351
  29.1 0.0 collective-permute-done.prev_raw
  29.1 0.0 copy-done.2
  29.1 0.0 copy-done
  29.1 0.0 copy-done.1
  29.1 6.7 %shard_map.65 = (f32[256,1024]{1,0:T(8,128)S(1)}, bf16[8,256,256]{2,1,0:T(8,128)(2,1)S(1)}, f32[256,1024]{1,0:T(8,128)S(1)}, f32[1,256]{1,0:T(1,128)S(1)}) custom-call(s32[1]{0:T(128)} %bitcast.place, f32[3,4,8]{2,1,0:T(4,128)S(1)} %copy-done, s32[1,512]{1,0:T(1,128)S(1)} %bitcast.8, bf16[64,1664]{1,0:T(8,128)(2,1)S(1)} %bitcast.4, f32[1,1024]{1,0:T(1,128)S(1)} %bitcast.5, ...), custom_call_target="tpu_custom_call" | custom-call | flops 1073741824 | bytes 6291456 | tf_op jit(solution)/shard_map/pallas_call | solution.py:327
  35.8 0.0 collective-permute-done.1.prev_value
  35.8 0.5 %shard_map.66 = (f32[256,1024]{1,0:T(8,128)S(1)}, f32[1,512]{1,0:T(1,128)S(1)}) custom-call(f32[256,1024]{1,0:T(8,128)S(1)} %get-tuple-element.14.opened, bf16[8,256,256]{2,1,0:T(8,128)(2,1)S(1)} %get-tuple-element.15.prev_weights, f32[1,1024]{1,0:T(1,128)S(1)} %bitcast.6, f32[1,256]{1,0:T(1,128)S(1)} %get-tuple-element.16.back_squares, ...), custom_call_target="tpu_custom_call" | custom-call | flops 134217728 | bytes 4194304 | tf_op jit(solution)/shard_map/pallas_call | solution.py:327
  36.3 4.6 %collective-permute-start.4 = (f32[1,512]{1,0:T(1,128)S(1)}, f32[1,512]{1,0:T(1,128)S(1)}, u32[]{:S(2)}, u32[]{:S(2)}) collective-permute-start(f32[1,512]{1,0:T(1,128)S(1)} %get-tuple-element.18.refs_0_), channel_id=1, source_target_pairs={{0,3},{1,2},{2,1},{3,0},{4,7},{5,6},{6,5},{7,4},{8,11},{9,10},{10,... | collective-permute-start | bytes 6152 | tf_op jit(solution)/shard_map/ppermute | solution.py:385
  40.9 0.2 collective-permute-start.3
  41.2 0.2 collective-permute-start.2
  41.4 1.0 %collective-permute-done.4.refs_3_ = f32[1,512]{1,0:T(1,128)S(1)} collective-permute-done((f32[1,512]{1,0:T(1,128)S(1)}, f32[1,512]{1,0:T(1,128)S(1)}, u32[]{:S(2)}, u32[]{:S(2)}) %collective-permute-start.4) | collective-permute-done | bytes 2080 | tf_op jit(solution)/shard_map/ppermute | solution.py:385
  42.4 0.9 %collective-permute-done.3.refs_2_ = f32[1,512]{1,0:T(1,128)S(1)} collective-permute-done((f32[1,512]{1,0:T(1,128)S(1)}, f32[1,512]{1,0:T(1,128)S(1)}, u32[]{:S(2)}, u32[]{:S(2)}) %collective-permute-start.3) | collective-permute-done | bytes 2080 | tf_op jit(solution)/shard_map/ppermute | solution.py:385
  43.4 0.0 collective-permute-done.2.refs_1_
  43.4 1.1 %shard_map.67 = bf16[512,1024]{1,0:T(8,128)(2,1)} custom-call(f32[1,512]{1,0:T(1,128)S(1)} %get-tuple-element.18.refs_0_, f32[1,512]{1,0:T(1,128)S(1)} %collective-permute-done.2.refs_1_, f32[1,512]{1,0:T(1,128)S(1)} %collective-permute-done.3.refs_2_, f32[1,512]{1,0:T(1,128)S(1)} %collective-permute-done.4.refs_3_, ...), custom_call_target="tpu_custom_call" | custom-call | flops 1572864 | bytes 3145728 | tf_op jit(solution)/shard_map/pallas_call | solution.py:327
Async XLA Ops:
  1.1 28.0 %collective-permute-start = (bf16[256,1024]{1,0:T(8,128)(2,1)S(1)}, bf16[256,1024]{1,0:T(8,128)(2,1)S(1)}, u32[]{:S(2)}, u32[]{:S(2)}) collective-permute-start(bf16[256,1024]{1,0:T(8,128)(2,1)S(1)} %slice.3), channel_id=1, source_target_pairs={{0,4},{4,8},{8,12},{12,16},{16,20},{20,24},{24,28},{28,0},{1,5},{5... | collective-permute-start | bytes 1572872 | tf_op jit(solution)/shard_map/ppermute | solution.py:338
  6.3 29.5 %collective-permute-start.1 = (bf16[256,1024]{1,0:T(8,128)(2,1)}, bf16[256,1024]{1,0:T(8,128)(2,1)S(1)}, u32[]{:S(2)}, u32[]{:S(2)}) collective-permute-start(bf16[256,1024]{1,0:T(8,128)(2,1)} %get-tuple-element.17), channel_id=1, source_target_pairs={{0,4},{4,8},{8,12},{12,16},{16,20},{20,24},{24,28},{1,5},{5,9},{9,... | collective-permute-start | bytes 1572872 | tf_op jit(solution)/shard_map/ppermute | solution.py:353
  9.5 19.6 %copy-start.2 = (s32[512]{0:T(512)S(1)}, s32[512]{0:T(512)}, u32[]{:S(2)}) copy-start(s32[512]{0:T(512)} %param.10) | copy-start | bytes 6148
  9.5 19.6 %all-to-all-start = ((bf16[8,8,1664]{2,1,0:T(8,128)(2,1)}), bf16[8,8,1664]{2,1,0:T(8,128)(2,1)S(1)}, u32[]{:S(2)}, u32[]{:S(2)}) async-start(bf16[8,8,1664]{2,1,0:T(8,128)(2,1)} %get-tuple-element.13), calls=%async_computation | async-start | bytes 425984 | tf_op jit(solution)/shard_map/all_to_all | solution.py:351
  14.1 15.0 %copy-start = (f32[3,4,8]{2,1,0:T(4,128)S(1)}, f32[3,4,8]{2,1,0:T(4,128)}, u32[]{:S(2)}) copy-start(f32[3,4,8]{2,1,0:T(4,128)} %scales.3) | copy-start | bytes 1156
  14.1 15.0 %copy-start.1 = (f32[1024]{0:T(1024)S(1)}, f32[1024]{0:T(1024)}, u32[]{:S(2)}) copy-start(f32[1024]{0:T(1024)} %param.11) | copy-start | bytes 12292
  36.3 6.1 %collective-permute-start.4 = (f32[1,512]{1,0:T(1,128)S(1)}, f32[1,512]{1,0:T(1,128)S(1)}, u32[]{:S(2)}, u32[]{:S(2)}) collective-permute-start(f32[1,512]{1,0:T(1,128)S(1)} %get-tuple-element.18.refs_0_), channel_id=1, source_target_pairs={{0,3},{1,2},{2,1},{3,0},{4,7},{5,6},{6,5},{7,4},{8,11},{9,10},{10,... | collective-permute-start | bytes 6152 | tf_op jit(solution)/shard_map/ppermute | solution.py:385
  40.9 2.4 %collective-permute-start.3 = (f32[1,512]{1,0:T(1,128)S(1)}, f32[1,512]{1,0:T(1,128)S(1)}, u32[]{:S(2)}, u32[]{:S(2)}) collective-permute-start(f32[1,512]{1,0:T(1,128)S(1)} %get-tuple-element.18.refs_0_), channel_id=1, source_target_pairs={{0,2},{1,3},{2,0},{3,1},{4,6},{5,7},{6,4},{7,5},{8,10},{9,11},{10,... | collective-permute-start | bytes 6152 | tf_op jit(solution)/shard_map/ppermute | solution.py:385
  41.2 2.2 %collective-permute-start.2 = (f32[1,512]{1,0:T(1,128)S(1)}, f32[1,512]{1,0:T(1,128)S(1)}, u32[]{:S(2)}, u32[]{:S(2)}) collective-permute-start(f32[1,512]{1,0:T(1,128)S(1)} %get-tuple-element.18.refs_0_), channel_id=1, source_target_pairs={{0,1},{1,0},{2,3},{3,2},{4,5},{5,4},{6,7},{7,6},{8,9},{9,8},{10,11... | collective-permute-start | bytes 6152 | tf_op jit(solution)/shard_map/ppermute | solution.py:385

commit v6 on v5

--- a/solution.py
+++ b/solution.py
@@ -12,7 +12,7 @@
 HD = 128
 CAP = 4
 LANES = 128
-SLOTS = CAP + 2
+SLOTS = CAP + 1
 EARLY = CAP + 1
 epsilon = 1e-06
 factor = math.log2(math.e) / math.sqrt(HD)
@@ -51,11 +51,20 @@
     return jnp.concatenate(parts, axis=0)
 
 
-def table_kernel(scale_rows, pieces, scales, ids, k_raw, v_raw, table, tail_value, keys, values, sums, packed, tails, sems, out_sems):
+def table_kernel(
+    scale_rows, pieces, scales_in, ids_in, k_raw, v_raw, table, tail_value, extra_out,
+    scales, ids, keys, values, sums, packed, tails, extra, extra_packed, sems, small_sems, out_sems,
+):
     tokens = ids.shape[1]
     half = tokens // 2
     heads = sums.shape[0]
     piece = heads * HD // pieces
+    small = [
+        pltpu.make_async_copy(scales_in, scales, small_sems.at[0]),
+        pltpu.make_async_copy(ids_in, ids, small_sems.at[1]),
+    ]
+    for copy in small:
+        copy.start()
     copies = []
     for number in range(pieces):
         cols = slice(number * piece, (number + 1) * piece)
@@ -63,6 +72,8 @@
             copy = pltpu.make_async_copy(source.at[:, cols], target.at[:, cols], sems.at[number, which])
             copy.start()
             copies.append(copy)
+    for copy in small:
+        copy.wait()
     row = ids[...]
     local = row - row[:, 0:1]
     last = local[:, tokens - 1 :]
@@ -77,25 +88,28 @@
     head_row = iota((heads, LANES), 0)
     meta = jnp.zeros((heads, LANES), i32)
     for index in range(SLOTS):
-        seg = row[:, 0:1] + (last if index == EARLY else index)
+        seg = row[:, 0:1] + index
         number = count[index : index + 1]
         for place, value in enumerate((seg & 127, seg >> 7, number & 127, number >> 7)):
             meta = jnp.where(lane == 4 * index + place, value, meta)
+    sums[:, 2 * SLOTS * HD :] = meta.astype(f32)
+    number = count[EARLY : EARLY + 1]
+    meta = jnp.where(lane == 0, number & 127, jnp.where(lane == 1, number >> 7, 0))
     tail_blocks = half // scale_rows
     scale = jnp.zeros((heads, LANES), f32)
     part = jnp.zeros((heads, LANES), i32)
     for block in range(tail_blocks):
         for head in range(heads):
             value = scales[1, scales.shape[1] - tail_blocks + block, head]
-            here = (lane >= 4 * SLOTS + 3 * block) & (lane < 4 * SLOTS + 3 * block + 3)
+            here = (lane >= 2 + 3 * block) & (lane < 5 + 3 * block)
             scale = jnp.where(here & (head_row == head), value, scale)
         for place in range(3):
-            part = jnp.where(lane == 4 * SLOTS + 3 * block + place, place, part)
+            part = jnp.where(lane == 2 + 3 * block + place, place, part)
     high = scale.astype(bf16).astype(f32)
     middle = (scale - high).astype(bf16).astype(f32)
     low = scale - high - middle
     scale = jnp.where(part == 0, high, jnp.where(part == 1, middle, low))
-    sums[:, 2 * SLOTS * HD :] = jnp.where(lane < 4 * SLOTS, meta.astype(f32), scale)
+    extra[:, 2 * HD :] = jnp.where(lane < 2, meta.astype(f32), scale)
     writes = []
     for number in range(pieces):
         found = []
@@ -106,19 +120,22 @@
                 value = dequantized(source, scales, 1 + which, head, cols, scale_rows)
                 if which:
                     tails[:, cols] = value[half:]
-                found.append((head, which * SLOTS, nn_dot(pick, value)))
-        for head, start, total in found:
+                found.append((head, which, nn_dot(pick, value)))
+        for head, which, total in found:
             for index in range(SLOTS):
-                where = slice((start + index) * HD, (start + index + 1) * HD)
+                where = slice((which * SLOTS + index) * HD, (which * SLOTS + index + 1) * HD)
                 sums[head : head + 1, where] = total[index : index + 1]
+            extra[head : head + 1, which * HD : (which + 1) * HD] = total[EARLY : EARLY + 1]
         cols = slice(number * piece, (number + 1) * piece)
         copy = pltpu.make_async_copy(tails.at[:, cols], tail_value.at[:, cols], out_sems.at[number])
         copy.start()
         writes.append(copy)
     packed[...] = jnp.broadcast_to(sums[...].astype(bf16)[None], packed.shape)
-    copy = pltpu.make_async_copy(packed, table, out_sems.at[pieces])
-    copy.start()
-    writes.append(copy)
+    extra_packed[...] = extra[...].astype(bf16)
+    for number, (source, target) in enumerate(((packed, table), (extra_packed, extra_out))):
+        copy = pltpu.make_async_copy(source, target, out_sems.at[pieces + number])
+        copy.start()
+        writes.append(copy)
     for copy in writes:
         copy.wait()
 
@@ -129,9 +146,9 @@
 
 def main_kernel(
     scale_rows, device_count,
-    place, scales, ids, table, gain, q_raw, k_raw, v_raw, prev_raw,
+    place, scales, ids, table, extra, gain, q_raw, k_raw, v_raw, prev_raw,
     open_out, prev_weights, back_out, back_squares,
-    near, far, picks, bias, inverse, prev_mask, prev_scales,
+    near, far, picks, bias, inverse, prev_mask, extras, is_early,
 ):
     step = pl.program_id(0)
     tokens = ids.shape[1]
@@ -162,19 +179,22 @@
         for index in range(SLOTS):
             seg = info[4 * index : 4 * index + 1] + 128.0 * info[4 * index + 1 : 4 * index + 2]
             number = info[4 * index + 2 : 4 * index + 3] + 128.0 * info[4 * index + 3 : 4 * index + 4]
-            if index == EARLY:
-                picked = (land == lands) & (entry_device == me - 1)
-            else:
-                is_open = seg == first.astype(f32)
-                picked = (land < lands) & (land.astype(f32) == seg)
-                picked = picked | ((land == lands) & is_open & (entry_device < me - 1))
-                picked = picked | ((land == lands + 1) & is_open & (entry_device < me))
-                picked = picked | ((land == lands + 2) & is_open & (entry_device == me - 1))
+            is_open = seg == first.astype(f32)
+            picked = (land < lands) & (land.astype(f32) == seg)
+            picked = picked | ((land == lands) & is_open & (entry_device < me - 1))
+            picked = picked | ((land == lands + 1) & is_open & (entry_device < me))
+            picked = picked | ((land == lands + 2) & is_open & (entry_device == me - 1))
             picked = picked.astype(f32)
             picks[index] = picked.astype(bf16)
             count = count + jnp.sum(
                 picked * jnp.where(entry_head == 0, number, 0.0), axis=1, keepdims=True
             )
+        early = ((iota((land_pad, HD), 0) == lands) & (me > 0)).astype(f32)
+        is_early[...] = early
+        info = extra[...].astype(f32)
+        for group in range(all_heads // heads):
+            extras[group] = info[group * heads : (group + 1) * heads]
+        count = count + early[:, 0:1] * (info[0:1, 2 * HD : 2 * HD + 1] + 128.0 * info[0:1, 2 * HD + 1 : 2 * HD + 2])
         inverse[...] = jnp.broadcast_to(1.0 / jnp.maximum(count, 1.0), inverse.shape)
         amount = jnp.broadcast_to(count, (land_pad, LANES))
         log_count = jnp.log2(jnp.maximum(amount, 1.0))
@@ -189,11 +209,6 @@
             live = (iota((half, LANES), 0) >= half - tail) & (row[:, left : left + LANES] == first)
             prev_mask[:, left : left + LANES] = jnp.where(live, 0.0, -jnp.inf)
         back_squares[...] = jnp.zeros(back_squares.shape, f32)
-        info = table[:, 2 * SLOTS * HD :].astype(f32).reshape(device_count, all_heads, LANES)
-        of_device = lax.broadcasted_iota(i32, info.shape, 0)
-        info = jnp.sum(jnp.where(of_device == me - 1, info, 0.0), axis=0)
-        for group in range(all_heads // heads):
-            prev_scales[group] = info[group * heads : (group + 1) * heads]
 
     def prepared(head):
         cols = slice(head * HD, (head + 1) * HD)
@@ -203,15 +218,15 @@
         value = dequantized(v_raw, scales, 2, index, cols, scale_rows).T
         pieces = []
         for block in range(half // scale_rows):
-            at = 4 * SLOTS + 3 * block
-            parts = prev_scales[step, head : head + 1, at : at + 3]
+            at = 2 * HD + 2 + 3 * block
+            parts = extras[step, head : head + 1, at : at + 3]
             scale = parts[:, 0:1] + parts[:, 1:2] + parts[:, 2:3]
             raw = prev_raw[block * scale_rows : (block + 1) * scale_rows, cols]
             pieces.append((raw.astype(f32) * scale).astype(bf16))
         prev_key = jnp.concatenate(pieces, axis=0)
         mine = (entry_head == index).astype(f32).astype(bf16)
-        land_key = jnp.zeros((land_pad, HD), f32)
-        land_value = jnp.zeros((land_pad, HD), f32)
+        land_key = is_early[...] * extras[step, head : head + 1, :HD]
+        land_value = is_early[...] * extras[step, head : head + 1, HD : 2 * HD]
         for slot in range(SLOTS):
             pick = picks[slot] * mine
             land_key = land_key + nn_dot(pick, table[:, slot * HD : (slot + 1) * HD])
@@ -335,21 +350,25 @@
             **more,
         )(*args)
 
-    prev_key = lax.ppermute(k_raw[half:], "seq", [(i, (i + 1) % devices) for i in range(devices)])
+    cycle = [(i, (i + 1) % devices) for i in range(devices)]
+    prev_key = lax.ppermute(k_raw[half:], "seq", cycle)
     table_pieces = 4
-    table, tail_value = call(
+    table, tail_value, extra = call(
         functools.partial(table_kernel, scale_rows, table_pieces),
-        [sds((devices, heads, wide), bf16), sds((half, width), bf16)],
-        [smem, vmem, hbm, hbm], (block_scales, ids, k_raw, v_raw),
-        64 * tokens * width, 4 * tokens * width, out_specs=[hbm, hbm], limit=whole_vmem,
+        [sds((devices, heads, wide), bf16), sds((half, width), bf16), sds((heads, 3 * HD), bf16)],
+        [hbm] * 4, (block_scales, ids, k_raw, v_raw),
+        64 * tokens * width, 4 * tokens * width, out_specs=[hbm] * 3, limit=whole_vmem,
         scratch=[
+            pltpu.SMEM(block_scales.shape, f32), pltpu.VMEM((1, tokens), i32),
             pltpu.VMEM((tokens, width), bf16), pltpu.VMEM((tokens, width), bf16),
             pltpu.VMEM((heads, wide), f32), pltpu.VMEM((devices, heads, wide), bf16), pltpu.VMEM((half, width), bf16),
-            pltpu.SemaphoreType.DMA((table_pieces, 2)), pltpu.SemaphoreType.DMA((table_pieces + 1,)),
+            pltpu.VMEM((heads, 3 * HD), f32), pltpu.VMEM((heads, 3 * HD), bf16),
+            pltpu.SemaphoreType.DMA((table_pieces, 2)), pltpu.SemaphoreType.DMA((2,)), pltpu.SemaphoreType.DMA((table_pieces + 2,)),
         ],
     )
     table = lax.all_to_all(table, "seq", 0, 0, tiled=True)
     table = table.reshape(entries, wide)
+    extra = lax.ppermute(extra, "seq", cycle)
     prev_value = lax.ppermute(tail_value, "seq", [(i - 1, i) for i in range(1, devices)])
     place = lax.axis_index("seq").astype(i32).reshape(1)
     gain = norm_gain.reshape(1, width)
@@ -365,14 +384,14 @@
     opened, prev_weights, back, back_squares = call(
         functools.partial(main_kernel, scale_rows, devices),
         [sds((half, width), f32), sds((heads, half, half), bf16), sds((half, width), f32), sds((1, half), f32)],
-        [smem, smem, whole(1, tokens), whole(entries, wide), pl.BlockSpec((1, piece), lambda s: (0, s))] + [rows_in] * 3 + [half_rows],
-        (place, block_scales, ids, table, gain, *(pltpu.with_memory_space_constraint(x, pltpu.HBM) for x in (q_raw, k_raw, v_raw)), prev_key),
+        [smem, smem, whole(1, tokens), whole(entries, wide), whole(heads, 3 * HD), pl.BlockSpec((1, piece), lambda s: (0, s))] + [rows_in] * 3 + [half_rows],
+        (place, block_scales, ids, table, extra, gain, *(pltpu.with_memory_space_constraint(x, pltpu.HBM) for x in (q_raw, k_raw, v_raw)), prev_key),
         8 * half * tokens * width, 12 * tokens * width, grid=(steps,),
         out_specs=[half_rows, pl.BlockSpec((step_heads, half, half), lambda s: (s, 0, 0)), half_rows, whole(1, half)],
         scratch=[
             pltpu.VMEM((half, half), f32), pltpu.VMEM((tokens, half), f32),
             pltpu.VMEM((SLOTS, land_pad, entries), bf16), pltpu.VMEM((land_pad, tokens), f32),
-            pltpu.VMEM((land_pad, HD), f32), pltpu.VMEM((half, half), f32), pltpu.VMEM((steps, step_heads, LANES), f32),
+            pltpu.VMEM((land_pad, HD), f32), pltpu.VMEM((half, half), f32), pltpu.VMEM((steps, step_heads, 3 * HD), f32), pltpu.VMEM((land_pad, HD), f32),
         ],
     )
     front, squares = call(

time: 44.9 us -> 44.6 us (level)
  the two profiles are of different devices: /device:TPU:17 before, /device:TPU:16 now
where the time goes in v6:
time: 44.6 us; the launch traced here: 43.7 us
  waiting for transfers between devices  16.8 us (38%)
  starting transfers between devices  13.5 us (30%)
  Pallas kernels  12.2 us (27%)
  local copies, waits for them, and re-layouts  1.09 us (2%)
    ppermute x1, waiting for transfers between devices, on_device(): extra = lax.ppermute(extra, 'seq', cycle)  15 us
    pallas_call x4, Pallas kernels, call(): pl.pallas_call(kernel, out_shape=out_shape, in_specs=in_specs, out_specs=...  12.2 us
    all_to_all x1, starting transfers between devices, on_device(): table = lax.all_to_all(table, 'seq', 0, 0, tiled=True)  5.14 us
    ppermute x1, starting transfers between devices, on_device(): lax.ppermute(tail_value, 'seq', [(i - 1, i) for i in range(1, devices)])  3.46 us
    ppermute x3, starting transfers between devices, on_device(): lax.ppermute(squares, 'head', [(i, i ^ d if pairs else (i + d) % head_dev...  1.92 us
    ppermute x3, waiting for transfers between devices, on_device(): lax.ppermute(squares, 'head', [(i, i ^ d if pairs else (i + d) % head_dev...  1.8 us
    ppermute x1, starting transfers between devices, on_device(): prev_key = lax.ppermute(k_raw[half:], 'seq', cycle)  1.54 us
    ppermute x1, starting transfers between devices, on_device(): extra = lax.ppermute(extra, 'seq', cycle)  1.46 us
  transfers between devices with their start and end apart: 7, of which 3 were waited for; matrix products, arithmetic and copies ran while one was open for 0% of the time, Pallas kernels for 24%

profile of v6, /device:TPU:16, one launch (start us, length us, event | category | flops | bytes accessed | tf_op | source)
XLA Modules:
  0.0 43.7 jit_solution(8504759134441130611)
XLA Ops:
  0.0 1.1 %slice.3 = bf16[256,1024]{1,0:T(8,128)(2,1)S(1)} slice(bf16[512,1024]{1,0:T(8,128)(2,1)} %k_raw.3), slice={[256:512], [0:1024]} | slice | bytes 1048576 | tf_op jit(solution)/shard_map/slice | solution.py:354
  1.1 1.5 %collective-permute-start.1 = (bf16[256,1024]{1,0:T(8,128)(2,1)S(1)}, bf16[256,1024]{1,0:T(8,128)(2,1)S(1)}, u32[]{:S(2)}, u32[]{:S(2)}) collective-permute-start(bf16[256,1024]{1,0:T(8,128)(2,1)S(1)} %slice.3), channel_id=1, source_target_pairs={{0,4},{4,8},{8,12},{12,16},{16,20},{20,24},{24,28},{28,0},{1,5},{5... | collective-permute-start | bytes 1572872 | tf_op jit(solution)/shard_map/ppermute | solution.py:354
  2.6 3.8 %shard_map.64 = (bf16[8,8,1408]{2,1,0:T(8,128)(2,1)}, bf16[256,1024]{1,0:T(8,128)(2,1)}, bf16[8,384]{1,0:T(8,128)(2,1)}) custom-call(f32[3,4,8]{2,1,0:T(4,128)} %scales.1, s32[1,512]{1,0:T(1,128)} %bitcast.7, bf16[512,1024]{1,0:T(8,128)(2,1)} %k_raw.3, bf16[512,1024]{1,0:T(8,128)(2,1)} %v_raw.3), custom_call_target="tpu_custom_call" | custom-call | flops 33554432 | bytes 2097152 | tf_op jit(solution)/shard_map/pallas_call | solution.py:342
  6.4 3.5 %collective-permute-start.2 = (bf16[256,1024]{1,0:T(8,128)(2,1)}, bf16[256,1024]{1,0:T(8,128)(2,1)S(1)}, u32[]{:S(2)}, u32[]{:S(2)}) collective-permute-start(bf16[256,1024]{1,0:T(8,128)(2,1)} %get-tuple-element.19), channel_id=1, source_target_pairs={{0,4},{4,8},{8,12},{12,16},{16,20},{20,24},{24,28},{1,5},{5,9},{9,... | collective-permute-start | bytes 1572872 | tf_op jit(solution)/shard_map/ppermute | solution.py:372
  9.9 0.0 copy-start.3
  9.9 0.0 copy-start.2
  9.9 5.1 %all-to-all-start = ((bf16[8,8,1408]{2,1,0:T(8,128)(2,1)}), bf16[8,8,1408]{2,1,0:T(8,128)(2,1)S(1)}, u32[]{:S(2)}, u32[]{:S(2)}) async-start(bf16[8,8,1408]{2,1,0:T(8,128)(2,1)} %get-tuple-element.14), calls=%async_computation | async-start | bytes 360448 | tf_op jit(solution)/shard_map/all_to_all | solution.py:369
  15.0 0.0 copy-done.3
  15.0 1.5 %collective-permute-start = (bf16[8,384]{1,0:T(8,128)(2,1)S(1)}, bf16[8,384]{1,0:T(8,128)(2,1)S(1)}, u32[]{:S(2)}, u32[]{:S(2)}) collective-permute-start(bf16[8,384]{1,0:T(8,128)(2,1)S(1)} %copy-done.3), channel_id=1, source_target_pairs={{0,4},{4,8},{8,12},{12,16},{16,20},{20,24},{24,28},{28,0},{1,5},{5... | collective-permute-start | bytes 18440 | tf_op jit(solution)/shard_map/ppermute | solution.py:371
  16.5 0.0 copy-start
  16.5 0.0 copy-start.1
  16.5 15.0 %collective-permute-done.extra = bf16[8,384]{1,0:T(8,128)(2,1)S(1)} collective-permute-done((bf16[8,384]{1,0:T(8,128)(2,1)S(1)}, bf16[8,384]{1,0:T(8,128)(2,1)S(1)}, u32[]{:S(2)}, u32[]{:S(2)}) %collective-permute-start) | collective-permute-done | bytes 6176 | tf_op jit(solution)/shard_map/ppermute | solution.py:371
  31.4 0.0 all-to-all-done
  31.5 0.0 collective-permute-done.1.prev_raw
  31.5 0.0 copy-done.2
  31.5 0.0 copy-done
  31.5 0.0 copy-done.1
  31.5 6.8 %shard_map.65 = (f32[256,1024]{1,0:T(8,128)S(1)}, bf16[8,256,256]{2,1,0:T(8,128)(2,1)S(1)}, f32[256,1024]{1,0:T(8,128)S(1)}, f32[1,256]{1,0:T(1,128)S(1)}) custom-call(s32[1]{0:T(128)} %bitcast.place, f32[3,4,8]{2,1,0:T(4,128)S(1)} %copy-done, s32[1,512]{1,0:T(1,128)S(1)} %bitcast.8, bf16[64,1408]{1,0:T(8,128)(2,1)S(1)} %bitcast.4, ...), custom_call_target="tpu_custom_call" | custom-call | flops 1073741824 | bytes 6291456 | tf_op jit(solution)/shard_map/pallas_call | solution.py:342
  38.3 0.0 collective-permute-done.2.prev_value
  38.3 0.5 %shard_map.66 = (f32[256,1024]{1,0:T(8,128)S(1)}, f32[1,512]{1,0:T(1,128)S(1)}) custom-call(f32[256,1024]{1,0:T(8,128)S(1)} %get-tuple-element.16.opened, bf16[8,256,256]{2,1,0:T(8,128)(2,1)S(1)} %get-tuple-element.17.prev_weights, f32[1,1024]{1,0:T(1,128)S(1)} %bitcast.6, f32[1,256]{1,0:T(1,128)S(1)} %get-tuple-element.18.back_squares, ...), custom_call_target="tpu_custom_call" | custom-call | flops 134217728 | bytes 4194304 | tf_op jit(solution)/shard_map/pallas_call | solution.py:342
  38.8 0.1 collective-permute-start.5
  38.9 1.6 %collective-permute-start.4 = (f32[1,512]{1,0:T(1,128)S(1)}, f32[1,512]{1,0:T(1,128)S(1)}, u32[]{:S(2)}, u32[]{:S(2)}) collective-permute-start(f32[1,512]{1,0:T(1,128)S(1)} %get-tuple-element.20.refs_0_), channel_id=1, source_target_pairs={{0,2},{1,3},{2,0},{3,1},{4,6},{5,7},{6,4},{7,5},{8,10},{9,11},{10,... | collective-permute-start | bytes 6152 | tf_op jit(solution)/shard_map/ppermute | solution.py:404
  40.5 0.3 collective-permute-start.3
  40.8 1.1 %collective-permute-done.5.refs_3_ = f32[1,512]{1,0:T(1,128)S(1)} collective-permute-done((f32[1,512]{1,0:T(1,128)S(1)}, f32[1,512]{1,0:T(1,128)S(1)}, u32[]{:S(2)}, u32[]{:S(2)}) %collective-permute-start.5) | collective-permute-done | bytes 2080 | tf_op jit(solution)/shard_map/ppermute | solution.py:404
  41.9 0.7 %collective-permute-done.4.refs_2_ = f32[1,512]{1,0:T(1,128)S(1)} collective-permute-done((f32[1,512]{1,0:T(1,128)S(1)}, f32[1,512]{1,0:T(1,128)S(1)}, u32[]{:S(2)}, u32[]{:S(2)}) %collective-permute-start.4) | collective-permute-done | bytes 2080 | tf_op jit(solution)/shard_map/ppermute | solution.py:404
  42.6 0.0 collective-permute-done.3.refs_1_
  42.6 1.1 %shard_map.67 = bf16[512,1024]{1,0:T(8,128)(2,1)} custom-call(f32[1,512]{1,0:T(1,128)S(1)} %get-tuple-element.20.refs_0_, f32[1,512]{1,0:T(1,128)S(1)} %collective-permute-done.3.refs_1_, f32[1,512]{1,0:T(1,128)S(1)} %collective-permute-done.4.refs_2_, f32[1,512]{1,0:T(1,128)S(1)} %collective-permute-done.5.refs_3_, ...), custom_call_target="tpu_custom_call" | custom-call | flops 1572864 | bytes 3145728 | tf_op jit(solution)/shard_map/pallas_call | solution.py:342
Async XLA Ops:
  1.1 30.4 %collective-permute-start.1 = (bf16[256,1024]{1,0:T(8,128)(2,1)S(1)}, bf16[256,1024]{1,0:T(8,128)(2,1)S(1)}, u32[]{:S(2)}, u32[]{:S(2)}) collective-permute-start(bf16[256,1024]{1,0:T(8,128)(2,1)S(1)} %slice.3), channel_id=1, source_target_pairs={{0,4},{4,8},{8,12},{12,16},{16,20},{20,24},{24,28},{28,0},{1,5},{5... | collective-permute-start | bytes 1572872 | tf_op jit(solution)/shard_map/ppermute | solution.py:354
  6.4 31.9 %collective-permute-start.2 = (bf16[256,1024]{1,0:T(8,128)(2,1)}, bf16[256,1024]{1,0:T(8,128)(2,1)S(1)}, u32[]{:S(2)}, u32[]{:S(2)}) collective-permute-start(bf16[256,1024]{1,0:T(8,128)(2,1)} %get-tuple-element.19), channel_id=1, source_target_pairs={{0,4},{4,8},{8,12},{12,16},{16,20},{20,24},{24,28},{1,5},{5,9},{9,... | collective-permute-start | bytes 1572872 | tf_op jit(solution)/shard_map/ppermute | solution.py:372
  9.9 5.2 %copy-start.3 = (bf16[8,384]{1,0:T(8,128)(2,1)S(1)}, bf16[8,384]{1,0:T(8,128)(2,1)}, u32[]{:S(2)}) copy-start(bf16[8,384]{1,0:T(8,128)(2,1)} %get-tuple-element.15) | copy-start | bytes 18436
  9.9 21.6 %copy-start.2 = (s32[512]{0:T(512)S(1)}, s32[512]{0:T(512)}, u32[]{:S(2)}) copy-start(s32[512]{0:T(512)} %param.10) | copy-start | bytes 6148
  9.9 21.6 %all-to-all-start = ((bf16[8,8,1408]{2,1,0:T(8,128)(2,1)}), bf16[8,8,1408]{2,1,0:T(8,128)(2,1)S(1)}, u32[]{:S(2)}, u32[]{:S(2)}) async-start(bf16[8,8,1408]{2,1,0:T(8,128)(2,1)} %get-tuple-element.14), calls=%async_computation | async-start | bytes 360448 | tf_op jit(solution)/shard_map/all_to_all | solution.py:369
  15.0 16.4 %collective-permute-start = (bf16[8,384]{1,0:T(8,128)(2,1)S(1)}, bf16[8,384]{1,0:T(8,128)(2,1)S(1)}, u32[]{:S(2)}, u32[]{:S(2)}) collective-permute-start(bf16[8,384]{1,0:T(8,128)(2,1)S(1)} %copy-done.3), channel_id=1, source_target_pairs={{0,4},{4,8},{8,12},{12,16},{16,20},{20,24},{24,28},{28,0},{1,5},{5... | collective-permute-start | bytes 18440 | tf_op jit(solution)/shard_map/ppermute | solution.py:371
  16.5 15.0 %copy-start = (f32[3,4,8]{2,1,0:T(4,128)S(1)}, f32[3,4,8]{2,1,0:T(4,128)}, u32[]{:S(2)}) copy-start(f32[3,4,8]{2,1,0:T(4,128)} %scales.1) | copy-start | bytes 1156
  16.5 15.0 %copy-start.1 = (f32[1024]{0:T(1024)S(1)}, f32[1024]{0:T(1024)}, u32[]{:S(2)}) copy-start(f32[1024]{0:T(1024)} %param.11) | copy-start | bytes 12292
  38.8 3.1 %collective-permute-start.5 = (f32[1,512]{1,0:T(1,128)S(1)}, f32[1,512]{1,0:T(1,128)S(1)}, u32[]{:S(2)}, u32[]{:S(2)}) collective-permute-start(f32[1,512]{1,0:T(1,128)S(1)} %get-tuple-element.20.refs_0_), channel_id=1, source_target_pairs={{0,3},{1,2},{2,1},{3,0},{4,7},{5,6},{6,5},{7,4},{8,11},{9,10},{10,... | collective-permute-start | bytes 6152 | tf_op jit(solution)/shard_map/ppermute | solution.py:404
  38.9 3.7 %collective-permute-start.4 = (f32[1,512]{1,0:T(1,128)S(1)}, f32[1,512]{1,0:T(1,128)S(1)}, u32[]{:S(2)}, u32[]{:S(2)}) collective-permute-start(f32[1,512]{1,0:T(1,128)S(1)} %get-tuple-element.20.refs_0_), channel_id=1, source_target_pairs={{0,2},{1,3},{2,0},{3,1},{4,6},{5,7},{6,4},{7,5},{8,10},{9,11},{10,... | collective-permute-start | bytes 6152 | tf_op jit(solution)/shard_map/ppermute | solution.py:404
  40.5 2.1 %collective-permute-start.3 = (f32[1,512]{1,0:T(1,128)S(1)}, f32[1,512]{1,0:T(1,128)S(1)}, u32[]{:S(2)}, u32[]{:S(2)}) collective-permute-start(f32[1,512]{1,0:T(1,128)S(1)} %get-tuple-element.20.refs_0_), channel_id=1, source_target_pairs={{0,1},{1,0},{2,3},{3,2},{4,5},{5,4},{6,7},{7,6},{8,9},{9,8},{10,11... | collective-permute-start | bytes 6152 | tf_op jit(solution)/shard_map/ppermute | solution.py:404
